TPU v7x, 32 devices: a whole 2x2x4 slice. The times are simulated.
32 devices in a mesh: expert: 4 (over x, core), wshard: 8 (over z, y).
Axes of the slice: x: 2, y: 2, z: 4, core: 2. Of those that a mesh axis runs over, the one named last changes fastest.
Arguments:
- tokens: bfloat16 [4096, 2048], P(('expert', 'wshard')), may hold values from -48 to 48
- segment_ids: int32 [4096], P('expert'), may hold values from 0 to 15, never falling along the last dimension, each value on 1 to 512 neighbouring positions
- routes: int32 [4096, 4], P(('expert', 'wshard')), may hold values from 0 to 7, all different within a row; in each aligned block of 128 rows (0 to 127, 128 to 255, ...) at most 128 rows name the same one
- attn_gain: float32 [2048], replicated, may hold values from 0.5 to 1.5
- query_weight: bfloat16 [2048, 2048], P('wshard'), may hold values from -0.125 to 0.125
- key_weight: bfloat16 [2048, 2048], P('wshard'), may hold values from -0.125 to 0.125
- value_weight: bfloat16 [2048, 2048], P('wshard'), may hold values from -0.125 to 0.125
- out_weight: bfloat16 [2048, 2048], P('wshard'), may hold values from -1 to 1
- query_gain: float32 [128], replicated, may hold values from 0.5 to 1.5
- key_gain: float32 [128], replicated, may hold values from 0.5 to 1.5
- ffn_gain: float32 [2048], replicated, may hold values from 0.5 to 1.5
- router_weight: bfloat16 [2048, 8], replicated, may hold values from -0.25 to 0.25
- gate_weight: bfloat16 [8, 2048, 1024], P('expert', 'wshard'), may hold values from -0.125 to 0.125
- up_weight: bfloat16 [8, 2048, 1024], P('expert', 'wshard'), may hold values from -0.125 to 0.125
- down_weight: bfloat16 [8, 1024, 2048], P('expert', None, 'wshard'), may hold values from -0.375 to 0.375
- d_output: bfloat16 [4096, 2048], P(('expert', 'wshard')), may hold values from -6 to 6
Outputs:
- output: bfloat16 [4096, 2048], P(('expert', 'wshard'))
- tokens_grad: bfloat16 [4096, 2048], P(('expert', 'wshard'))
- attn_gain_grad: float32 [2048], replicated
- query_weight_grad: float32 [2048, 2048], P('wshard')
- key_weight_grad: float32 [2048, 2048], P('wshard')
- value_weight_grad: float32 [2048, 2048], P('wshard')
- out_weight_grad: float32 [2048, 2048], P('wshard')
- query_gain_grad: float32 [128], replicated
- key_gain_grad: float32 [128], replicated
- ffn_gain_grad: float32 [2048], replicated
- router_weight_grad: float32 [2048, 8], replicated
- gate_weight_grad: float32 [8, 2048, 1024], P('expert', 'wshard')
- up_weight_grad: float32 [8, 2048, 1024], P('expert', 'wshard')
- down_weight_grad: float32 [8, 1024, 2048], P('expert', None, 'wshard')
- stream_rms: float32 [4], replicated
Inputs may be any that keep to these rules, and one draw needn't show every extreme that they name: `routes`: each row names 4 different experts. Among the 128 rows of one device no expert is named more than 128 times, a bound that some block reaches. `segment_ids`: segment numbers never fall along the tokens; a segment holds 1 to 512 tokens, and some segment holds exactly 512.
All inputs are finite; a program needn't handle non-finite values.
Results may differ from a plain program's by a relative error of at most 0.023.
Values may be sent and summed in bfloat16 or wider, within the bound.
No kernel may reach another device: no remote copies, remote signals or barrier semaphores. Data moves between devices by JAX's collectives and lax.ppermute only.
A program may use at most 384 MiB of HBM per device.

v0:
```python
import math

import jax
import jax.numpy as jnp
from jax import lax
from jax.sharding import PartitionSpec as P

HEADS = 16
HEAD_DIM = 128


epsilon = 1e-06
rope_base = 50000.0
highest = lax.Precision.HIGHEST


def as_sent(x):
    return jax.tree.map(lambda a: a.astype(jnp.bfloat16) if a.dtype == jnp.float32 else a, x)


def norm_rows(values, gain_vector):
    inverse = lax.rsqrt(jnp.mean(values * values, axis=-1, keepdims=True) + epsilon)
    return (values * inverse * gain_vector, inverse)


def norm_back(values, inverse, gain_vector, grad_rows):
    scaled = values * inverse
    leading = tuple(range(grad_rows.ndim - 1))
    gain_grad = jnp.sum(grad_rows * scaled, axis=leading)
    weighted = grad_rows * gain_vector
    values_grad = inverse * (
        weighted - scaled * jnp.mean(weighted * scaled, axis=-1, keepdims=True)
    )
    return (values_grad, gain_grad)


def rope_tables(positions):
    half_dim = HEAD_DIM // 2
    frequency = rope_base ** (-2.0 * jnp.arange(half_dim, dtype=jnp.float32) / HEAD_DIM)
    angles = positions.astype(jnp.float32)[:, None] * frequency[None, :]
    return (jnp.cos(angles)[:, None, :], jnp.sin(angles)[:, None, :])


def rotate(values, cosine_table, sine_table):
    half_dim = values.shape[-1] // 2
    first_half = values[..., :half_dim]
    second_half = values[..., half_dim:]
    return jnp.concatenate(
        [
            first_half * cosine_table - second_half * sine_table,
            second_half * cosine_table + first_half * sine_table,
        ],
        axis=-1,
    )


def route_table(routes, experts, capacity):
    flat_routes = routes.reshape(-1)
    route_count = flat_routes.shape[0]
    expert_hits = (flat_routes[:, None] == jnp.arange(experts, dtype=jnp.int32)[None, :]).astype(
        jnp.int32
    )
    slot_index = jnp.sum((jnp.cumsum(expert_hits, axis=0) - 1) * expert_hits, axis=1)
    slot_table = (
        jnp.full((experts, capacity), route_count, jnp.int32)
        .at[flat_routes, slot_index]
        .set(jnp.arange(route_count, dtype=jnp.int32))
    )
    return (flat_routes, slot_index, slot_table)


def masked_scores(query_side, key_side, mask, root_dim):
    raw_scores = (
        jnp.einsum("qhd,khd->hqk", query_side, key_side, preferred_element_type=jnp.float32)
        / root_dim
    )
    return jnp.where(mask, raw_scores, -1e30)


def softmax_parts(scores):
    row_max = jnp.max(scores, axis=-1, keepdims=True)
    exponent = jnp.exp(scores - row_max)
    row_total = jnp.sum(exponent, axis=-1, keepdims=True)
    return (exponent / row_total, row_max + jnp.log(row_total))


def attention_back(query_side, key_side, value_side, mixed_grad, mask, log_total, root_dim):
    probs_again = jnp.exp(masked_scores(query_side, key_side, mask, root_dim) - log_total)
    probs_grad = jnp.einsum(
        "qhd,khd->hqk", mixed_grad, value_side, preferred_element_type=jnp.float32
    )
    scores_grad = (
        probs_again * (probs_grad - jnp.sum(probs_again * probs_grad, axis=-1, keepdims=True))
    ).astype(jnp.bfloat16)
    query_side_grad = (
        jnp.einsum("hqk,khd->qhd", scores_grad, key_side, preferred_element_type=jnp.float32)
        / root_dim
    )
    key_side_grad = (
        jnp.einsum("hqk,qhd->khd", scores_grad, query_side, preferred_element_type=jnp.float32)
        / root_dim
    )
    value_side_grad = jnp.einsum(
        "hqk,qhd->khd",
        probs_again.astype(jnp.bfloat16),
        mixed_grad,
        preferred_element_type=jnp.float32,
    )
    return (query_side_grad, key_side_grad, value_side_grad)


def local(
    tokens,
    segment_ids,
    routes,
    attn_gain,
    query_weight,
    key_weight,
    value_weight,
    out_weight,
    query_gain,
    key_gain,
    ffn_gain,
    router_weight,
    gate_weight,
    up_weight,
    down_weight,
    d_output,
):
    local_rows = tokens.shape[0]
    model_width = tokens.shape[1]
    seq_len = segment_ids.shape[0]
    owners = lax.axis_size("expert")
    local_experts = gate_weight.shape[0]
    experts = local_experts * owners
    top_count = routes.shape[1]
    capacity = 2 * local_rows * top_count // experts
    root_dim = math.sqrt(HEAD_DIM)
    first_row = lax.axis_index("wshard") * local_rows
    cosine_table, sine_table = rope_tables(first_row + jnp.arange(local_rows, dtype=jnp.int32))
    stream = tokens.astype(jnp.float32)
    normed, attn_inverse = norm_rows(stream, attn_gain)
    normed_low = normed.astype(jnp.bfloat16)
    query_full, key_full, value_full, out_full = (
        lax.all_gather(query_weight, "wshard", axis=0, tiled=True),
        lax.all_gather(key_weight, "wshard", axis=0, tiled=True),
        lax.all_gather(value_weight, "wshard", axis=0, tiled=True),
        lax.all_gather(out_weight, "wshard", axis=0, tiled=True),
    )
    query_raw = jnp.dot(normed_low, query_full, preferred_element_type=jnp.float32).reshape(
        local_rows, HEADS, HEAD_DIM
    )
    key_raw = jnp.dot(normed_low, key_full, preferred_element_type=jnp.float32).reshape(
        local_rows, HEADS, HEAD_DIM
    )
    value_low = jnp.dot(normed_low, value_full, preferred_element_type=jnp.float32).astype(
        jnp.bfloat16
    )
    query_normed, query_inverse = norm_rows(query_raw, query_gain)
    key_normed, key_inverse = norm_rows(key_raw, key_gain)
    query_low = rotate(query_normed, cosine_table, sine_table).astype(jnp.bfloat16)
    key_heads = rotate(key_normed, cosine_table, sine_table).astype(jnp.bfloat16)
    key_low = key_heads.reshape(local_rows, model_width)
    own_segments = lax.dynamic_slice_in_dim(segment_ids, first_row, local_rows)
    same_segment = (own_segments[:, None] == segment_ids[None, :])[None]
    keys_all, values_all = (
        lax.all_gather(key_low, "wshard", axis=0, tiled=True),
        lax.all_gather(value_low, "wshard", axis=0, tiled=True),
    )
    attn_probs, log_total = softmax_parts(
        masked_scores(query_low, keys_all.reshape(seq_len, HEADS, HEAD_DIM), same_segment, root_dim)
    )
    mixed_rows = jnp.einsum(
        "hqk,khd->qhd",
        attn_probs.astype(jnp.bfloat16),
        values_all.reshape(seq_len, HEADS, HEAD_DIM),
        preferred_element_type=jnp.float32,
    )
    mixed_low = mixed_rows.reshape(local_rows, model_width).astype(jnp.bfloat16)
    attended = jnp.dot(mixed_low, out_full, preferred_element_type=jnp.float32)
    middle = stream + attended
    ffn_normed, ffn_inverse = norm_rows(middle, ffn_gain)
    ffn_low = ffn_normed.astype(jnp.bfloat16)
    logits = jnp.dot(ffn_low, router_weight, preferred_element_type=jnp.float32)
    expert_hits = routes[:, :, None] == jnp.arange(experts, dtype=jnp.int32)[None, None, :]
    picked_logits = jnp.sum(jnp.where(expert_hits, logits[:, None, :], 0.0), axis=2)
    mixing = jax.nn.softmax(picked_logits, axis=1)
    flat_routes, slot_index, slot_table = route_table(routes, experts, capacity)
    route_count = local_rows * top_count
    filled = (slot_table < route_count)[..., None]
    route_index = jnp.minimum(slot_table, route_count - 1)
    outgoing = jnp.where(filled, ffn_low[route_index // top_count], jnp.zeros((), jnp.bfloat16))
    arrived = lax.all_to_all(
        outgoing.reshape(owners, local_experts, capacity, model_width),
        "expert",
        split_axis=0,
        concat_axis=0,
        tiled=True,
    )
    gate_full, up_full, down_full = (
        lax.all_gather(gate_weight, "wshard", axis=1, tiled=True),
        lax.all_gather(up_weight, "wshard", axis=1, tiled=True),
        lax.all_gather(down_weight, "wshard", axis=2, tiled=True),
    )
    gate_pre = jnp.einsum("secd,edf->secf", arrived, gate_full, preferred_element_type=jnp.float32)
    up_pre = jnp.einsum("secd,edf->secf", arrived, up_full, preferred_element_type=jnp.float32)
    activated = jax.nn.silu(gate_pre)
    hidden_low = (activated * up_pre).astype(jnp.bfloat16)
    produced = jnp.einsum(
        "secf,efd->secd", hidden_low, down_full, preferred_element_type=jnp.float32
    ).astype(jnp.bfloat16)
    returned = lax.all_to_all(produced, "expert", split_axis=0, concat_axis=0, tiled=True).reshape(
        experts, capacity, model_width
    )
    routed = returned[flat_routes, slot_index].reshape(local_rows, top_count, model_width)
    expert_out = jnp.einsum("tk,tkd->td", mixing, routed, preferred_element_type=jnp.float32)
    final_stream = middle + expert_out
    output = final_stream.astype(jnp.bfloat16)
    final_grad = d_output.astype(jnp.float32)
    mixing_grad = jnp.einsum("td,tkd->tk", final_grad, routed, preferred_element_type=jnp.float32)
    route_grad = (
        (mixing[:, :, None] * final_grad[:, None, :])
        .astype(jnp.bfloat16)
        .reshape(route_count, model_width)
    )
    outgoing_grad = jnp.where(filled, route_grad[route_index], jnp.zeros((), jnp.bfloat16))
    arrived_grad = lax.all_to_all(
        outgoing_grad.reshape(owners, local_experts, capacity, model_width),
        "expert",
        split_axis=0,
        concat_axis=0,
        tiled=True,
    )
    gate_back, up_back, down_back = (
        lax.all_gather(gate_weight, "wshard", axis=1, tiled=True),
        lax.all_gather(up_weight, "wshard", axis=1, tiled=True),
        lax.all_gather(down_weight, "wshard", axis=2, tiled=True),
    )
    down_grad_all = jnp.einsum(
        "secf,secd->efd", hidden_low, arrived_grad, preferred_element_type=jnp.float32
    )
    hidden_grad = jnp.einsum(
        "secd,efd->secf", arrived_grad, down_back, preferred_element_type=jnp.float32
    )
    sigmoid_gate = jax.nn.sigmoid(gate_pre)
    gate_grad_low = (
        hidden_grad * up_pre * sigmoid_gate * (1.0 + gate_pre * (1.0 - sigmoid_gate))
    ).astype(jnp.bfloat16)
    up_grad_low = (hidden_grad * activated).astype(jnp.bfloat16)
    gate_grad_all = jnp.einsum(
        "secd,secf->edf", arrived, gate_grad_low, preferred_element_type=jnp.float32
    )
    up_grad_all = jnp.einsum(
        "secd,secf->edf", arrived, up_grad_low, preferred_element_type=jnp.float32
    )
    rows_grad = jnp.einsum(
        "secf,edf->secd", gate_grad_low, gate_back, preferred_element_type=jnp.float32
    )
    rows_grad = (
        rows_grad
        + jnp.einsum("secf,edf->secd", up_grad_low, up_back, preferred_element_type=jnp.float32)
    ).astype(jnp.bfloat16)
    back_rows = lax.all_to_all(
        rows_grad, "expert", split_axis=0, concat_axis=0, tiled=True
    ).reshape(experts, capacity, model_width)
    gate_weight_grad, up_weight_grad, down_weight_grad = (
        lax.psum_scatter(
            gate_grad_all.astype(jnp.bfloat16), "wshard", scatter_dimension=1, tiled=True
        ).astype(jnp.float32),
        lax.psum_scatter(
            up_grad_all.astype(jnp.bfloat16), "wshard", scatter_dimension=1, tiled=True
        ).astype(jnp.float32),
        lax.psum_scatter(
            down_grad_all.astype(jnp.bfloat16), "wshard", scatter_dimension=2, tiled=True
        ).astype(jnp.float32),
    )
    ffn_grad = jnp.sum(
        back_rows[flat_routes, slot_index].reshape(local_rows, top_count, model_width),
        axis=1,
        dtype=jnp.float32,
    )
    picked_grad = mixing * (mixing_grad - jnp.sum(mixing * mixing_grad, axis=1, keepdims=True))
    logits_grad = jnp.sum(jnp.where(expert_hits, picked_grad[:, :, None], 0.0), axis=1)
    router_grad = jnp.einsum(
        "td,te->de", ffn_low.astype(jnp.float32), logits_grad, precision=highest
    )
    ffn_grad = ffn_grad + jnp.einsum(
        "te,de->td", logits_grad, router_weight.astype(jnp.float32), precision=highest
    )
    middle_from_ffn, ffn_gain_grad = norm_back(middle, ffn_inverse, ffn_gain, ffn_grad)
    middle_grad = final_grad + middle_from_ffn
    attended_low = middle_grad.astype(jnp.bfloat16)
    sequence_parts = (key_low, value_low)
    fetched = lax.all_gather(
        as_sent((query_weight, key_weight, value_weight, out_weight) + sequence_parts),
        "wshard",
        axis=0,
        tiled=True,
    )
    query_back, key_back, value_back, out_back = (fetched[0], fetched[1], fetched[2], fetched[3])
    sequence_back = fetched[4:]
    out_grad_all = jnp.einsum(
        "td,te->de", mixed_low, attended_low, preferred_element_type=jnp.float32
    )
    mixed_grad_low = (
        jnp.einsum("te,de->td", attended_low, out_back, preferred_element_type=jnp.float32)
        .astype(jnp.bfloat16)
        .reshape(local_rows, HEADS, HEAD_DIM)
    )
    keys_seq = sequence_back[0].reshape(seq_len, HEADS, HEAD_DIM)
    values_seq = sequence_back[1].reshape(seq_len, HEADS, HEAD_DIM)
    query_rot_grad, keys_grad_seq, values_grad_seq = attention_back(
        query_low, keys_seq, values_seq, mixed_grad_low, same_segment, log_total, root_dim
    )
    key_grad_rows, value_grad_rows = (
        lax.psum_scatter(
            keys_grad_seq.reshape(seq_len, model_width).astype(jnp.bfloat16),
            "wshard",
            scatter_dimension=0,
            tiled=True,
        ).astype(jnp.float32),
        lax.psum_scatter(
            values_grad_seq.reshape(seq_len, model_width).astype(jnp.bfloat16),
            "wshard",
            scatter_dimension=0,
            tiled=True,
        ).astype(jnp.float32),
    )
    key_rot_grad = key_grad_rows.reshape(local_rows, HEADS, HEAD_DIM)
    query_raw_grad, query_gain_grad = norm_back(
        query_raw, query_inverse, query_gain, rotate(query_rot_grad, cosine_table, -sine_table)
    )
    key_raw_grad, key_gain_grad = norm_back(
        key_raw, key_inverse, key_gain, rotate(key_rot_grad, cosine_table, -sine_table)
    )
    query_grad_low = query_raw_grad.reshape(local_rows, model_width).astype(jnp.bfloat16)
    key_grad_low = key_raw_grad.reshape(local_rows, model_width).astype(jnp.bfloat16)
    value_grad_low = value_grad_rows.astype(jnp.bfloat16)
    query_grad_all = jnp.einsum(
        "td,te->de", normed_low, query_grad_low, preferred_element_type=jnp.float32
    )
    key_grad_all = jnp.einsum(
        "td,te->de", normed_low, key_grad_low, preferred_element_type=jnp.float32
    )
    value_grad_all = jnp.einsum(
        "td,te->de", normed_low, value_grad_low, preferred_element_type=jnp.float32
    )
    normed_grad = jnp.einsum(
        "te,de->td", query_grad_low, query_back, preferred_element_type=jnp.float32
    )
    normed_grad = normed_grad + jnp.einsum(
        "te,de->td", key_grad_low, key_back, preferred_element_type=jnp.float32
    )
    normed_grad = normed_grad + jnp.einsum(
        "te,de->td", value_grad_low, value_back, preferred_element_type=jnp.float32
    )
    stream_from_attn, attn_gain_grad = norm_back(stream, attn_inverse, attn_gain, normed_grad)
    tokens_grad = (middle_grad + stream_from_attn).astype(jnp.bfloat16)
    query_part, key_part, value_part, out_part = (
        lax.psum_scatter(
            query_grad_all.astype(jnp.bfloat16), "wshard", scatter_dimension=0, tiled=True
        ).astype(jnp.float32),
        lax.psum_scatter(
            key_grad_all.astype(jnp.bfloat16), "wshard", scatter_dimension=0, tiled=True
        ).astype(jnp.float32),
        lax.psum_scatter(
            value_grad_all.astype(jnp.bfloat16), "wshard", scatter_dimension=0, tiled=True
        ).astype(jnp.float32),
        lax.psum_scatter(
            out_grad_all.astype(jnp.bfloat16), "wshard", scatter_dimension=0, tiled=True
        ).astype(jnp.float32),
    )
    query_weight_grad, key_weight_grad, value_weight_grad, out_weight_grad = (
        lax.psum(query_part.astype(jnp.bfloat16), "expert").astype(jnp.float32),
        lax.psum(key_part.astype(jnp.bfloat16), "expert").astype(jnp.float32),
        lax.psum(value_part.astype(jnp.bfloat16), "expert").astype(jnp.float32),
        lax.psum(out_part.astype(jnp.bfloat16), "expert").astype(jnp.float32),
    )
    squares = jnp.stack(
        [
            jnp.sum(middle * middle),
            jnp.sum(final_stream * final_stream),
            jnp.sum(attended * attended),
            jnp.sum(expert_out * expert_out),
        ]
    )
    attn_gain_grad, ffn_gain_grad, query_gain_grad, key_gain_grad, router_grad, squares = lax.psum(
        (attn_gain_grad, ffn_gain_grad, query_gain_grad, key_gain_grad, router_grad, squares),
        ("expert", "wshard"),
    )
    everything = local_rows * owners * lax.axis_size("wshard") * model_width
    stream_rms = jnp.sqrt(squares / everything)
    return (
        output,
        tokens_grad,
        attn_gain_grad,
        query_weight_grad,
        key_weight_grad,
        value_weight_grad,
        out_weight_grad,
        query_gain_grad,
        key_gain_grad,
        ffn_gain_grad,
        router_grad,
        gate_weight_grad,
        up_weight_grad,
        down_weight_grad,
        stream_rms,
    )


def solution(mesh):
    return jax.shard_map(
        local,
        mesh=mesh,
        in_specs=(
            P(("expert", "wshard"), None),
            P("expert"),
            P(("expert", "wshard"), None),
            P(),
            P("wshard", None),
            P("wshard", None),
            P("wshard", None),
            P("wshard", None),
            P(),
            P(),
            P(),
            P(),
            P("expert", "wshard", None),
            P("expert", "wshard", None),
            P("expert", None, "wshard"),
            P(("expert", "wshard"), None),
        ),
        out_specs=(
            P(("expert", "wshard"), None),
            P(("expert", "wshard"), None),
            P(),
            P("wshard", None),
            P("wshard", None),
            P("wshard", None),
            P("wshard", None),
            P(),
            P(),
            P(),
            P(),
            P("expert", "wshard", None),
            P("expert", "wshard", None),
            P("expert", None, "wshard"),
            P(),
        ),
        check_vma=False,
    )
```

profile of v0, /device:TPU:0, one launch (start us, length us, event | category | flops | bytes accessed | tf_op | source)
XLA Modules:
  0.0 2788.7 jit_solution(11628938577065850110)
XLA Ops:
  11.7 126.1 %all-gather.14.cloned.1.call-done = bf16[2048,2048]{1,0:T(8,128)(2,1)} async-done(((bf16[256,2048]{1,0:T(8,128)(2,1)}), bf16[2048,2048]{1,0:T(8,128)(2,1)}) %all-gather.14.cloned.1.call-update) | async-done | bytes 8388624 | tf_op jit(solution)/shard_map/all_gather | solution.py:145
  143.1 120.0 %all-gather.16.cloned.1.call-done = bf16[2048,2048]{1,0:T(8,128)(2,1)} async-done(((bf16[256,2048]{1,0:T(8,128)(2,1)}), bf16[2048,2048]{1,0:T(8,128)(2,1)}) %all-gather.16.cloned.1.call-update) | async-done | bytes 8388624 | tf_op jit(solution)/shard_map/all_gather | solution.py:146
  271.4 117.0 %all-gather.10.cloned.1.call-done = bf16[2048,2048]{1,0:T(8,128)(2,1)} async-done(((bf16[256,2048]{1,0:T(8,128)(2,1)}), bf16[2048,2048]{1,0:T(8,128)(2,1)}) %all-gather.10.cloned.1.call-update) | async-done | bytes 8388624 | tf_op jit(solution)/shard_map/all_gather | solution.py:147
  398.7 22.1 scatter_fusion
  421.1 43.0 %all-gather.18.cloned.1.call-done = bf16[1024,2048]{0,1:T(8,128)(2,1)} async-done(((bf16[128,2048]{0,1:T(8,128)(2,1)}), bf16[1024,2048]{0,1:T(8,128)(2,1)}) %all-gather.18.cloned.1.call-update) | async-done | bytes 4194320 | tf_op jit(solution)/shard_map/all_gather | solution.py:167
  473.7 64.6 %all-gather.12.cloned.1.call-done = bf16[1024,2048]{1,0:T(8,128)(2,1)} async-done(((bf16[128,2048]{1,0:T(8,128)(2,1)}), bf16[1024,2048]{1,0:T(8,128)(2,1)}) %all-gather.12.cloned.1.call-update) | async-done | bytes 4194320 | tf_op jit(solution)/shard_map/all_gather | solution.py:168
  545.5 118.0 %all-gather.20.cloned.1.call-done = bf16[2048,2048]{1,0:T(8,128)(2,1)} async-done(((bf16[256,2048]{1,0:T(8,128)(2,1)}), bf16[2048,2048]{1,0:T(8,128)(2,1)}) %all-gather.20.cloned.1.call-update) | async-done | bytes 8388624 | tf_op jit(solution)/shard_map/all_gather | solution.py:148
  685.9 102.9 %all-gather.22.cloned.1.call-done = bf16[2,2048,1024]{2,1,0:T(8,128)(2,1)} async-done(((bf16[2,256,1024]{2,1,0:T(8,128)(2,1)}), bf16[2,2048,1024]{2,1,0:T(8,128)(2,1)}) %all-gather.22.cloned.1.call-update) | async-done | bytes 8388624 | tf_op jit(solution)/shard_map/all_gather | solution.py:201
  788.8 11.2 fusion.6
  800.0 114.2 %all-gather.24.cloned.1.call-done = bf16[2,2048,1024]{2,1,0:T(8,128)(2,1)} async-done(((bf16[2,256,1024]{2,1,0:T(8,128)(2,1)}), bf16[2,2048,1024]{2,1,0:T(8,128)(2,1)}) %all-gather.24.cloned.1.call-update) | async-done | bytes 8388624 | tf_op jit(solution)/shard_map/all_gather | solution.py:202
  914.1 12.4 fusion.25
  926.5 113.3 %all-gather.26.cloned.1.call-done = bf16[2,1024,2048]{2,1,0:T(8,128)(2,1)} async-done(((bf16[2,1024,256]{2,1,0:T(8,128)(2,1)}), bf16[2,1024,2048]{2,1,0:T(8,128)(2,1)}) %all-gather.26.cloned.1.call-update) | async-done | bytes 8388624 | tf_op jit(solution)/shard_map/all_gather | solution.py:203
  1063.9 39.6 %all-to-all-done.1 = bf16[4,2,128,2048]{3,2,1,0:T(8,128)(2,1)} async-done(((bf16[4,2,128,2048]{3,2,1,0:T(8,128)(2,1)}), bf16[4,2,128,2048]{3,2,1,0:T(8,128)(2,1)}, u32[]{:S(2)}, u32[]{:S(2)}) %all-to-all-start.1) | async-done | bytes 4194336 | tf_op jit(solution)/shard_map/all_to_all | solution.py:212
  1131.4 51.8 %all_to_all.20 = bf16[4,2,128,2048]{3,2,1,0:T(8,128)(2,1)} all-to-all(bf16[4,2,128,2048]{3,2,1,0:T(8,128)(2,1)S(1)} %broadcast_select_fusion), channel_id=1, replica_groups=mesh['expert'=4,'wshard'=8] {'expert'}, dimensions={0} | all-to-all | bytes 8388608 | tf_op jit(solution)/shard_map/all_to_all | solution.py:227
  1183.2 13.9 fusion.23
  1197.1 12.5 fusion
  1209.6 11.1 fusion.16
  1232.9 45.8 %all-to-all-done.3 = bf16[4,2,128,2048]{3,2,1,0:T(8,128)(2,1)} async-done(((bf16[4,2,128,2048]{3,2,1,0:T(8,128)(2,1)}), bf16[4,2,128,2048]{3,2,1,0:T(8,128)(2,1)}, u32[]{:S(2)}, u32[]{:S(2)}) %all-to-all-start.3) | async-done | bytes 4194336 | tf_op jit(solution)/shard_map/all_to_all | solution.py:263
  1354.1 58.6 %reduce-scatter.28.cloned.1.call-done = bf16[128,2048]{1,0:T(8,128)(2,1)} async-done(((bf16[1024,2048]{1,0:T(8,128)(2,1)}), bf16[128,2048]{1,0:T(8,128)(2,1)}) %reduce-scatter.28.cloned.1.call-update) | async-done | bytes 524304
  1445.8 58.7 %reduce-scatter.30.cloned.1.call-done = bf16[128,2048]{1,0:T(8,128)(2,1)} async-done(((bf16[1024,2048]{1,0:T(8,128)(2,1)}), bf16[128,2048]{1,0:T(8,128)(2,1)}) %reduce-scatter.30.cloned.1.call-update) | async-done | bytes 524304
  1522.0 10.7 bitcast_convert_fusion.1
  1533.0 10.7 bitcast_convert_fusion
  1543.7 113.0 %reduce-scatter.20.cloned.1.call-done = bf16[256,2048]{1,0:T(8,128)(2,1)} async-done(((bf16[2048,2048]{1,0:T(8,128)(2,1)}), bf16[256,2048]{1,0:T(8,128)(2,1)}) %reduce-scatter.20.cloned.1.call-update) | async-done | bytes 1048592 | tf_op jit(solution)/shard_map/reduce_scatter | solution.py:369
  1656.7 152.1 %reduce-scatter.14.cloned.1.call-done = bf16[256,2048]{1,0:T(8,128)(2,1)} async-done(((bf16[2048,2048]{1,0:T(8,128)(2,1)}), bf16[256,2048]{1,0:T(8,128)(2,1)}) %reduce-scatter.14.cloned.1.call-update) | async-done | bytes 1048592 | tf_op jit(solution)/shard_map/reduce_scatter | solution.py:360
  1808.8 151.5 %reduce-scatter.16.cloned.1.call-done = bf16[256,2048]{1,0:T(8,128)(2,1)} async-done(((bf16[2048,2048]{1,0:T(8,128)(2,1)}), bf16[256,2048]{1,0:T(8,128)(2,1)}) %reduce-scatter.16.cloned.1.call-update) | async-done | bytes 1048592 | tf_op jit(solution)/shard_map/reduce_scatter | solution.py:363
  1960.3 152.0 %reduce-scatter.18.cloned.1.call-done = bf16[256,2048]{1,0:T(8,128)(2,1)} async-done(((bf16[2048,2048]{1,0:T(8,128)(2,1)}), bf16[256,2048]{1,0:T(8,128)(2,1)}) %reduce-scatter.18.cloned.1.call-update) | async-done | bytes 1048592 | tf_op jit(solution)/shard_map/reduce_scatter | solution.py:366
  2133.2 43.4 %all-reduce = (f32[2048]{0:T(1024)}, f32[128]{0:T(128)}, f32[128]{0:T(128)}, f32[2048]{0:T(1024)}, f32[4]{0:T(128)S(1)}) all-reduce(f32[2048]{0:T(1024)S(1)} %get-tuple-element.17, f32[128]{0:T(128)S(1)} %bitcast_reduce_fusion.1, f32[128]{0:T(128)S(1)} %bitcast_reduce_fusion, ...), channel_id=1, replica_groups=mesh['expert'=4,'wshard'=8] {'expert','wshard'}, use_global_device_ids=true, to_apply=%region_24.25 | all-reduce | flops 4356 | bytes 34848 | tf_op jit(solution)/shard_map/psum | solution.py:387
  2177.1 87.7 %reduce-scatter.22.cloned.1.call-done = bf16[2,256,1024]{2,1,0:T(8,128)(2,1)} async-done(((bf16[2,2048,1024]{2,1,0:T(8,128)(2,1)}), bf16[2,256,1024]{2,1,0:T(8,128)(2,1)}) %reduce-scatter.22.cloned.1.call-update) | async-done | bytes 1048592 | tf_op jit(solution)/shard_map/reduce_scatter | solution.py:267
  2267.7 149.2 %reduce-scatter.24.cloned.1.call-done = bf16[2,256,1024]{2,1,0:T(8,128)(2,1)} async-done(((bf16[2,2048,1024]{2,1,0:T(8,128)(2,1)}), bf16[2,256,1024]{2,1,0:T(8,128)(2,1)}) %reduce-scatter.24.cloned.1.call-update) | async-done | bytes 1048592 | tf_op jit(solution)/shard_map/reduce_scatter | solution.py:270
  2419.6 149.1 %reduce-scatter.26.cloned.1.call-done = bf16[2,1024,256]{2,1,0:T(8,128)(2,1)} async-done(((bf16[2,1024,2048]{2,1,0:T(8,128)(2,1)}), bf16[2,1024,256]{2,1,0:T(8,128)(2,1)}) %reduce-scatter.26.cloned.1.call-update) | async-done | bytes 1048592 | tf_op jit(solution)/shard_map/reduce_scatter | solution.py:273
  2571.5 85.1 %all-reduce.7.cloned.1.call-done = (bf16[256,2048]{1,0:T(8,128)(2,1)}, bf16[256,2048]{1,0:T(8,128)(2,1)}, bf16[256,2048]{1,0:T(8,128)(2,1)}, bf16[256,2048]{1,0:T(8,128)(2,1)}) async-done(((bf16[256,2048]{1,0:T(8,128)(2,1)}, bf16[256,2048]{1,0:T(8,128)(2,1)}, bf16[256,2048]{1,0:T(8,128)(2,1)}, bf16[256,2048]{1,0:T(8,128)(2,1)}), (bf16[256,2048]{1,0:T(8,128)(2,1)}, bf16[256,2048]{1,0:T(8,128)(2,1)}, ...) | async-done | bytes 4194320 | tf_op jit(solution)/shard_map/psum | solution.py:374
  2665.4 114.8 %all-reduce.5.cloned.1.call-done = f32[2048,8]{0,1:T(8,128)} async-done(((f32[2048,8]{0,1:T(8,128)}), f32[2048,8]{0,1:T(8,128)}) %all-reduce.5.cloned.1.call-update) | async-done | bytes 65552 | tf_op jit(solution)/shard_map/psum | solution.py:387
  (275 shorter events, 297.7 us)
Async XLA Ops:
  7.2 1056.4 %copy-start = (bf16[2048,8]{0,1:T(8,128)(2,1)S(1)}, bf16[2048,8]{0,1:T(8,128)(2,1)}, u32[]{:S(2)}) copy-start(bf16[2048,8]{0,1:T(8,128)(2,1)} %param.27) | copy-start | bytes 98308
  7.2 130.6 %copy-start.4 = (bf16[128,2048]{1,0:T(8,128)(2,1)S(1)}, bf16[128,2048]{1,0:T(8,128)(2,1)}, u32[]{:S(2)}) copy-start(bf16[128,2048]{1,0:T(8,128)(2,1)} %param.16) | copy-start | bytes 1572868
  7.2 130.6 %all-gather.14.cloned.1.call-start = ((), (), s32[]{:S(2)}) async-start(), calls=%async_computation.15 | async-start | bytes 9437184 | tf_op jit(solution)/shard_map/all_gather | solution.py:145
  7.9 255.2 %all-gather.16.cloned.1.call-start = ((), (), s32[]{:S(2)}) async-start(), calls=%async_computation.16 | async-start | bytes 9437184 | tf_op jit(solution)/shard_map/all_gather | solution.py:146
  8.7 379.7 %all-gather.10.cloned.1.call-start = ((), (), s32[]{:S(2)}) async-start(), calls=%async_computation.13 | async-start | bytes 9437184 | tf_op jit(solution)/shard_map/all_gather | solution.py:147
  9.4 454.7 %all-gather.18.cloned.1.call-start = ((), (), s32[]{:S(2)}) async-start(), calls=%async_computation.17 | async-start | bytes 4718592 | tf_op jit(solution)/shard_map/all_gather | solution.py:167
  10.7 377.6 %copy-start.35 = (f32[128]{0:T(128)}, f32[128]{0:T(128)S(1)}, u32[]{:S(2)}) copy-start(f32[128]{0:T(128)S(1)} %add_rsqrt_fusion.3) | copy-start | bytes 1540
  11.7 257.5 %copy-start.28 = (f32[128,64]{1,0:T(8,128)}, f32[128,64]{1,0:T(8,128)S(1)}, u32[]{:S(2)}) copy-start(f32[128,64]{1,0:T(8,128)S(1)} %get-tuple-element.69) | copy-start | bytes 98308
  11.7 251.4 %copy-start.21 = (f32[2048]{0:T(1024)S(1)}, f32[2048]{0:T(1024)}, u32[]{:S(2)}) copy-start(f32[2048]{0:T(1024)} %param.19) | copy-start | bytes 24580
  270.0 194.2 %copy-start.15 = (bf16[128,16,64]{2,0,1:T(8,128)(2,1)}, bf16[128,16,64]{2,0,1:T(8,128)(2,1)S(1)}, u32[]{:S(2)}) copy-start(bf16[128,16,64]{2,0,1:T(8,128)(2,1)S(1)} %get-tuple-element.54) | copy-start | bytes 786436
  270.0 194.1 %copy-start.17 = (bf16[128,16,64]{2,0,1:T(8,128)(2,1)}, bf16[128,16,64]{2,0,1:T(8,128)(2,1)S(1)}, u32[]{:S(2)}) copy-start(bf16[128,16,64]{2,0,1:T(8,128)(2,1)S(1)} %get-tuple-element.55) | copy-start | bytes 786436
  271.3 267.0 %all-gather.12.cloned.1.call-start = ((), (), s32[]{:S(2)}) async-start(), calls=%async_computation.14 | async-start | bytes 4718592 | tf_op jit(solution)/shard_map/all_gather | solution.py:168
  393.9 269.6 %all-gather.20.cloned.1.call-start = ((), (), s32[]{:S(2)}) async-start(), calls=%async_computation.18 | async-start | bytes 9437184 | tf_op jit(solution)/shard_map/all_gather | solution.py:148
  394.5 394.3 %all-gather.22.cloned.1.call-start = ((), (), s32[]{:S(2)}) async-start(), calls=%async_computation.19 | async-start | bytes 9437184 | tf_op jit(solution)/shard_map/all_gather | solution.py:201
  395.2 518.9 %all-gather.24.cloned.1.call-start = ((), (), s32[]{:S(2)}) async-start(), calls=%async_computation.20 | async-start | bytes 9437184 | tf_op jit(solution)/shard_map/all_gather | solution.py:202
  396.0 643.8 %all-gather.26.cloned.1.call-start = ((), (), s32[]{:S(2)}) async-start(), calls=%async_computation.21 | async-start | bytes 9437184 | tf_op jit(solution)/shard_map/all_gather | solution.py:203
  670.1 393.5 %copy-start.1 = (bf16[128,2048]{1,0:T(8,128)(2,1)}, bf16[128,2048]{1,0:T(8,128)(2,1)S(1)}, u32[]{:S(2)}) copy-start(bf16[128,2048]{1,0:T(8,128)(2,1)S(1)} %multiply_convert_fusion.3) | copy-start | bytes 1572868
  680.7 108.1 %all-to-all-start = ((bf16[4,2,128,2048]{3,2,1,0:T(8,128)(2,1)}), bf16[4,2,128,2048]{3,2,1,0:T(8,128)(2,1)}, u32[]{:S(2)}, u32[]{:S(2)}) async-start(bf16[4,2,128,2048]{3,2,1,0:T(8,128)(2,1)} %broadcast_select_fusion.1), calls=%async_computation | async-start | bytes 8388608 | tf_op jit(solution)/shard_map/all_to_all | solution.py:193
  1050.2 53.2 %all-to-all-start.1 = ((bf16[4,2,128,2048]{3,2,1,0:T(8,128)(2,1)}), bf16[4,2,128,2048]{3,2,1,0:T(8,128)(2,1)}, u32[]{:S(2)}, u32[]{:S(2)}) async-start(bf16[4,2,128,2048]{3,2,1,0:T(8,128)(2,1)} %copy.202), calls=%async_computation.1 | async-start | bytes 8388608 | tf_op jit(solution)/shard_map/all_to_all | solution.py:212
  1225.4 53.3 %all-to-all-start.3 = ((bf16[4,2,128,2048]{3,2,1,0:T(8,128)(2,1)}), bf16[4,2,128,2048]{3,2,1,0:T(8,128)(2,1)}, u32[]{:S(2)}, u32[]{:S(2)}) async-start(bf16[4,2,128,2048]{3,2,1,0:T(8,128)(2,1)} %copy.205), calls=%async_computation.3 | async-start | bytes 8388608 | tf_op jit(solution)/shard_map/all_to_all | solution.py:263
  1230.5 182.2 %reduce-scatter.28.cloned.1.call-start = ((), (), s32[]{:S(2)}) async-start(), calls=%async_computation.30 | async-start | bytes 4718592
  1327.4 177.1 %reduce-scatter.30.cloned.1.call-start = ((), (), s32[]{:S(2)}) async-start(), calls=%async_computation.31 | async-start | bytes 4718592
  1340.8 315.9 %reduce-scatter.20.cloned.1.call-start = ((), (), s32[]{:S(2)}) async-start(), calls=%async_computation.25 | async-start | bytes 9437184 | tf_op jit(solution)/shard_map/reduce_scatter | solution.py:369
  1347.4 461.4 %reduce-scatter.14.cloned.1.call-start = ((), (), s32[]{:S(2)}) async-start(), calls=%async_computation.22 | async-start | bytes 9437184 | tf_op jit(solution)/shard_map/reduce_scatter | solution.py:360
  1431.5 528.9 %reduce-scatter.16.cloned.1.call-start = ((), (), s32[]{:S(2)}) async-start(), calls=%async_computation.23 | async-start | bytes 9437184 | tf_op jit(solution)/shard_map/reduce_scatter | solution.py:363
  1445.4 667.0 %reduce-scatter.18.cloned.1.call-start = ((), (), s32[]{:S(2)}) async-start(), calls=%async_computation.24 | async-start | bytes 9437184 | tf_op jit(solution)/shard_map/reduce_scatter | solution.py:366
  1511.3 753.6 %reduce-scatter.22.cloned.1.call-start = ((), (), s32[]{:S(2)}) async-start(), calls=%async_computation.27 | async-start | bytes 9437184 | tf_op jit(solution)/shard_map/reduce_scatter | solution.py:267
  1522.0 894.9 %reduce-scatter.24.cloned.1.call-start = ((), (), s32[]{:S(2)}) async-start(), calls=%async_computation.28 | async-start | bytes 9437184 | tf_op jit(solution)/shard_map/reduce_scatter | solution.py:270
  1532.7 1036.0 %reduce-scatter.26.cloned.1.call-start = ((), (), s32[]{:S(2)}) async-start(), calls=%async_computation.29 | async-start | bytes 9437184 | tf_op jit(solution)/shard_map/reduce_scatter | solution.py:273
  1543.6 568.8 %copy-start.2 = (bf16[128,2048]{1,0:T(8,128)(2,1)S(1)}, bf16[128,2048]{1,0:T(8,128)(2,1)}, u32[]{:S(2)}) copy-start(bf16[128,2048]{1,0:T(8,128)(2,1)} %copy-done.1) | copy-start | bytes 1572868
  1543.6 1112.9 %all-reduce.7.cloned.1.call-start = ((), (), s32[]{:S(2)}) async-start(), calls=%async_computation.32 | async-start | bytes 8388608 | tf_op jit(solution)/shard_map/psum | solution.py:374
  2112.3 667.9 %all-reduce.5.cloned.1.call-start = ((), (), s32[]{:S(2)}) async-start(), calls=%async_computation.26 | async-start | bytes 131072 | tf_op jit(solution)/shard_map/psum | solution.py:387
  (41 other events, 905.2 us)
Sparse Core Ops, SparseCore 0:
  10.2 127.6 all-gather.13
  140.0 123.1 all-gather.15
  265.2 123.1 all-gather.9
  390.9 73.2 all-gather.17
  466.7 71.5 all-gather.11
  540.3 123.1 all-gather.19
  665.7 123.0 all-gather.21
  791.0 123.0 all-gather.23
  916.2 123.5 all-gather.25
  1327.5 85.1 reduce-scatter.27
  1416.8 87.6 reduce-scatter.29
  1507.9 148.7 reduce-scatter.19
  1660.8 147.9 reduce-scatter.13
  1812.3 148.0 reduce-scatter.15
  1964.3 148.0 reduce-scatter.17
  2115.8 149.0 reduce-scatter.21
  2268.8 148.0 reduce-scatter.23
  2420.3 148.3 reduce-scatter.25
  2571.5 85.0 all-reduce.6
  2662.6 117.6 all-reduce.4
where the time goes:
time: 2800 us; the launch traced here: 2790 us
  waiting for transfers between devices  2280 us (81%)
  matrix products  214 us (8%)
  local copies, waits for them, and re-layouts  106 us (4%)
  blocking collectives  95.2 us (3%)
  other arithmetic  59.9 us (2%)
    reduce_scatter x1, waiting for transfers between devices, local(): lax.psum_scatter(query_grad_all.astype(jnp.bfloat16), 'wshard', scatter_d...  152 us
    reduce_scatter x1, waiting for transfers between devices, local(): lax.psum_scatter(value_grad_all.astype(jnp.bfloat16), 'wshard', scatter_d...  152 us
    reduce_scatter x1, waiting for transfers between devices, local(): lax.psum_scatter(key_grad_all.astype(jnp.bfloat16), 'wshard', scatter_dim...  152 us
    reduce_scatter x1, waiting for transfers between devices, local(): lax.psum_scatter(up_grad_all.astype(jnp.bfloat16), 'wshard', scatter_dime...  149 us
    reduce_scatter x1, waiting for transfers between devices, local(): lax.psum_scatter(down_grad_all.astype(jnp.bfloat16), 'wshard', scatter_di...  149 us
    all_gather x1, waiting for transfers between devices, local(): lax.all_gather(query_weight, 'wshard', axis=0, tiled=True)  126 us
    unnamed x22, waiting for transfers between devices  122 us
    all_gather x1, waiting for transfers between devices, local(): lax.all_gather(key_weight, 'wshard', axis=0, tiled=True)  120 us
  transfers between devices with their start and end apart: 23, of which 22 were waited for; matrix products, arithmetic and copies ran while one was open for 9% of the time, Pallas kernels for 0%

commit v1 on v0

v1 whole, which is shorter than its diff:
```python
import functools
import math

import jax
import jax.numpy as jnp
from jax import lax
from jax.experimental import pallas as pl
from jax.experimental.pallas import tpu as pltpu
from jax.sharding import PartitionSpec as P

HEADS = 16
HEAD_DIM = 128
epsilon = 1e-06
rope_base = 50000.0
highest = lax.Precision.HIGHEST
bf16 = jnp.bfloat16
f32 = jnp.float32

NN = (((1,), (0,)), ((), ()))
NT = (((1,), (1,)), ((), ()))
TN = (((0,), (0,)), ((), ()))


def mm(a, b, dims=NN):
    return lax.dot_general(a, b, dims, preferred_element_type=f32)


def ring_order(n):
    return list(range(0, n, 2)) + list(range(n - 1, 0, -2))


class Ring:
    def __init__(self, axis):
        self.axis = axis
        self.n = n = lax.axis_size(axis)
        order = ring_order(n)
        self.down = [(order[i], order[(i + 1) % n]) for i in range(n)]
        self.up = [(b, a) for a, b in self.down]
        place = [order.index(w) for w in range(n)]
        here = jnp.asarray(place, jnp.int32)[lax.axis_index(axis)]
        self.half = n // 2
        self.offsets = [0]
        for s in range(1, self.half):
            self.offsets += [-s, s]
        self.offsets.append(-self.half)
        table = jnp.asarray(order, jnp.int32)
        self.owner = table[(here + jnp.asarray(self.offsets, jnp.int32) + n) % n]

    def gather(self, own, far_up=False):
        got = {0: own}
        down = up = own
        for s in range(1, self.half + 1):
            if s < self.half or not far_up:
                down = lax.ppermute(down, self.axis, self.down)
                got[-s] = down
            if s < self.half or far_up:
                up = lax.ppermute(up, self.axis, self.up)
                got[s if s < self.half else -s] = up
        return [got[o] for o in self.offsets]

    def scatter(self, parts, far_up=False):
        part = dict(zip(self.offsets, parts))
        part[self.half] = part[-self.half]

        def chain(length, sign, perm):
            moving = part[sign * length]
            for s in range(length - 1, -1, -1):
                came = lax.ppermute(moving, self.axis, perm)
                if s:
                    moving = (came.astype(f32) + part[sign * s].astype(f32)).astype(bf16)
            return came.astype(f32)

        ahead = chain(self.half - (1 if far_up else 0), 1, self.down)
        behind = chain(self.half - (0 if far_up else 1), -1, self.up)
        return part[0].astype(f32) + ahead + behind


def bits_of(size):
    return [1 << b for b in range(size.bit_length() - 1)]


def swap(x, axis, bit):
    return lax.ppermute(x, axis, [(i, i ^ bit) for i in range(lax.axis_size(axis))])


def gather_bits(x, axis):
    index = lax.axis_index(axis)
    out = x[None]
    for bit in reversed(bits_of(lax.axis_size(axis))):
        came = swap(out, axis, bit)
        high = (index & bit) != 0
        out = jnp.stack([jnp.where(high, came, out), jnp.where(high, out, came)], axis=1)
        out = out.reshape((-1,) + x.shape)
    return out


def scatter_bits(x, axis):
    index = lax.axis_index(axis)
    for bit in bits_of(lax.axis_size(axis)):
        pairs = x.reshape((-1, 2) + x.shape[1:])
        high = (index & bit) != 0
        keep = jnp.where(high, pairs[:, 1], pairs[:, 0])
        came = swap(jnp.where(high, pairs[:, 0], pairs[:, 1]), axis, bit)
        x = (keep.astype(f32) + came.astype(f32)).astype(bf16)
    return x[0]


def sum_all(x):
    for axis in ("expert", "wshard"):
        for bit in bits_of(lax.axis_size(axis)):
            x = x + swap(x, axis, bit)
    return x


def relative(owners):
    rel = [0]
    for bit in reversed(bits_of(owners)):
        rel += [r ^ bit for r in rel]
    return rel


def gather_relative(x, axis):
    blocks = [x]
    for bit in reversed(bits_of(lax.axis_size(axis))):
        blocks += [swap(b, axis, bit) for b in blocks]
    return blocks


def scatter_relative(blocks, axis):
    for bit in bits_of(lax.axis_size(axis)):
        half = len(blocks) // 2
        came = [swap(b.astype(bf16), axis, bit) for b in blocks[half:]]
        blocks = [b + c.astype(f32) for b, c in zip(blocks[:half], came)]
    return blocks[0]


def expert_kernel(n, owner, x_ref, g_ref, m_ref, *refs):
    weights = refs[:n]
    y_ref, dx_ref, mg_ref = refs[n : n + 3]
    grads = refs[n + 3 :]
    depth = weights[0].shape[0] // 3

    @pl.when(pl.program_id(0) == 0)
    def _():
        y_ref[...] = jnp.zeros_like(y_ref)
        dx_ref[...] = jnp.zeros_like(dx_ref)
        mg_ref[...] = jnp.zeros_like(mg_ref)

    columns = [pl.ds(pl.multiple_of(owner[j] * depth, depth), depth) for j in range(n)]
    gate = up = back = None
    for j in range(n):
        x, g = x_ref[:, columns[j]], g_ref[:, columns[j]]
        a = mm(x, weights[j][:depth])
        b = mm(x, weights[j][depth : 2 * depth])
        c = mm(g, weights[j][2 * depth :])
        gate, up, back = (a, b, c) if j == 0 else (gate + a, up + b, back + c)
    sig = 1.0 / (1.0 + jnp.exp(-gate))
    act = gate * sig
    hidden = act * up
    mix = m_ref[...]
    mg_ref[...] += jnp.sum(hidden * back, axis=1, keepdims=True)
    mixed = (mix * hidden).astype(bf16)
    hidden_grad = mix * back
    gate_grad = (hidden_grad * up * sig * (1.0 + gate * (1.0 - sig))).astype(bf16)
    up_grad = (hidden_grad * act).astype(bf16)
    for j in range(n):
        x, g = x_ref[:, columns[j]], g_ref[:, columns[j]]
        y_ref[:, columns[j]] += mm(mixed, weights[j][2 * depth :], NT)
        dx_ref[:, columns[j]] += mm(gate_grad, weights[j][:depth], NT) + mm(
            up_grad, weights[j][depth : 2 * depth], NT
        )
        grads[j][:depth] = mm(x, gate_grad, TN).astype(bf16)
        grads[j][depth : 2 * depth] = mm(x, up_grad, TN).astype(bf16)
        grads[j][2 * depth :] = mm(g, mixed, TN).astype(bf16)


def expert_pass(owner, x, g, mix, weights, width=256):
    n = len(weights)
    rows, model = x.shape
    deep, hidden = weights[0].shape

    def full(columns):
        return pl.BlockSpec((rows, columns), lambda f, o: (0, 0), pipeline_mode=pl.Buffered(1))

    part = pl.BlockSpec((deep, width), lambda f, o: (0, f))
    out = pl.pallas_call(
        functools.partial(expert_kernel, n),
        grid_spec=pltpu.PrefetchScalarGridSpec(
            num_scalar_prefetch=1,
            grid=(hidden // width,),
            in_specs=[full(model), full(model), full(1)] + [part] * n,
            out_specs=[full(model), full(model), full(1)] + [part] * n,
        ),
        out_shape=[jax.ShapeDtypeStruct((rows, model), f32)] * 2
        + [jax.ShapeDtypeStruct((rows, 1), f32)]
        + [jax.ShapeDtypeStruct((deep, hidden), bf16)] * n,
        compiler_params=pltpu.CompilerParams(vmem_limit_bytes=56 << 20),
    )(owner, x, g, mix, *weights)
    return out[0], out[1], out[2], out[3:]


def inverse_rms(values):
    return lax.rsqrt(jnp.mean(values * values, axis=-1, keepdims=True) + epsilon)


def norm_back(values, inverse, gain_vector, grad_rows):
    scaled = values * inverse
    weighted = grad_rows * gain_vector
    return inverse * (weighted - scaled * jnp.mean(weighted * scaled, axis=-1, keepdims=True))


def rotate(values, cosine, sine):
    half_dim = values.shape[-1] // 2
    first, second = values[..., :half_dim], values[..., half_dim:]
    return jnp.concatenate([first * cosine - second * sine, second * cosine + first * sine], axis=-1)


def by_head(rows, heads):
    return rows.reshape(rows.shape[0], heads, HEAD_DIM).transpose(1, 0, 2)


def by_row(heads):
    return heads.transpose(1, 0, 2).reshape(heads.shape[1], -1)


def local(
    tokens,
    segment_ids,
    routes,
    attn_gain,
    query_weight,
    key_weight,
    value_weight,
    out_weight,
    query_gain,
    key_gain,
    ffn_gain,
    router_weight,
    gate_weight,
    up_weight,
    down_weight,
    d_output,
):
    rows, model = tokens.shape
    owners, shards = lax.axis_size("expert"), lax.axis_size("wshard")
    rank = lax.axis_index("expert")
    local_experts = gate_weight.shape[0]
    experts = local_experts * owners
    heads = HEADS // shards
    wide = heads * HEAD_DIM
    root_dim = math.sqrt(HEAD_DIM)
    ring = Ring("wshard")
    rel = relative(owners)

    token_blocks = ring.gather(tokens)
    quarter = query_weight.shape[0] // owners
    own_rows = jnp.stack(
        [
            lax.dynamic_slice_in_dim(w, rank * quarter, quarter).reshape(quarter, shards, wide)
            for w in (query_weight, key_weight, value_weight)
        ],
        axis=2,
    )
    own_columns = lax.all_to_all(
        own_rows.transpose(1, 0, 2, 3), "wshard", split_axis=0, concat_axis=0, tiled=True
    )
    qkv_weight = (
        gather_bits(own_columns.reshape(shards, quarter, 3 * wide), "expert")
        .transpose(1, 0, 2, 3)
        .reshape(model, 3 * wide)
    )
    named = jnp.sum(
        (routes[:, :, None] == jnp.arange(experts, dtype=jnp.int32)).astype(f32), axis=1
    )
    named_all = jnp.concatenate(gather_relative(named, "expert"), axis=0)
    grad_all = jnp.concatenate(gather_relative(d_output, "expert"), axis=0)
    packed = [
        jnp.concatenate([gate_weight[i], up_weight[i], down_weight[i].T], axis=0)
        for i in range(local_experts)
    ]
    expert_weights = [ring.gather(packed[i], far_up=i % 2 == 1) for i in range(local_experts)]

    stream_all = jnp.concatenate(token_blocks, axis=0).astype(f32)
    inverse_all = inverse_rms(stream_all)
    normed_all = (stream_all * inverse_all * attn_gain).astype(bf16)
    sequence = rows * shards
    position = (ring.owner[:, None] * rows + jnp.arange(rows, dtype=jnp.int32)).reshape(-1)
    frequency = rope_base ** (
        -2.0 * jnp.arange(HEAD_DIM // 2, dtype=f32) / HEAD_DIM
    )
    angles = position.astype(f32)[:, None] * frequency[None, :]
    cosine, sine = jnp.cos(angles), jnp.sin(angles)
    segments = segment_ids.reshape(shards, rows)[ring.owner].reshape(-1)
    same = (segments[:, None] == segments[None, :])[None]

    raw = mm(normed_all, qkv_weight)
    query_raw = by_head(raw[:, :wide], heads)
    key_raw = by_head(raw[:, wide : 2 * wide], heads)
    values = by_head(raw[:, 2 * wide :].astype(bf16), heads)
    query_inverse, key_inverse = inverse_rms(query_raw), inverse_rms(key_raw)
    queries = rotate(query_raw * query_inverse * query_gain, cosine, sine).astype(bf16)
    keys = rotate(key_raw * key_inverse * key_gain, cosine, sine).astype(bf16)
    scores = jnp.einsum("hqd,hkd->hqk", queries, keys, preferred_element_type=f32) / root_dim
    scores = jnp.where(same, scores, -1e30)
    exponent = jnp.exp(scores - jnp.max(scores, axis=-1, keepdims=True))
    probs = exponent / jnp.sum(exponent, axis=-1, keepdims=True)
    probs_low = probs.astype(bf16)
    mixed = by_row(
        jnp.einsum("hqk,hkd->hqd", probs_low, values, preferred_element_type=f32).astype(bf16)
    )
    attended_part = mm(mixed, out_weight).astype(bf16).reshape(shards, rows, model)
    attended = ring.scatter([attended_part[j] for j in range(shards)])

    stream = tokens.astype(f32)
    middle = stream + attended
    ffn_inverse = inverse_rms(middle)
    ffn_low = (middle * ffn_inverse * ffn_gain).astype(bf16)

    ffn_all = jnp.concatenate(gather_relative(ffn_low, "expert"), axis=0)
    logits = mm(ffn_all, router_weight)
    logits = jnp.where(named_all > 0, logits, -jnp.inf)
    lifted = jnp.exp(logits - jnp.max(logits, axis=1, keepdims=True))
    mixing = lifted / jnp.sum(lifted, axis=1, keepdims=True)
    which = jnp.arange(experts, dtype=jnp.int32)[None, :]
    produced = row_grads = None
    mixing_grads = []
    weight_parts = []
    for i in range(local_experts):
        mix = jnp.sum(
            jnp.where(which == rank * local_experts + i, mixing, 0.0), axis=1, keepdims=True
        )
        y, dx, mg, parts = expert_pass(ring.owner, ffn_all, grad_all, mix, expert_weights[i])
        produced = y if i == 0 else produced + y
        row_grads = dx if i == 0 else row_grads + dx
        mixing_grads.append(mg)
        weight_parts.append(parts)

    def split(values):
        return [values[j * rows : (j + 1) * rows] for j in range(owners)]

    ffn_grad = scatter_relative(split(row_grads), "expert")
    expert_out = scatter_relative(split(produced), "expert")
    mixing_own = mixing[:rows]
    mixing_grad = jnp.zeros_like(mixing_own)
    for r, block in zip(rel, split(jnp.concatenate(mixing_grads, axis=1))):
        came = block
        if r:
            came = lax.ppermute(block, "expert", [(i, i ^ r) for i in range(owners)])
        for i in range(local_experts):
            at = which == (rank ^ r) * local_experts + i
            mixing_grad = jnp.where(at, came[:, i : i + 1], mixing_grad)

    final_stream = middle + expert_out
    output = final_stream.astype(bf16)
    logits_grad = mixing_own * (
        mixing_grad - jnp.sum(mixing_own * mixing_grad, axis=1, keepdims=True)
    )
    router_grad = lax.dot_general(
        logits_grad, ffn_low.astype(f32), TN, precision=highest, preferred_element_type=f32
    )
    ffn_grad = ffn_grad + lax.dot_general(
        logits_grad, router_weight.astype(f32), NT, precision=highest, preferred_element_type=f32
    )
    ffn_gain_grad = jnp.sum(ffn_grad * (middle * ffn_inverse), axis=0)
    middle_grad = d_output.astype(f32) + norm_back(middle, ffn_inverse, ffn_gain, ffn_grad)
    attended_low = middle_grad.astype(bf16)

    attended_all = jnp.concatenate(ring.gather(attended_low), axis=0)
    mixed_grad = by_head(mm(attended_all, out_weight, NT).astype(bf16), heads)
    out_grad = mm(mixed, attended_all, TN)
    probs_grad = jnp.einsum("hqd,hkd->hqk", mixed_grad, values, preferred_element_type=f32)
    scores_grad = (
        probs * (probs_grad - jnp.sum(probs * probs_grad, axis=-1, keepdims=True))
    ).astype(bf16)
    query_rot = jnp.einsum("hqk,hkd->hqd", scores_grad, keys, preferred_element_type=f32) / root_dim
    key_rot = jnp.einsum("hqk,hqd->hkd", scores_grad, queries, preferred_element_type=f32) / root_dim
    value_grad = jnp.einsum(
        "hqk,hqd->hkd", probs_low, mixed_grad, preferred_element_type=f32
    ).astype(bf16)
    query_grad = rotate(query_rot, cosine, -sine)
    key_grad = rotate(key_rot, cosine, -sine)
    query_gain_grad = jnp.sum(query_grad * (query_raw * query_inverse), axis=(0, 1))
    key_gain_grad = jnp.sum(key_grad * (key_raw * key_inverse), axis=(0, 1))
    query_low = norm_back(query_raw, query_inverse, query_gain, query_grad).astype(bf16)
    key_low = norm_back(key_raw, key_inverse, key_gain, key_grad).astype(bf16)
    raw_grad = jnp.concatenate([by_row(query_low), by_row(key_low), by_row(value_grad)], axis=1)

    normed_part = mm(raw_grad, qkv_weight, NT)
    attn_gain_grad = jnp.sum(normed_part * (stream_all * inverse_all), axis=0)
    normed_part = normed_part.astype(bf16).reshape(shards, rows, model)
    normed_grad = ring.scatter([normed_part[j] for j in range(shards)])
    tokens_grad = (
        middle_grad + norm_back(stream, inverse_all[:rows], attn_gain, normed_grad)
    ).astype(bf16)

    qkv_grad = mm(normed_all, raw_grad, TN).astype(bf16)
    qkv_grad = qkv_grad.reshape(shards, owners, quarter, 3 * wide).transpose(1, 0, 2, 3)
    qkv_grad = scatter_bits(qkv_grad, "expert")
    qkv_grad = lax.all_to_all(qkv_grad, "wshard", split_axis=0, concat_axis=0, tiled=True)
    qkv_grad = gather_bits(qkv_grad, "expert").reshape(owners, shards, quarter, 3, wide)
    qkv_grad = qkv_grad.transpose(3, 0, 2, 1, 4).reshape(3, owners * quarter, model).astype(f32)
    out_grad = out_grad.astype(bf16).reshape(owners, -1, model)
    out_grad = gather_bits(scatter_bits(out_grad, "expert"), "expert")
    out_grad = out_grad.reshape(-1, model).astype(f32)
    summed = [ring.scatter(weight_parts[i], far_up=i % 2 == 1) for i in range(local_experts)]
    depth = gate_weight.shape[1]
    gate_weight_grad = jnp.stack([s[:depth] for s in summed])
    up_weight_grad = jnp.stack([s[depth : 2 * depth] for s in summed])
    down_weight_grad = jnp.stack([s[2 * depth :].T for s in summed])

    squares = jnp.stack(
        [
            jnp.sum(middle * middle),
            jnp.sum(final_stream * final_stream),
            jnp.sum(attended * attended),
            jnp.sum(expert_out * expert_out),
        ]
    )
    early = jnp.concatenate([router_grad.reshape(-1), ffn_gain_grad, jnp.pad(squares, (0, 124))])
    early = sum_all(early.reshape(-1, 128)).reshape(-1)
    late = jnp.concatenate([attn_gain_grad, query_gain_grad, key_gain_grad])
    late = sum_all(late.reshape(-1, 128)).reshape(-1)
    router_size = experts * model
    router_weight_grad = early[:router_size].reshape(experts, model).T
    ffn_gain_grad = early[router_size : router_size + model]
    stream_rms = jnp.sqrt(
        early[router_size + model : router_size + model + 4] / (rows * owners * shards * model)
    )
    return (
        output,
        tokens_grad,
        late[:model],
        qkv_grad[0],
        qkv_grad[1],
        qkv_grad[2],
        out_grad,
        late[model : model + HEAD_DIM],
        late[model + HEAD_DIM :],
        ffn_gain_grad,
        router_weight_grad,
        gate_weight_grad,
        up_weight_grad,
        down_weight_grad,
        stream_rms,
    )


def solution(mesh):
    rows = P(("expert", "wshard"), None)
    shard = P("wshard", None)
    wide = P("expert", "wshard", None)
    tall = P("expert", None, "wshard")
    return jax.shard_map(
        local,
        mesh=mesh,
        in_specs=(rows, P("expert"), rows, P(), shard, shard, shard, shard)
        + (P(), P(), P(), P(), wide, wide, tall, rows),
        out_specs=(rows, rows, P(), shard, shard, shard, shard)
        + (P(), P(), P(), P(), wide, wide, tall, P()),
        check_vma=False,
    )
```

time: 2800 us -> 1050 us (0.38)
  waiting for transfers between devices: 2280 us -> 641 us
  matrix products: 214 us -> 42.9 us
  blocking collectives: 95.2 us -> 0 us
  starting transfers between devices: 16.8 us -> 105 us
  Pallas kernels: 0 us -> 70.2 us
  other arithmetic: 59.9 us -> 91.9 us
    reduce_scatter x7 -> x0, waiting for transfers between devices: 955 us -> none  [the longest x1 152 us: local(): lax.psum_scatter(query_grad_all.astype(jnp.bfloat16), 'wshard', scatter_d...]
    all_gather x9 -> x0, waiting for transfers between devices: 919 us -> none  [the longest x1 126 us: local(): lax.all_gather(query_weight, 'wshard', axis=0, tiled=True)]
    ppermute x0 -> x94, waiting for transfers between devices: none -> 631 us  [the longest x28 285 us: chain(): came = lax.ppermute(moving, self.axis, perm)]
    psum x2 -> x0, waiting for transfers between devices: 200 us -> none  [the longest x1 115 us: local(): lax.psum((attn_gain_grad, ffn_gain_grad, query_gain_grad, key_gain_grad,...]
    dot_general x32 -> x14, matrix products: 214 us -> 33.9 us  [the longest x7 20.5 us: mm(): return lax.dot_general(a, b, dims, preferred_element_type=f32)]
    unnamed x22 -> x0, waiting for transfers between devices: 122 us -> none
    ppermute x0 -> x94, starting transfers between devices: none -> 94.6 us  [the longest x28 26.6 us: chain(): came = lax.ppermute(moving, self.axis, perm)]
    all_to_all x3 -> x2, waiting for transfers between devices: 85.3 us -> 9.27 us  [the longest x1 9.26 us: local(): lax.all_to_all(own_rows.transpose(1, 0, 2, 3), 'wshard', split_axis=0, co...]
  transfers between devices with their start and end apart: 23 -> 96, of which waited for: 22 -> 43; matrix products, arithmetic and copies ran while one was open for 9% -> 16% of each run, Pallas kernels for 0% -> 3%
where the time goes in v1:
time: 1050 us; the launch traced here: 1040 us
  waiting for transfers between devices  641 us (61%)
  starting transfers between devices  105 us (10%)
  other arithmetic  91.9 us (9%)
  local copies, waits for them, and re-layouts  90.6 us (9%)
  Pallas kernels  70.2 us (7%)
  matrix products  42.9 us (4%)
    ppermute x28, waiting for transfers between devices, chain(): came = lax.ppermute(moving, self.axis, perm)  285 us
    ppermute x15, waiting for transfers between devices, gather(): down = lax.ppermute(down, self.axis, self.down)  188 us
    ppermute x35, waiting for transfers between devices, swap(): lax.ppermute(x, axis, [(i, i ^ bit) for i in range(lax.axis_size(axis))])  139 us
    pallas_call x2, Pallas kernels, expert_pass(): pl.pallas_call(functools.partial(expert_kernel, n), grid_spec=pltpu.Prefe...  70.2 us
    convert_element_type x16, other arithmetic, chain(): moving = (came.astype(f32) + part[sign * s].astype(f32)).astype(bf16)  27.8 us
    ppermute x28, starting transfers between devices, chain(): came = lax.ppermute(moving, self.axis, perm)  26.6 us
    ppermute x15, starting transfers between devices, gather(): down = lax.ppermute(down, self.axis, self.down)  26 us
    ppermute x35, starting transfers between devices, swap(): lax.ppermute(x, axis, [(i, i ^ bit) for i in range(lax.axis_size(axis))])  25.4 us
  transfers between devices with their start and end apart: 96, of which 43 were waited for; matrix products, arithmetic and copies ran while one was open for 16% of the time, Pallas kernels for 3%

profile of v1, /device:TPU:0, one launch (start us, length us, event | category | flops | bytes accessed | tf_op | source)
XLA Modules:
  0.0 1044.2 jit_solution(2076799200536811332)
XLA Ops:
  7.1 6.3 all-to-all-start
  25.9 9.3 all-to-all-done
  48.2 24.6 %collective-permute-done.2 = bf16[128,2048]{1,0:T(8,128)(2,1)} collective-permute-done((bf16[128,2048]{1,0:T(8,128)(2,1)}, bf16[128,2048]{1,0:T(8,128)(2,1)}, u32[]{:S(2)}, u32[]{:S(2)}) %collective-permute-start.2) | collective-permute-done | bytes 524320 | tf_op jit(solution)/shard_map/ppermute | solution.py:54
  80.1 9.2 collective-permute-done.4
  93.1 10.2 collective-permute-done.6
  117.3 8.9 fusion.81
  151.0 63.7 %collective-permute-done.13 = bf16[128,2048]{1,0:T(8,128)(2,1)S(1)} collective-permute-done((bf16[128,2048]{1,0:T(8,128)(2,1)}, bf16[128,2048]{1,0:T(8,128)(2,1)S(1)}, u32[]{:S(2)}, u32[]{:S(2)}) %collective-permute-start.13) | collective-permute-done | bytes 524320 | tf_op jit(solution)/shard_map/ppermute | solution.py:68
  219.5 43.4 %collective-permute-done.11 = bf16[128,2048]{1,0:T(8,128)(2,1)S(1)} collective-permute-done((bf16[128,2048]{1,0:T(8,128)(2,1)S(1)}, bf16[128,2048]{1,0:T(8,128)(2,1)S(1)}, u32[]{:S(2)}, u32[]{:S(2)}) %collective-permute-start.11) | collective-permute-done | bytes 524320 | tf_op jit(solution)/shard_map/ppermute | solution.py:68
  268.0 8.5 collective-permute-done.19
  280.4 11.3 %collective-permute-done.12 = bf16[128,2048]{1,0:T(8,128)(2,1)} collective-permute-done((bf16[128,2048]{1,0:T(8,128)(2,1)}, bf16[128,2048]{1,0:T(8,128)(2,1)}, u32[]{:S(2)}, u32[]{:S(2)}) %collective-permute-start.12) | collective-permute-done | bytes 524320 | tf_op jit(solution)/shard_map/ppermute | solution.py:68
  293.5 18.9 %collective-permute-done.15 = bf16[128,2048]{1,0:T(8,128)(2,1)} collective-permute-done((bf16[128,2048]{1,0:T(8,128)(2,1)}, bf16[128,2048]{1,0:T(8,128)(2,1)}, u32[]{:S(2)}, u32[]{:S(2)}) %collective-permute-start.15) | collective-permute-done | bytes 524320 | tf_op jit(solution)/shard_map/ppermute | solution.py:68
  327.0 30.0 %collective-permute-done.29.refs_5_ = bf16[768,1024]{1,0:T(8,128)(2,1)} collective-permute-done((bf16[768,1024]{1,0:T(8,128)(2,1)}, bf16[768,1024]{1,0:T(8,128)(2,1)}, u32[]{:S(2)}, u32[]{:S(2)}) %collective-permute-start.29) | collective-permute-done | bytes 1572896 | tf_op jit(solution)/shard_map/ppermute | solution.py:54
  366.4 28.3 %collective-permute-done.36.refs_5_ = bf16[768,1024]{1,0:T(8,128)(2,1)} collective-permute-done((bf16[768,1024]{1,0:T(8,128)(2,1)}, bf16[768,1024]{1,0:T(8,128)(2,1)}, u32[]{:S(2)}, u32[]{:S(2)}) %collective-permute-start.36) | collective-permute-done | bytes 1572896 | tf_op jit(solution)/shard_map/ppermute | solution.py:54
  394.7 19.9 %collective-permute-done.38.refs_7_ = bf16[768,1024]{1,0:T(8,128)(2,1)} collective-permute-done((bf16[768,1024]{1,0:T(8,128)(2,1)}, bf16[768,1024]{1,0:T(8,128)(2,1)}, u32[]{:S(2)}, u32[]{:S(2)}) %collective-permute-start.38) | collective-permute-done | bytes 1572896 | tf_op jit(solution)/shard_map/ppermute | solution.py:57
  414.6 35.0 %shard_map.299 = (f32[512,2048]{1,0:T(8,128)}, f32[512,2048]{1,0:T(8,128)}, f32[512,1]{1,0:T(8,128)}, bf16[768,1024]{1,0:T(8,128)(2,1)}, bf16[768,1024]{1,0:T(8,...) custom-call(s32[8]{0:T(128)} %copy-done.78, ...), custom_call_target="tpu_custom_call" | custom-call | tf_op jit(solution)/shard_map/pallas_call | solution.py:186
  451.6 35.2 %shard_map.298 = (f32[512,2048]{1,0:T(8,128)}, f32[512,2048]{1,0:T(8,128)}, f32[512,1]{1,0:T(8,128)}, bf16[768,1024]{1,0:T(8,128)(2,1)}, bf16[768,1024]{1,0:T(8,...) custom-call(s32[8]{0:T(128)} %copy-done.78, ...), custom_call_target="tpu_custom_call" | custom-call | tf_op jit(solution)/shard_map/pallas_call | solution.py:186
  503.4 12.0 %collective-permute-done.44 = bf16[128,2048]{1,0:T(8,128)(2,1)S(1)} collective-permute-done((bf16[128,2048]{1,0:T(8,128)(2,1)S(1)}, bf16[128,2048]{1,0:T(8,128)(2,1)S(1)}, u32[]{:S(2)}, u32[]{:S(2)}) %collective-permute-start.44) | collective-permute-done | bytes 524320 | tf_op jit(solution)/shard_map/ppermute | solution.py:83
  516.2 9.6 collective-permute-done.41
  540.8 31.9 %collective-permute-done.77 = f32[145,128]{1,0:T(8,128)S(1)} collective-permute-done((f32[145,128]{1,0:T(8,128)S(1)}, f32[145,128]{1,0:T(8,128)S(1)}, u32[]{:S(2)}, u32[]{:S(2)}) %collective-permute-start.77) | collective-permute-done | bytes 74272 | tf_op jit(solution)/shard_map/ppermute | solution.py:83
  572.8 36.2 %collective-permute-done.78 = f32[145,128]{1,0:T(8,128)S(1)} collective-permute-done((f32[145,128]{1,0:T(8,128)S(1)}, f32[145,128]{1,0:T(8,128)S(1)}, u32[]{:S(2)}, u32[]{:S(2)}) %collective-permute-start.78) | collective-permute-done | bytes 74272 | tf_op jit(solution)/shard_map/ppermute | solution.py:83
  638.3 36.6 %collective-permute-done.50 = bf16[128,2048]{1,0:T(8,128)(2,1)S(1)} collective-permute-done((bf16[128,2048]{1,0:T(8,128)(2,1)}, bf16[128,2048]{1,0:T(8,128)(2,1)S(1)}, u32[]{:S(2)}, u32[]{:S(2)}) %collective-permute-start.50) | collective-permute-done | bytes 524320 | tf_op jit(solution)/shard_map/ppermute | solution.py:54
  678.3 38.6 %collective-permute-done.52 = bf16[128,2048]{1,0:T(8,128)(2,1)S(1)} collective-permute-done((bf16[128,2048]{1,0:T(8,128)(2,1)S(1)}, bf16[128,2048]{1,0:T(8,128)(2,1)S(1)}, u32[]{:S(2)}, u32[]{:S(2)}) %collective-permute-start.52) | collective-permute-done | bytes 524320 | tf_op jit(solution)/shard_map/ppermute | solution.py:54
  725.5 22.8 %collective-permute-done.91 = bf16[768,1024]{1,0:T(8,128)(2,1)S(1)} collective-permute-done((bf16[768,1024]{1,0:T(8,128)(2,1)S(1)}, bf16[768,1024]{1,0:T(8,128)(2,1)S(1)}, u32[]{:S(2)}, u32[]{:S(2)}) %collective-permute-start.91) | collective-permute-done | bytes 1572896 | tf_op jit(solution)/shard_map/ppermute | solution.py:68
  775.6 6.5 convolution_convert_fusion.1
  818.3 10.1 collective-permute-done.56
  830.5 6.9 collective-permute-done.73
  845.4 38.8 %collective-permute-done.92 = bf16[768,1024]{1,0:T(8,128)(2,1)S(1)} collective-permute-done((bf16[768,1024]{1,0:T(8,128)(2,1)S(1)}, bf16[768,1024]{1,0:T(8,128)(2,1)S(1)}, u32[]{:S(2)}, u32[]{:S(2)}) %collective-permute-start.92) | collective-permute-done | bytes 1572896 | tf_op jit(solution)/shard_map/ppermute | solution.py:68
  903.2 48.1 %collective-permute-done.58 = bf16[128,2048]{1,0:T(8,128)(2,1)S(1)} collective-permute-done((bf16[128,2048]{1,0:T(8,128)(2,1)S(1)}, bf16[128,2048]{1,0:T(8,128)(2,1)S(1)}, u32[]{:S(2)}, u32[]{:S(2)}) %collective-permute-start.58) | collective-permute-done | bytes 524320 | tf_op jit(solution)/shard_map/ppermute | solution.py:68
  962.1 12.6 %collective-permute-done.69 = bf16[1,8,64,768]{3,2,1,0:T(8,128)(2,1)S(1)} collective-permute-done((bf16[1,8,64,768]{3,2,1,0:T(8,128)(2,1)}, bf16[1,8,64,768]{3,2,1,0:T(8,128)(2,1)S(1)}, u32[]{:S(2)}, u32[]{:S(2)}) %collective-permute-start.69) | collective-permute-done | bytes 786464 | tf_op jit(solution)/shard_map/ppermute | solution.py:83
  979.9 11.8 %collective-permute-done.93 = bf16[768,1024]{1,0:T(8,128)(2,1)} collective-permute-done((bf16[768,1024]{1,0:T(8,128)(2,1)}, bf16[768,1024]{1,0:T(8,128)(2,1)}, u32[]{:S(2)}, u32[]{:S(2)}) %collective-permute-start.93) | collective-permute-done | bytes 1572896 | tf_op jit(solution)/shard_map/ppermute | solution.py:68
  1008.5 10.7 %reshape.558 = f32[4,8,64,3,256]{4,3,2,1,0:T(4,128)} reshape(f32[2,2,8,64,768]{4,3,2,1,0:T(8,128)} %copy.192) | data formatting | bytes 12582912 | tf_op jit(solution)/shard_map/convert_element_type | solution.py:401
  1019.2 14.3 %fusion.73 = (f32[1,4,64,8,256]{4,0,2,3,1:T(1,128)S(1)}, f32[1,4,64,8,256]{4,0,2,3,1:T(1,128)S(1)}, f32[1,4,64,8,256]{4,0,2,3,1:T(1,128)S(1)}) fusion(f32[3,4,64,8,256]{4,0,2,3,1:T(4,128)} %bitcast.276), kind=kLoop, calls=%fused_computation.271 | loop fusion | bytes 12582912 | tf_op jit(solution)/shard_map/slice | solution.py:435
  (535 shorter events, 331.1 us)
Async XLA Ops:
  19.7 131.0 %collective-permute-start.25 = (bf16[768,1024]{1,0:T(8,128)(2,1)}, bf16[768,1024]{1,0:T(8,128)(2,1)}, u32[]{:S(2)}, u32[]{:S(2)}) collective-permute-start(bf16[768,1024]{1,0:T(8,128)(2,1)} %pad_maximum_fusion.5.refs_0_), channel_id=1, source_target_pairs={{0,2},{2,4},{4,6},{6,7},{7,5},{5,3},{3,1},{1,0},{8,10},{10,12},{12... | collective-permute-start | bytes 4718600 | tf_op jit(solution)/shard_map/ppermute | solution.py:54
  135.8 83.2 %collective-permute-start.26 = (bf16[768,1024]{1,0:T(8,128)(2,1)}, bf16[768,1024]{1,0:T(8,128)(2,1)}, u32[]{:S(2)}, u32[]{:S(2)}) collective-permute-start(bf16[768,1024]{1,0:T(8,128)(2,1)} %pad_maximum_fusion.5.refs_0_), channel_id=1, source_target_pairs={{2,0},{4,2},{6,4},{7,6},{5,7},{3,5},{1,3},{0,1},{10,8},{12,10},{14... | collective-permute-start | bytes 4718600 | tf_op jit(solution)/shard_map/ppermute | solution.py:57
  137.7 80.1 %collective-permute-start.33 = (bf16[768,1024]{1,0:T(8,128)(2,1)S(1)}, bf16[768,1024]{1,0:T(8,128)(2,1)}, u32[]{:S(2)}, u32[]{:S(2)}) collective-permute-start(bf16[768,1024]{1,0:T(8,128)(2,1)S(1)} %pad_maximum_fusion.6.refs_0_), channel_id=1, source_target_pairs={{2,0},{4,2},{6,4},{7,6},{5,7},{3,5},{1,3},{0,1},{10,8},{12,10},{14... | collective-permute-start | bytes 4718600 | tf_op jit(solution)/shard_map/ppermute | solution.py:57
  147.3 67.4 %collective-permute-start.13 = (bf16[128,2048]{1,0:T(8,128)(2,1)}, bf16[128,2048]{1,0:T(8,128)(2,1)S(1)}, u32[]{:S(2)}, u32[]{:S(2)}) collective-permute-start(bf16[128,2048]{1,0:T(8,128)(2,1)} %get-tuple-element.174), channel_id=1, source_target_pairs={{2,0},{4,2},{6,4},{7,6},{5,7},{3,5},{1,3},{0,1},{10,8},{12,10},{14... | collective-permute-start | bytes 1572872 | tf_op jit(solution)/shard_map/ppermute | solution.py:68
  150.1 64.6 %collective-permute-start.10 = (bf16[128,2048]{1,0:T(8,128)(2,1)S(1)}, bf16[128,2048]{1,0:T(8,128)(2,1)S(1)}, u32[]{:S(2)}, u32[]{:S(2)}) collective-permute-start(bf16[128,2048]{1,0:T(8,128)(2,1)S(1)} %add_convert_fusion.19), channel_id=1, source_target_pairs={{0,2},{2,4},{4,6},{6,7},{7,5},{5,3},{3,1},{1,0},{8,10},{10,12},{12... | collective-permute-start | bytes 1572872 | tf_op jit(solution)/shard_map/ppermute | solution.py:68
  150.7 127.6 %collective-permute-start.32 = (bf16[768,1024]{1,0:T(8,128)(2,1)S(1)}, bf16[768,1024]{1,0:T(8,128)(2,1)S(1)}, u32[]{:S(2)}, u32[]{:S(2)}) collective-permute-start(bf16[768,1024]{1,0:T(8,128)(2,1)S(1)} %pad_maximum_fusion.6.refs_0_), channel_id=1, source_target_pairs={{0,2},{2,4},{4,6},{6,7},{7,5},{5,3},{3,1},{1,0},{8,10},{10,12},{12... | collective-permute-start | bytes 4718600 | tf_op jit(solution)/shard_map/ppermute | solution.py:54
  214.7 64.7 %collective-permute-start.27 = (bf16[768,1024]{1,0:T(8,128)(2,1)}, bf16[768,1024]{1,0:T(8,128)(2,1)}, u32[]{:S(2)}, u32[]{:S(2)}) collective-permute-start(bf16[768,1024]{1,0:T(8,128)(2,1)} %collective-permute-done.25.refs_1_), channel_id=1, source_target_pairs={{0,2},{2,4},{4,6},{6,7},{7,5},{5,3},{3,1},{1,0},{8,10},{10,12},{12... | collective-permute-start | bytes 4718600 | tf_op jit(solution)/shard_map/ppermute | solution.py:54
  217.8 61.7 %collective-permute-start.35 = (bf16[768,1024]{1,0:T(8,128)(2,1)}, bf16[768,1024]{1,0:T(8,128)(2,1)}, u32[]{:S(2)}, u32[]{:S(2)}) collective-permute-start(bf16[768,1024]{1,0:T(8,128)(2,1)} %collective-permute-done.33.refs_2_), channel_id=1, source_target_pairs={{2,0},{4,2},{6,4},{7,6},{5,7},{3,5},{1,3},{0,1},{10,8},{12,10},{14... | collective-permute-start | bytes 4718600 | tf_op jit(solution)/shard_map/ppermute | solution.py:57
  219.0 46.5 %collective-permute-start.14 = (bf16[128,2048]{1,0:T(8,128)(2,1)S(1)}, bf16[128,2048]{1,0:T(8,128)(2,1)S(1)}, u32[]{:S(2)}, u32[]{:S(2)}) collective-permute-start(bf16[128,2048]{1,0:T(8,128)(2,1)S(1)} %get-tuple-element.172), channel_id=1, source_target_pairs={{2,0},{4,2},{6,4},{7,6},{5,7},{3,5},{1,3},{0,1},{10,8},{12,10},{14... | collective-permute-start | bytes 1572872 | tf_op jit(solution)/shard_map/ppermute | solution.py:68
  265.5 54.0 %collective-permute-start.28 = (bf16[768,1024]{1,0:T(8,128)(2,1)}, bf16[768,1024]{1,0:T(8,128)(2,1)}, u32[]{:S(2)}, u32[]{:S(2)}) collective-permute-start(bf16[768,1024]{1,0:T(8,128)(2,1)} %collective-permute-done.26.refs_2_), channel_id=1, source_target_pairs={{2,0},{4,2},{6,4},{7,6},{5,7},{3,5},{1,3},{0,1},{10,8},{12,10},{14... | collective-permute-start | bytes 4718600 | tf_op jit(solution)/shard_map/ppermute | solution.py:57
  291.7 65.3 %collective-permute-start.29 = (bf16[768,1024]{1,0:T(8,128)(2,1)}, bf16[768,1024]{1,0:T(8,128)(2,1)}, u32[]{:S(2)}, u32[]{:S(2)}) collective-permute-start(bf16[768,1024]{1,0:T(8,128)(2,1)} %collective-permute-done.27.refs_3_), channel_id=1, source_target_pairs={{0,2},{2,4},{4,6},{6,7},{7,5},{5,3},{3,1},{1,0},{8,10},{10,12},{12... | collective-permute-start | bytes 4718600 | tf_op jit(solution)/shard_map/ppermute | solution.py:54
  312.4 46.4 %collective-permute-start.37 = (bf16[768,1024]{1,0:T(8,128)(2,1)}, bf16[768,1024]{1,0:T(8,128)(2,1)}, u32[]{:S(2)}, u32[]{:S(2)}) collective-permute-start(bf16[768,1024]{1,0:T(8,128)(2,1)} %collective-permute-done.35.refs_4_), channel_id=1, source_target_pairs={{2,0},{4,2},{6,4},{7,6},{5,7},{3,5},{1,3},{0,1},{10,8},{12,10},{14... | collective-permute-start | bytes 4718600 | tf_op jit(solution)/shard_map/ppermute | solution.py:57
  325.4 126.2 %collective-permute-start.30 = (bf16[768,1024]{1,0:T(8,128)(2,1)}, bf16[768,1024]{1,0:T(8,128)(2,1)}, u32[]{:S(2)}, u32[]{:S(2)}) collective-permute-start(bf16[768,1024]{1,0:T(8,128)(2,1)} %collective-permute-done.28.refs_4_), channel_id=1, source_target_pairs={{2,0},{4,2},{6,4},{7,6},{5,7},{3,5},{1,3},{0,1},{10,8},{12,10},{14... | collective-permute-start | bytes 4718600 | tf_op jit(solution)/shard_map/ppermute | solution.py:57
  358.8 92.8 %collective-permute-start.31 = (bf16[768,1024]{1,0:T(8,128)(2,1)}, bf16[768,1024]{1,0:T(8,128)(2,1)}, u32[]{:S(2)}, u32[]{:S(2)}) collective-permute-start(bf16[768,1024]{1,0:T(8,128)(2,1)} %collective-permute-done.29.refs_5_), channel_id=1, source_target_pairs={{0,2},{2,4},{4,6},{6,7},{7,5},{5,3},{3,1},{1,0},{8,10},{10,12},{12... | collective-permute-start | bytes 4718600 | tf_op jit(solution)/shard_map/ppermute | solution.py:54
  359.6 55.0 %collective-permute-start.38 = (bf16[768,1024]{1,0:T(8,128)(2,1)}, bf16[768,1024]{1,0:T(8,128)(2,1)}, u32[]{:S(2)}, u32[]{:S(2)}) collective-permute-start(bf16[768,1024]{1,0:T(8,128)(2,1)} %collective-permute-done.37.refs_6_), channel_id=1, source_target_pairs={{2,0},{4,2},{6,4},{7,6},{5,7},{3,5},{1,3},{0,1},{10,8},{12,10},{14... | collective-permute-start | bytes 4718600 | tf_op jit(solution)/shard_map/ppermute | solution.py:57
  533.6 83.2 %collective-permute-start.80 = (bf16[768,1024]{1,0:T(8,128)(2,1)}, bf16[768,1024]{1,0:T(8,128)(2,1)}, u32[]{:S(2)}, u32[]{:S(2)}) collective-permute-start(bf16[768,1024]{1,0:T(8,128)(2,1)} %get-tuple-element.44), channel_id=1, source_target_pairs={{0,2},{2,4},{4,6},{6,7},{7,5},{5,3},{3,1},{1,0},{8,10},{10,12},{12... | collective-permute-start | bytes 4718600 | tf_op jit(solution)/shard_map/ppermute | solution.py:68
  538.0 83.3 %collective-permute-start.84 = (bf16[768,1024]{1,0:T(8,128)(2,1)}, bf16[768,1024]{1,0:T(8,128)(2,1)}, u32[]{:S(2)}, u32[]{:S(2)}) collective-permute-start(bf16[768,1024]{1,0:T(8,128)(2,1)} %get-tuple-element.48), channel_id=1, source_target_pairs={{2,0},{4,2},{6,4},{7,6},{5,7},{3,5},{1,3},{0,1},{10,8},{12,10},{14... | collective-permute-start | bytes 4718600 | tf_op jit(solution)/shard_map/ppermute | solution.py:68
  538.6 86.8 %collective-permute-start.87 = (bf16[768,1024]{1,0:T(8,128)(2,1)}, bf16[768,1024]{1,0:T(8,128)(2,1)}, u32[]{:S(2)}, u32[]{:S(2)}) collective-permute-start(bf16[768,1024]{1,0:T(8,128)(2,1)} %get-tuple-element.52), channel_id=1, source_target_pairs={{0,2},{2,4},{4,6},{6,7},{7,5},{5,3},{3,1},{1,0},{8,10},{10,12},{12... | collective-permute-start | bytes 4718600 | tf_op jit(solution)/shard_map/ppermute | solution.py:68
  540.1 93.6 %collective-permute-start.90 = (bf16[768,1024]{1,0:T(8,128)(2,1)}, bf16[768,1024]{1,0:T(8,128)(2,1)}, u32[]{:S(2)}, u32[]{:S(2)}) collective-permute-start(bf16[768,1024]{1,0:T(8,128)(2,1)} %get-tuple-element.55), channel_id=1, source_target_pairs={{2,0},{4,2},{6,4},{7,6},{5,7},{3,5},{1,3},{0,1},{10,8},{12,10},{14... | collective-permute-start | bytes 4718600 | tf_op jit(solution)/shard_map/ppermute | solution.py:68
  621.3 97.8 %collective-permute-start.81 = (bf16[768,1024]{1,0:T(8,128)(2,1)S(1)}, bf16[768,1024]{1,0:T(8,128)(2,1)S(1)}, u32[]{:S(2)}, u32[]{:S(2)}) collective-permute-start(bf16[768,1024]{1,0:T(8,128)(2,1)S(1)} %add_convert_fusion.9), channel_id=1, source_target_pairs={{0,2},{2,4},{4,6},{6,7},{7,5},{5,3},{3,1},{1,0},{8,10},{10,12},{12... | collective-permute-start | bytes 4718600 | tf_op jit(solution)/shard_map/ppermute | solution.py:68
  625.4 96.4 %collective-permute-start.85 = (bf16[768,1024]{1,0:T(8,128)(2,1)S(1)}, bf16[768,1024]{1,0:T(8,128)(2,1)S(1)}, u32[]{:S(2)}, u32[]{:S(2)}) collective-permute-start(bf16[768,1024]{1,0:T(8,128)(2,1)S(1)} %add_convert_fusion.6), channel_id=1, source_target_pairs={{2,0},{4,2},{6,4},{7,6},{5,7},{3,5},{1,3},{0,1},{10,8},{12,10},{14... | collective-permute-start | bytes 4718600 | tf_op jit(solution)/shard_map/ppermute | solution.py:68
  633.7 90.0 %collective-permute-start.88 = (bf16[768,1024]{1,0:T(8,128)(2,1)S(1)}, bf16[768,1024]{1,0:T(8,128)(2,1)S(1)}, u32[]{:S(2)}, u32[]{:S(2)}) collective-permute-start(bf16[768,1024]{1,0:T(8,128)(2,1)S(1)} %add_convert_fusion.4), channel_id=1, source_target_pairs={{0,2},{2,4},{4,6},{6,7},{7,5},{5,3},{3,1},{1,0},{8,10},{10,12},{12... | collective-permute-start | bytes 4718600 | tf_op jit(solution)/shard_map/ppermute | solution.py:68
  721.0 121.1 %collective-permute-start.82 = (bf16[768,1024]{1,0:T(8,128)(2,1)}, bf16[768,1024]{1,0:T(8,128)(2,1)}, u32[]{:S(2)}, u32[]{:S(2)}) collective-permute-start(bf16[768,1024]{1,0:T(8,128)(2,1)} %add_convert_fusion.8), channel_id=1, source_target_pairs={{0,2},{2,4},{4,6},{6,7},{7,5},{5,3},{3,1},{1,0},{8,10},{10,12},{12... | collective-permute-start | bytes 4718600 | tf_op jit(solution)/shard_map/ppermute | solution.py:68
  815.9 143.3 %collective-permute-start.86 = (bf16[768,1024]{1,0:T(8,128)(2,1)}, bf16[768,1024]{1,0:T(8,128)(2,1)}, u32[]{:S(2)}, u32[]{:S(2)}) collective-permute-start(bf16[768,1024]{1,0:T(8,128)(2,1)} %add_convert_fusion.5), channel_id=1, source_target_pairs={{2,0},{4,2},{6,4},{7,6},{5,7},{3,5},{1,3},{0,1},{10,8},{12,10},{14... | collective-permute-start | bytes 4718600 | tf_op jit(solution)/shard_map/ppermute | solution.py:68
  816.8 163.1 %collective-permute-start.89 = (bf16[768,1024]{1,0:T(8,128)(2,1)}, bf16[768,1024]{1,0:T(8,128)(2,1)}, u32[]{:S(2)}, u32[]{:S(2)}) collective-permute-start(bf16[768,1024]{1,0:T(8,128)(2,1)} %add_convert_fusion.3), channel_id=1, source_target_pairs={{0,2},{2,4},{4,6},{6,7},{7,5},{5,3},{3,1},{1,0},{8,10},{10,12},{12... | collective-permute-start | bytes 4718600 | tf_op jit(solution)/shard_map/ppermute | solution.py:68
  837.5 46.7 %collective-permute-start.92 = (bf16[768,1024]{1,0:T(8,128)(2,1)S(1)}, bf16[768,1024]{1,0:T(8,128)(2,1)S(1)}, u32[]{:S(2)}, u32[]{:S(2)}) collective-permute-start(bf16[768,1024]{1,0:T(8,128)(2,1)S(1)} %copy-done.61), channel_id=1, source_target_pairs={{2,0},{4,2},{6,4},{7,6},{5,7},{3,5},{1,3},{0,1},{10,8},{12,10},{14... | collective-permute-start | bytes 4718600 | tf_op jit(solution)/shard_map/ppermute | solution.py:68
  839.7 46.4 %collective-permute-start.68 = (bf16[1,8,64,768]{3,2,1,0:T(8,128)(2,1)S(1)}, bf16[1,8,64,768]{3,2,1,0:T(8,128)(2,1)S(1)}, u32[]{:S(2)}, u32[]{:S(2)}) collective-permute-start(bf16[1,8,64,768]{3,2,1,0:T(8,128)(2,1)S(1)} %select_bitcast_fusion.7), channel_id=1, source_target_pairs={{0,16},{8,24},{16,0},{24,8},{1,17},{9,25},{17,1},{25,9},{2,18},{10... | collective-permute-start | bytes 2359304 | tf_op jit(solution)/shard_map/ppermute | solution.py:83
  842.1 49.4 %collective-permute-start.57 = (bf16[128,2048]{1,0:T(8,128)(2,1)}, bf16[128,2048]{1,0:T(8,128)(2,1)}, u32[]{:S(2)}, u32[]{:S(2)}) collective-permute-start(bf16[128,2048]{1,0:T(8,128)(2,1)} %get-tuple-element.165), channel_id=1, source_target_pairs={{0,2},{2,4},{4,6},{6,7},{7,5},{5,3},{3,1},{1,0},{8,10},{10,12},{12... | collective-permute-start | bytes 1572872 | tf_op jit(solution)/shard_map/ppermute | solution.py:68
  887.3 68.2 %all-to-all-start.1 = ((bf16[8,64,768]{2,1,0:T(8,128)(2,1)}), bf16[8,64,768]{2,1,0:T(8,128)(2,1)}, u32[]{:S(2)}, u32[]{:S(2)}) async-start(bf16[8,64,768]{2,1,0:T(8,128)(2,1)} %fusion.45), calls=%async_computation.1 | async-start | bytes 1572864 | tf_op jit(solution)/shard_map/all_to_all | solution.py:399
  891.6 67.7 %collective-permute-start.83 = (bf16[768,1024]{1,0:T(8,128)(2,1)}, bf16[768,1024]{1,0:T(8,128)(2,1)}, u32[]{:S(2)}, u32[]{:S(2)}) collective-permute-start(bf16[768,1024]{1,0:T(8,128)(2,1)} %add_convert_fusion.7), channel_id=1, source_target_pairs={{0,2},{2,4},{4,6},{6,7},{7,5},{5,3},{3,1},{1,0},{8,10},{10,12},{12... | collective-permute-start | bytes 4718600 | tf_op jit(solution)/shard_map/ppermute | solution.py:68
  897.5 53.7 %collective-permute-start.58 = (bf16[128,2048]{1,0:T(8,128)(2,1)S(1)}, bf16[128,2048]{1,0:T(8,128)(2,1)S(1)}, u32[]{:S(2)}, u32[]{:S(2)}) collective-permute-start(bf16[128,2048]{1,0:T(8,128)(2,1)S(1)} %get-tuple-element.163), channel_id=1, source_target_pairs={{0,2},{2,4},{4,6},{6,7},{7,5},{5,3},{3,1},{1,0},{8,10},{10,12},{12... | collective-permute-start | bytes 1572872 | tf_op jit(solution)/shard_map/ppermute | solution.py:68
  899.3 54.5 %collective-permute-start.61 = (bf16[128,2048]{1,0:T(8,128)(2,1)S(1)}, bf16[128,2048]{1,0:T(8,128)(2,1)S(1)}, u32[]{:S(2)}, u32[]{:S(2)}) collective-permute-start(bf16[128,2048]{1,0:T(8,128)(2,1)S(1)} %get-tuple-element.164), channel_id=1, source_target_pairs={{2,0},{4,2},{6,4},{7,6},{5,7},{3,5},{1,3},{0,1},{10,8},{12,10},{14... | collective-permute-start | bytes 1572872 | tf_op jit(solution)/shard_map/ppermute | solution.py:68
  (151 other events, 3002.6 us)

commit v2 on v1

v2 whole, which is shorter than its diff:
```python
import functools
import math

import jax
import jax.numpy as jnp
from jax import lax
from jax.experimental import pallas as pl
from jax.experimental.pallas import tpu as pltpu
from jax.sharding import PartitionSpec as P

HEADS = 16
HEAD_DIM = 128
epsilon = 1e-06
rope_base = 50000.0
highest = lax.Precision.HIGHEST
bf16 = jnp.bfloat16
f32 = jnp.float32

NN = (((1,), (0,)), ((), ()))
NT = (((1,), (1,)), ((), ()))
TN = (((0,), (0,)), ((), ()))


def mm(a, b, dims=NN):
    return lax.dot_general(a, b, dims, preferred_element_type=f32)


def tie(*arrays):
    return lax.optimization_barrier(arrays)


def after(x, *others):
    return lax.optimization_barrier((x, others))[0]


def ring_order(n):
    return list(range(0, n, 2)) + list(range(n - 1, 0, -2))


class Ring:
    def __init__(self, axis, groups=1):
        self.axis = axis
        total = lax.axis_size(axis)
        n = total // groups
        order = ring_order(n)
        self.down = [
            (g * n + order[i], g * n + order[(i + 1) % n]) for g in range(groups) for i in range(n)
        ]
        self.up = [(b, a) for a, b in self.down]
        place = [order.index(w % n) for w in range(total)]
        here = jnp.asarray(place, jnp.int32)[lax.axis_index(axis)]
        self.half = n // 2
        self.offsets = [0]
        for s in range(1, self.half):
            self.offsets += [-s, s]
        self.offsets.append(-self.half)
        table = jnp.asarray(order, jnp.int32)
        first = lax.axis_index(axis) // n * n
        self.owner = first + table[(here + jnp.asarray(self.offsets, jnp.int32) + n) % n]

    def hop(self, moving):
        return {
            sign: lax.ppermute(block, self.axis, self.down if sign == 1 else self.up)
            for sign, block in moving.items()
        }

    def gather(self, own, halves=False, hook=None):
        got = {0: own}
        moving = {1: own, -1: own}
        for s in range(1, self.half + 1):
            if s == self.half:
                if halves:
                    middle = own.shape[0] // 2
                    moving = {1: moving[1][:middle], -1: moving[-1][middle:]}
                else:
                    moving.pop(-1)
            if hook:
                moving = hook(s, moving)
            moving = self.hop(moving)
            for sign, block in moving.items():
                got[-s * sign] = block
        blocks = [got[o] for o in self.offsets]
        return blocks + [moving[-1]] if halves else blocks

    def begin(self, parts, halves=False):
        moving = {1: parts[2 * self.half - 1]}
        if halves:
            moving[-1] = parts[-1]
        return self.hop(moving)

    def scatter(self, parts, halves=False, hook=None):
        return self.finish(parts, self.begin(parts, halves), halves, hook)

    def finish(self, parts, moving, halves=False, hook=None):
        part = dict(zip(self.offsets, parts))
        moving = dict(moving)
        for s in range(2, self.half + 1):
            distance = self.half - s + 1
            for sign in (1, -1):
                own = part[sign * distance]
                if sign not in moving:
                    moving[sign] = own
                elif moving[sign].shape == own.shape:
                    moving[sign] = (moving[sign].astype(f32) + own.astype(f32)).astype(bf16)
                else:
                    middle = own.shape[0] // 2
                    low, high = own[:middle], own[middle:]
                    if sign == 1:
                        low = (moving[sign].astype(f32) + low.astype(f32)).astype(bf16)
                    else:
                        high = (moving[sign].astype(f32) + high.astype(f32)).astype(bf16)
                    moving[sign] = jnp.concatenate([low, high], axis=0)
            if hook:
                moving = hook(s, moving)
            moving = self.hop(moving)
        if hook:
            moving = hook(self.half + 1, moving)
        total = part[0].astype(f32)
        for block in moving.values():
            total = total + block.astype(f32)
        return total


def bits_of(size):
    return [1 << b for b in range(size.bit_length() - 1)]


def swap(x, axis, bit):
    return lax.ppermute(x, axis, [(i, i ^ bit) for i in range(lax.axis_size(axis))])


def gather_bits(x, axis, holds=()):
    index = lax.axis_index(axis)
    out = x[None]
    for k, bit in enumerate(reversed(bits_of(lax.axis_size(axis)))):
        came = swap(out, axis, bit)
        if k < len(holds):
            came = after(came, holds[k])
        high = (index & bit) != 0
        out = jnp.stack([jnp.where(high, came, out), jnp.where(high, out, came)], axis=1)
        out = out.reshape((-1,) + x.shape)
    return out


def scatter_bits(x, axis):
    index = lax.axis_index(axis)
    for bit in bits_of(lax.axis_size(axis)):
        pairs = x.reshape((-1, 2) + x.shape[1:])
        high = (index & bit) != 0
        keep = jnp.where(high, pairs[:, 1], pairs[:, 0])
        came = swap(jnp.where(high, pairs[:, 0], pairs[:, 1]), axis, bit)
        x = (keep.astype(f32) + came.astype(f32)).astype(bf16)
    return x[0]


class Sum:
    def __init__(self, x):
        self.total = x
        self.left = [
            (axis, bit) for axis in ("expert", "wshard") for bit in bits_of(lax.axis_size(axis))
        ]

    def step(self):
        if self.left:
            self.total = self.total + swap(self.total, *self.left.pop(0))
        return self.total

    def finish(self):
        while self.left:
            self.step()
        return self.total


class Group:
    def __init__(self, split):
        self.owners = lax.axis_size("expert")
        self.split = split
        self.far = lax.axis_size("wshard") // 2
        self.rel = [0]
        for bit in reversed(bits_of(self.owners)):
            self.rel += [r ^ bit for r in self.rel]

    def far_block(self, x):
        return [swap(x, "wshard", self.far)] if self.split == 2 else []

    def join(self, own, far):
        if far:
            own = [block for pair in zip(own, far) for block in pair]
        return jnp.concatenate(own, axis=0)

    def gather(self, x, hook=None):
        blocks = [x]
        for bit in reversed(bits_of(self.owners)):
            came = [swap(b, "expert", bit) for b in blocks]
            if hook:
                came = hook(came)
            blocks += came
        return blocks

    def scatter(self, x):
        for bit in bits_of(self.owners):
            half = x.shape[0] // 2
            send = x[half:].astype(bf16)
            x = x[:half] + swap(send, "expert", bit).astype(f32)
        return x

    def exchange(self, x):
        x = x.reshape((self.owners, self.split, -1) + x.shape[1:])
        own = x[:, 0]
        if self.split == 2:
            own = own + swap(x[:, 1], "wshard", self.far)
        return [
            lax.ppermute(own[k], "expert", [(i, i ^ r) for i in range(self.owners)]) if r else own[k]
            for k, r in enumerate(self.rel)
        ]


def expert_kernel(n, depth, width, sums, owner, x_ref, g_ref, m_ref, *refs):
    weights, refs = refs[:n], refs[n:]
    before, refs = refs[:sums], refs[sums:]
    (y_ref, dx_ref, mg_ref), refs = refs[:3], refs[3:]
    grads, refs = refs[:n], refs[n:]
    w_buf, d_buf, mixed_ref, gate_ref, up_ref, w_sem, d_sem, s_sem = refs
    step, steps = pl.program_id(0), pl.num_programs(0)
    slot = step % 2
    starts = [sum(w.shape[0] for w in weights[:j]) for j in range(n)]

    def columns(at):
        return pl.ds(pl.multiple_of(at * width, width), width)

    def rows_of(j):
        return pl.ds(starts[j], weights[j].shape[0])

    def get(at, j):
        return pltpu.make_async_copy(
            weights[j].at[:, columns(at)], w_buf.at[at % 2, rows_of(j)], w_sem.at[at % 2, j]
        )

    def put(at, j):
        return pltpu.make_async_copy(
            d_buf.at[at % 2, rows_of(j)], grads[j].at[:, columns(at)], d_sem.at[at % 2, j]
        )

    def resume(k):
        return pltpu.make_async_copy(before[k], (y_ref, dx_ref)[k], s_sem.at[k])

    @pl.when(step == 0)
    def _():
        for j in range(n):
            get(step, j).start()
        for k in range(sums):
            resume(k).start()
        if not sums:
            y_ref[...] = jnp.zeros_like(y_ref)
            dx_ref[...] = jnp.zeros_like(dx_ref)
        mg_ref[...] = jnp.zeros_like(mg_ref)

    @pl.when(step + 1 < steps)
    def _():
        for j in range(n):
            get(step + 1, j).start()

    for j in range(n):
        get(step, j).wait()

    @pl.when(step >= 2)
    def _():
        for j in range(n):
            put(step - 2, j).wait()

    places = []
    for j in range(w_buf.shape[1] // (3 * depth)):
        at = pl.ds(pl.multiple_of(owner[j] * depth, depth), depth)
        places.append((at, [pl.ds((3 * j + part) * depth, depth) for part in range(3)]))
    count = x_ref.shape[0]
    tile = min(count, 512)
    for start in range(0, count, tile):
        here = pl.ds(start, tile)
        gate = up = back = None
        for at, rows in places:
            x, g = x_ref[here, at], g_ref[here, at]
            a, b, c = (
                mm(x, w_buf[slot, rows[0]]),
                mm(x, w_buf[slot, rows[1]]),
                mm(g, w_buf[slot, rows[2]]),
            )
            gate, up, back = (a, b, c) if gate is None else (gate + a, up + b, back + c)
        sig = 1.0 / (1.0 + jnp.exp(-gate))
        act = gate * sig
        hidden = act * up
        mix = m_ref[here]
        mg_ref[here] += jnp.sum(hidden * back, axis=1, keepdims=True)
        mixed_ref[here] = (mix * hidden).astype(bf16)
        hidden_grad = mix * back
        gate_ref[here] = (hidden_grad * up * sig * (1.0 + gate * (1.0 - sig))).astype(bf16)
        up_ref[here] = (hidden_grad * act).astype(bf16)

    if sums:

        @pl.when(step == 0)
        def _():
            for k in range(sums):
                resume(k).wait()

    mixed, gate_grad, up_grad = mixed_ref[...], gate_ref[...], up_ref[...]
    for at, rows in places:
        x, g = x_ref[:, at], g_ref[:, at]
        y_ref[:, at] += mm(mixed, w_buf[slot, rows[2]], NT)
        dx_ref[:, at] += mm(gate_grad, w_buf[slot, rows[0]], NT) + mm(
            up_grad, w_buf[slot, rows[1]], NT
        )
        d_buf[slot, rows[0]] = mm(x, gate_grad, TN).astype(bf16)
        d_buf[slot, rows[1]] = mm(x, up_grad, TN).astype(bf16)
        d_buf[slot, rows[2]] = mm(g, mixed, TN).astype(bf16)
    for j in range(n):
        put(step, j).start()

    @pl.when(step == steps - 1)
    def _():
        for j in range(n):
            put(step - 1, j).wait()
            put(step, j).wait()


def expert_pass(owner, x, g, mix, weights, sums, width):
    n = len(weights)
    rows, model = x.shape
    deep, hidden = sum(w.shape[0] for w in weights), weights[0].shape[1]

    def full(columns):
        return pl.BlockSpec((rows, columns), lambda f, o: (0, 0), pipeline_mode=pl.Buffered(1))

    anywhere = pl.BlockSpec(memory_space=pl.ANY)
    out = pl.pallas_call(
        functools.partial(expert_kernel, n, model // owner.shape[0], width, len(sums)),
        grid_spec=pltpu.PrefetchScalarGridSpec(
            num_scalar_prefetch=1,
            grid=(hidden // width,),
            in_specs=[full(model), full(g.shape[1]), full(1)] + [anywhere] * (n + len(sums)),
            out_specs=[full(model), full(model), full(1)] + [anywhere] * n,
            scratch_shapes=[
                pltpu.VMEM((2, deep, width), bf16),
                pltpu.VMEM((2, deep, width), bf16),
                pltpu.VMEM((rows, width), bf16),
                pltpu.VMEM((rows, width), bf16),
                pltpu.VMEM((rows, width), bf16),
                pltpu.SemaphoreType.DMA((2, n)),
                pltpu.SemaphoreType.DMA((2, n)),
                pltpu.SemaphoreType.DMA((2,)),
            ],
        ),
        out_shape=[jax.ShapeDtypeStruct((rows, model), f32)] * 2
        + [jax.ShapeDtypeStruct((rows, 1), f32)]
        + [jax.ShapeDtypeStruct(w.shape, bf16) for w in weights],
        compiler_params=pltpu.CompilerParams(vmem_limit_bytes=60 << 20),
        cost_estimate=pl.CostEstimate(
            flops=18 * rows * model * hidden, transcendentals=0, bytes_accessed=4 * deep * hidden
        ),
    )(owner, x, g, mix, *weights, *sums)
    return list(out[:2]), out[2], list(out[3:])


def inverse_rms(values):
    return lax.rsqrt(jnp.mean(values * values, axis=-1, keepdims=True) + epsilon)


def norm_back(values, inverse, gain_vector, grad_rows):
    scaled = values * inverse
    weighted = grad_rows * gain_vector
    return inverse * (weighted - scaled * jnp.mean(weighted * scaled, axis=-1, keepdims=True))


def rotate(values, cosine, sine):
    return values * cosine + pltpu.roll(values, HEAD_DIM // 2, 1) * sine


def each_block(count, size, body):
    def one(k, carry):
        body(pl.ds(pl.multiple_of(k * size, size), size))
        return carry

    lax.fori_loop(0, count // size, one, 0)


def head_columns(h, part=0, heads=1):
    return pl.ds((part * heads + h) * HEAD_DIM, HEAD_DIM)


def scores_of(low_ref, seg_ref, segs_ref, here, h, heads):
    keys = low_ref[:, head_columns(h, 1, heads)]
    scores = mm(low_ref[here, head_columns(h)], keys, NT) * (1.0 / math.sqrt(HEAD_DIM))
    return jnp.where(seg_ref[here] == segs_ref[...], scores, -1e30)


def attention_kernel(n, heads, block, *refs):
    tokens, refs = refs[:n], refs[n:]
    w_ref, out_ref, gain_ref, qg_ref, kg_ref, cos_ref, sin_ref, seg_ref, segs_ref = refs[:9]
    normed_ref, inverse_ref, raw_ref, low_ref, lse_ref, mixed_ref = refs[9:15]
    parts = refs[15:]
    rows = tokens[0].shape[0]
    wide = heads * HEAD_DIM
    for b in range(n):
        here = pl.ds(b * rows, rows)
        x = tokens[b][...].astype(f32)
        inverse = inverse_rms(x)
        inverse_ref[here] = inverse
        normed_ref[here] = (x * inverse * gain_ref[...]).astype(bf16)

    def project(here):
        raw = mm(normed_ref[here], w_ref[...])
        raw_ref[here] = raw[:, : 2 * wide]
        low_ref[here, 2 * wide :] = raw[:, 2 * wide :].astype(bf16)
        for part, g_ref in ((0, qg_ref), (1, kg_ref)):
            for h in range(heads):
                at = (part * heads + h) * HEAD_DIM
                u = raw[:, at : at + HEAD_DIM]
                u = u * inverse_rms(u) * g_ref[...]
                low_ref[here, at : at + HEAD_DIM] = rotate(u, cos_ref[here], sin_ref[here]).astype(bf16)

    count = normed_ref.shape[0]
    each_block(count, block, project)

    def attend(here):
        for h in range(heads):
            scores = scores_of(low_ref, seg_ref, segs_ref, here, h, heads)
            top = jnp.max(scores, axis=-1, keepdims=True)
            lifted = jnp.exp(scores - top)
            total = jnp.sum(lifted, axis=-1, keepdims=True)
            probs = (lifted * (1.0 / total)).astype(bf16)
            lse_ref[here, h : h + 1] = top + jnp.log(total)
            mixed_ref[here, head_columns(h)] = mm(
                probs, low_ref[:, head_columns(h, 2, heads)]
            ).astype(bf16)

    each_block(count, block, attend)
    for b in range(n):
        parts[b][...] = mm(mixed_ref[pl.ds(b * rows, rows)], out_ref[...]).astype(bf16)


def attention_back_kernel(n, heads, block, *refs):
    grads, tokens, refs = refs[:n], refs[n : 2 * n], refs[2 * n :]
    w_ref, out_ref, qg_ref, kg_ref, cos_ref, sin_ref, seg_ref, segs_ref = refs[:8]
    inverse_ref, raw_ref, low_ref, lse_ref = refs[8:12]
    raw_grad_ref, gain_ref, head_gain_ref = refs[12:15]
    parts, refs = refs[15 : 15 + n], refs[15 + n :]
    mixed_ref, query_ref, key_ref, value_ref = refs
    rows = tokens[0].shape[0]
    wide = heads * HEAD_DIM
    scale = 1.0 / math.sqrt(HEAD_DIM)
    for b in range(n):
        mixed_ref[pl.ds(b * rows, rows)] = mm(grads[b][...], out_ref[...], NT).astype(bf16)
    key_ref[...] = jnp.zeros_like(key_ref)
    value_ref[...] = jnp.zeros_like(value_ref)

    def attend(here):
        for h in range(heads):
            at = head_columns(h)
            scores = scores_of(low_ref, seg_ref, segs_ref, here, h, heads)
            probs = jnp.exp(scores - lse_ref[here, h : h + 1])
            mixed_grad = mixed_ref[here, at]
            probs_grad = mm(mixed_grad, low_ref[:, head_columns(h, 2, heads)], NT)
            mean = jnp.sum(probs * probs_grad, axis=-1, keepdims=True)
            scores_grad = (probs * (probs_grad - mean)).astype(bf16)
            query_ref[here, at] = mm(scores_grad, low_ref[:, head_columns(h, 1, heads)]) * scale
            key_ref[:, at] += mm(scores_grad, low_ref[here, at], TN) * scale
            value_ref[:, at] += mm(probs.astype(bf16), mixed_grad, TN)

    count = mixed_ref.shape[0]
    each_block(count, block, attend)
    head_gain_ref[...] = jnp.zeros_like(head_gain_ref)

    def norms_back(here):
        raw_grad_ref[here, 2 * wide :] = value_ref[here].astype(bf16)
        for part, g_ref, rot_ref in ((0, qg_ref, query_ref), (1, kg_ref, key_ref)):
            for h in range(heads):
                at = (part * heads + h) * HEAD_DIM
                grad = rotate(rot_ref[here, head_columns(h)], cos_ref[here], -sin_ref[here])
                u = raw_ref[here, at : at + HEAD_DIM]
                inverse = inverse_rms(u)
                head_gain_ref[part : part + 1] += jnp.sum(
                    grad * (u * inverse), axis=0, keepdims=True
                )
                raw_grad_ref[here, at : at + HEAD_DIM] = norm_back(
                    u, inverse, g_ref[...], grad
                ).astype(bf16)

    each_block(count, block, norms_back)
    gain = None
    for b in range(n):
        here = pl.ds(b * rows, rows)
        part = mm(raw_grad_ref[here], w_ref[...], NT)
        parts[b][...] = part.astype(bf16)
        scaled = tokens[b][...].astype(f32) * inverse_ref[here]
        one = jnp.sum(part * scaled, axis=0, keepdims=True)
        gain = one if gain is None else gain + one
    gain_ref[...] = gain


def in_vmem(kernel, shapes, arrays, flops, scratch=()):
    return pl.pallas_call(
        kernel,
        in_specs=[pl.BlockSpec(memory_space=pltpu.VMEM)] * len(arrays),
        out_specs=[pl.BlockSpec(memory_space=pltpu.VMEM)] * len(shapes),
        out_shape=[jax.ShapeDtypeStruct(*shape) for shape in shapes],
        scratch_shapes=list(scratch),
        compiler_params=pltpu.CompilerParams(vmem_limit_bytes=60 << 20),
        cost_estimate=pl.CostEstimate(
            flops=flops,
            transcendentals=0,
            bytes_accessed=sum(a.size * a.dtype.itemsize for a in arrays),
        ),
    )(*arrays)


def local(
    tokens,
    segment_ids,
    routes,
    attn_gain,
    query_weight,
    key_weight,
    value_weight,
    out_weight,
    query_gain,
    key_gain,
    ffn_gain,
    router_weight,
    gate_weight,
    up_weight,
    down_weight,
    d_output,
):
    rows, model = tokens.shape
    owners, shards = lax.axis_size("expert"), lax.axis_size("wshard")
    rank = lax.axis_index("expert")
    local_experts = gate_weight.shape[0]
    experts = local_experts * owners
    heads = HEADS // shards
    wide = heads * HEAD_DIM
    ring = Ring("wshard")
    split = 2 if rows * owners <= 512 else 1
    far = shards // split
    group = Group(split)
    weight_ring = Ring("wshard", split)
    upper = lax.axis_index("wshard") >= far

    held = {}
    quarter = query_weight.shape[0] // owners
    own_rows = jnp.concatenate(
        [
            lax.dynamic_slice_in_dim(w, rank * quarter, quarter)
            .reshape(quarter, shards, wide)
            .transpose(1, 0, 2)
            for w in (query_weight, key_weight, value_weight)
        ],
        axis=2,
    )
    own_columns = lax.all_to_all(own_rows, "wshard", split_axis=0, concat_axis=0, tiled=True)
    named = jnp.sum(
        (routes[:, :, None] == jnp.arange(128, dtype=jnp.int32)).astype(bf16), axis=1
    )
    grad_rows = jnp.concatenate([d_output, named], axis=1)
    grad_far = group.far_block(grad_rows)

    def token_hook(s, moving):
        if s == 3:
            moving, held["columns"], held["grad"] = tie(moving, own_columns, grad_far)
            held["two"] = moving
        if s == ring.half:
            held["last"] = moving
        return moving

    token_blocks = ring.gather(tokens, hook=token_hook)
    qkv_weight = gather_bits(held["columns"], "expert", [held["last"]])
    qkv_weight = qkv_weight.transpose(1, 0, 2, 3).reshape(model, 3 * wide)
    grad_own = group.gather(after(grad_rows, held["two"]))
    grad_far = [b for block in held["grad"] for b in group.gather(block)]

    weights, _ = tie((gate_weight, up_weight, down_weight), held["two"])
    packed = [
        jnp.concatenate([weights[0][i], weights[1][i], weights[2][i].T], axis=0)
        for i in range(local_experts)
    ]
    half = packed[0].shape[1] // 2

    def cross(i, start):
        if split == 1:
            return packed[i][:0]
        send = jnp.where(upper, packed[i][:, :half], packed[i][:, half:])
        return swap(after(send, start), "wshard", far)

    def crossed(i, came):
        if split == 1:
            return packed[i]
        return jnp.concatenate(
            [jnp.where(upper, packed[i][:, half:], packed[i][:, :half]), came], axis=0
        )

    halves = split == 2
    block_owner = weight_ring.owner
    if split == 2:
        block_owner = jnp.stack([block_owner, block_owner ^ far], axis=1).reshape(-1)
    cross_first = cross(0, token_blocks[-1])

    sequence = rows * shards
    position = (ring.owner[:, None] * rows + jnp.arange(rows, dtype=jnp.int32)).reshape(-1)
    frequency = rope_base ** (-2.0 * jnp.arange(HEAD_DIM // 2, dtype=f32) / HEAD_DIM)
    angles = position.astype(f32)[:, None] * frequency[None, :]
    cosine, sine = jnp.cos(angles), jnp.sin(angles)
    tables = (
        jnp.concatenate([cosine, cosine], axis=1),
        jnp.concatenate([-sine, sine], axis=1),
    )
    segments = segment_ids.reshape(shards, rows)[ring.owner].reshape(-1)
    segments = (segments[:, None], segments[None, :])
    gains = (query_gain[None], key_gain[None])
    tile = 256
    normed_all, inverse_all, raw, low, log_total, mixed, *attended_part = in_vmem(
        functools.partial(attention_kernel, shards, heads, tile),
        [
            ((sequence, model), bf16),
            ((sequence, 1), f32),
            ((sequence, 2 * wide), f32),
            ((sequence, 3 * wide), bf16),
            ((sequence, heads), f32),
            ((sequence, wide), bf16),
        ]
        + [((rows, model), bf16)] * shards,
        [*token_blocks, qkv_weight, out_weight, attn_gain[None], *gains, *tables, *segments],
        2 * sequence * wide * (4 * model + 2 * sequence),
    )
    attended_part, cross_first, grad_own, grad_far = tie(
        attended_part, cross_first, grad_own, grad_far
    )
    first_block = crossed(0, cross_first)

    def attended_sum():
        part = dict(zip(ring.offsets, attended_part))
        moving = {1: part.pop(-ring.half)}
        for s in range(1, ring.half + 1):
            distance = ring.half - s + 1
            if distance < ring.half:
                for sign in (1, -1):
                    own = part[sign * distance]
                    if sign in moving:
                        own = (moving[sign].astype(f32) + own.astype(f32)).astype(bf16)
                    moving[sign] = own
            if s == 2:
                held["first"] = weight_ring.gather(after(first_block, moving), halves)
                held["second"] = cross(1, moving)
            if s == ring.half and weight_ring.half == 2:
                moving, near = tie(moving, held["first"][1:3])
                held["first"][1:3] = near
            moving = ring.hop(moving)
        total = part[0].astype(f32)
        for block in moving.values():
            total = total + block.astype(f32)
        return total

    attended = attended_sum()
    attended, cross_second = tie(attended, held["second"])

    stream = tokens.astype(f32)
    middle = stream + attended
    ffn_inverse = inverse_rms(middle)
    ffn_low = (middle * ffn_inverse * ffn_gain).astype(bf16)

    ffn_far = group.far_block(ffn_low)
    ffn_own = group.gather(ffn_low)
    second_block = crossed(1, after(cross_second, ffn_far or ffn_low))
    second_weights = weight_ring.gather(second_block, halves)
    ffn_far = [b for block in ffn_far for b in group.gather(block)]
    ffn_all = group.join(ffn_own, ffn_far)
    grad_and_names = group.join(grad_own, grad_far)
    first_weights = held["first"]
    near = 2 * weight_ring.half - 1
    ffn_all, first_weights, second_weights[:near] = tie(
        ffn_all, first_weights, second_weights[:near]
    )
    logits = mm(ffn_all, router_weight)
    logits = jnp.where(grad_and_names[:, model : model + experts] > 0, logits, -jnp.inf)
    lifted = jnp.exp(logits - jnp.max(logits, axis=1, keepdims=True))
    mixing = lifted / jnp.sum(lifted, axis=1, keepdims=True)
    which = jnp.arange(experts, dtype=jnp.int32)[None, :]
    mixes = [
        jnp.sum(jnp.where(which == rank * local_experts + i, mixing, 0.0), axis=1, keepdims=True)
        for i in range(local_experts)
    ]
    width = 256 if split == 2 else 128
    first_out = expert_pass(
        block_owner, ffn_all, grad_and_names, mixes[0], first_weights, [], width
    )
    first_out, second_weights[near:] = tie(first_out, second_weights[near:])
    sums, first_mixing, first_parts = first_out
    second_out = expert_pass(
        block_owner, ffn_all, grad_and_names, mixes[1], second_weights, sums, width
    )

    def first_hook(s, moving):
        if s == 2:
            held["h1"] = moving
        if s == weight_ring.half + 1:
            held["h2"] = moving
        return moving

    first_moving = weight_ring.begin(first_parts, halves)
    second_out, first_moving = tie(second_out, first_moving)
    (produced, row_grads), second_mixing, second_parts = second_out
    mixing_grads = [first_mixing, second_mixing]
    first_sum = weight_ring.finish(first_parts, first_moving, halves, hook=first_hook)
    came = group.exchange(jnp.concatenate(mixing_grads, axis=1))

    def far_sum(x, *hold):
        if split == 1:
            return x
        count = x.shape[0] // 2
        return x[:count] + swap(after(x[count:].astype(bf16), hold), "wshard", far).astype(f32)

    ffn_grad = far_sum(group.scatter(row_grads), held["h2"], came)
    mixing_own = mixing[:rows]
    mixing_grad = jnp.zeros_like(mixing_own)
    for r, block in zip(group.rel, came):
        for i in range(local_experts):
            at = which == (rank ^ r) * local_experts + i
            mixing_grad = jnp.where(at, block[:, i : i + 1], mixing_grad)

    logits_grad = mixing_own * (
        mixing_grad - jnp.sum(mixing_own * mixing_grad, axis=1, keepdims=True)
    )
    router_grad = lax.dot_general(
        logits_grad, ffn_low.astype(f32), TN, precision=highest, preferred_element_type=f32
    )
    ffn_grad = ffn_grad + lax.dot_general(
        logits_grad, router_weight.astype(f32), NT, precision=highest, preferred_element_type=f32
    )
    ffn_gain_grad = jnp.sum(ffn_grad * (middle * ffn_inverse), axis=0)
    middle_grad = d_output.astype(f32) + norm_back(middle, ffn_inverse, ffn_gain, ffn_grad)
    attended_low = middle_grad.astype(bf16)

    attended_blocks = ring.gather(attended_low)
    attended_all = attended_blocks[-1]
    produced = group.scatter(after(produced, attended_low))
    second_parts, first_sum, produced = after((second_parts, first_sum, produced), attended_all)

    def uncross(total):
        if split == 1:
            return total[:0]
        return swap(total[3 * depth :].astype(bf16), "wshard", far)

    def uncrossed(total, other):
        if split == 1:
            return total
        own, other = total[: 3 * depth], other.astype(f32)
        return jnp.concatenate(
            [jnp.where(upper, other, own), jnp.where(upper, own, other)], axis=1
        )

    depth = gate_weight.shape[1]
    first_home = uncross(first_sum)
    expert_part = produced[rows:] if split == 2 else produced[:0]
    expert_far = group.far_block(expert_part.astype(bf16))
    second_moving = weight_ring.begin(second_parts, halves)
    raw_grad, attn_gain_grad, head_gain_grad, *normed_part = in_vmem(
        functools.partial(attention_back_kernel, shards, heads, tile),
        [((sequence, 3 * wide), bf16), ((1, model), f32), ((2, HEAD_DIM), f32)]
        + [((rows, model), bf16)] * shards,
        [*attended_blocks, *token_blocks, qkv_weight, out_weight, *gains, *tables, *segments]
        + [inverse_all, raw, low, log_total],
        2 * sequence * wide * (4 * model + 5 * sequence),
        [pltpu.VMEM((sequence, wide), dtype) for dtype in (bf16, f32, f32, f32)],
    )
    normed_part, raw_grad, second_moving, first_home = tie(
        normed_part, raw_grad, second_moving, first_home
    )
    query_gain_grad, key_gain_grad = head_gain_grad[0], head_gain_grad[1]
    router_size = experts * model
    squares = jnp.stack([jnp.sum(middle * middle), jnp.sum(attended * attended)])
    small = Sum(
        jnp.concatenate(
            [
                router_grad.reshape(-1),
                ffn_gain_grad,
                attn_gain_grad[0],
                query_gain_grad,
                key_gain_grad,
                jnp.pad(squares, (0, 126)),
            ]
        ).reshape(-1, 128)
    )

    def normed_hook(s, moving):
        if 1 < s <= ring.half:
            moving, small.total = tie(moving, small.step())
        held["n%d" % s] = moving
        return moving

    normed_grad = ring.scatter(normed_part, hook=normed_hook)
    tokens_grad = (
        middle_grad + norm_back(stream, inverse_all[:rows], attn_gain, normed_grad)
    ).astype(bf16)

    qkv_grad = mm(normed_all, raw_grad, TN).astype(bf16)
    qkv_grad = qkv_grad.reshape(shards, owners, quarter, 3 * wide).transpose(1, 0, 2, 3)
    qkv_grad = scatter_bits(qkv_grad, "expert")
    qkv_grad = lax.all_to_all(qkv_grad, "wshard", split_axis=0, concat_axis=0, tiled=True)
    qkv_grad = gather_bits(qkv_grad, "expert")
    query_weight_grad, key_weight_grad, value_weight_grad = [
        qkv_grad[..., i * wide : (i + 1) * wide]
        .transpose(0, 2, 1, 3)
        .reshape(owners * quarter, model)
        .astype(f32)
        for i in range(3)
    ]
    out_grad = mm(mixed, after(jnp.concatenate(attended_blocks, axis=0), held["n2"]), TN)
    out_grad = out_grad.astype(bf16).reshape(owners, -1, model)
    out_grad = gather_bits(scatter_bits(out_grad, "expert"), "expert")
    out_grad = out_grad.reshape(-1, model).astype(f32)

    def second_hook(s, moving):
        if s == 2:
            moving = after(moving, held["n%d" % ring.half])
        return moving

    second_sum = weight_ring.finish(second_parts, second_moving, halves, hook=second_hook)
    expert_far = after(expert_far, normed_grad)
    summed = [uncrossed(first_sum, first_home), uncrossed(second_sum, uncross(second_sum))]
    expert_out = produced[:rows]
    for block in expert_far:
        expert_out = expert_out + block.astype(f32)
    final_stream = middle + expert_out
    output = final_stream.astype(bf16)
    gate_weight_grad = jnp.stack([s[:depth] for s in summed])
    up_weight_grad = jnp.stack([s[depth : 2 * depth] for s in summed])
    down_weight_grad = jnp.stack([s[2 * depth :].T for s in summed])

    total = small.finish().reshape(-1)
    squares = Sum(
        jnp.pad(
            jnp.stack([jnp.sum(final_stream * final_stream), jnp.sum(expert_out * expert_out)]),
            (0, 126),
        ).reshape(1, 128)
    ).finish()[0]
    sizes = [router_size, model, model, HEAD_DIM, HEAD_DIM, 2]
    starts = [sum(sizes[:k]) for k in range(len(sizes))]
    router_sum, ffn_gain_grad, attn_gain_grad, query_gain_grad, key_gain_grad, near_squares = [
        total[a : a + b] for a, b in zip(starts, sizes)
    ]
    router_weight_grad = router_sum.reshape(experts, model).T
    squares = jnp.stack([near_squares[0], squares[0], near_squares[1], squares[1]])
    stream_rms = jnp.sqrt(squares / (rows * owners * shards * model))
    return (
        output,
        tokens_grad,
        attn_gain_grad,
        query_weight_grad,
        key_weight_grad,
        value_weight_grad,
        out_grad,
        query_gain_grad,
        key_gain_grad,
        ffn_gain_grad,
        router_weight_grad,
        gate_weight_grad,
        up_weight_grad,
        down_weight_grad,
        stream_rms,
    )


def solution(mesh):
    rows = P(("expert", "wshard"), None)
    shard = P("wshard", None)
    wide = P("expert", "wshard", None)
    tall = P("expert", None, "wshard")
    return jax.shard_map(
        local,
        mesh=mesh,
        in_specs=(rows, P("expert"), rows, P(), shard, shard, shard, shard)
        + (P(), P(), P(), P(), wide, wide, tall, rows),
        out_specs=(rows, rows, P(), shard, shard, shard, shard)
        + (P(), P(), P(), P(), wide, wide, tall, P()),
        check_vma=False,
    )
```

time: 1050 us -> 843 us (0.80)
  waiting for transfers between devices: 641 us -> 434 us
  Pallas kernels: 70.2 us -> 133 us
  matrix products: 42.9 us -> 10.4 us
  local copies, waits for them, and re-layouts: 90.6 us -> 61.8 us
  other arithmetic: 91.9 us -> 67 us
  starting transfers between devices: 105 us -> 128 us
    ppermute x59 -> x47, waiting for transfers between devices: 493 us -> 204 us  [the longest x44 181 us: hop(): lax.ppermute(block, self.axis, self.down if sign == 1 else self.up)]
    ppermute x35 -> x45, waiting for transfers between devices: 139 us -> 209 us  [swap(): lax.ppermute(x, axis, [(i, i ^ bit) for i in range(lax.axis_size(axis))])]
    pallas_call x2 -> x4, Pallas kernels: 70.2 us -> 133 us  [the longest x2 82.9 us: expert_pass(): pl.pallas_call(functools.partial(expert_kernel, n, model // owner.shape[0...]
    convert_element_type x22 -> x15, other arithmetic: 33.9 us -> 4.33 us  [the longest x2 1.79 us: finish(): high = (moving[sign].astype(f32) + high.astype(f32)).astype(bf16)]
    all_to_all x1, waiting for transfers between devices: 0.01 us -> 20.5 us  [local(): lax.all_to_all(qkv_grad, 'wshard', split_axis=0, concat_axis=0, tiled=True)]
    ppermute x35 -> x45, starting transfers between devices: 25.4 us -> 41.4 us  [swap(): lax.ppermute(x, axis, [(i, i ^ bit) for i in range(lax.axis_size(axis))])]
    dot_general x7 -> x3, matrix products: 20.5 us -> 6.4 us  [mm(): return lax.dot_general(a, b, dims, preferred_element_type=f32)]
    slice x18 -> x22, local copies, waits for them, and re-layouts: 27.3 us -> 13.6 us  [the longest x4 5.95 us: scatter(): send = x[half:].astype(bf16)]
  transfers between devices with their start and end apart: 96 -> 94, of which waited for: 43 -> 44; matrix products, arithmetic and copies ran while one was open for 16% -> 12% of each run, Pallas kernels for 3% -> 16%
where the time goes in v2:
time: 843 us; the launch traced here: 837 us
  waiting for transfers between devices  434 us (51%)
  Pallas kernels  133 us (16%)
  starting transfers between devices  128 us (15%)
  other arithmetic  67 us (8%)
  local copies, waits for them, and re-layouts  61.8 us (7%)
  matrix products  10.4 us (1%)
    ppermute x45, waiting for transfers between devices, swap(): lax.ppermute(x, axis, [(i, i ^ bit) for i in range(lax.axis_size(axis))])  209 us
    ppermute x44, waiting for transfers between devices, hop(): lax.ppermute(block, self.axis, self.down if sign == 1 else self.up)  181 us
    pallas_call x2, Pallas kernels, expert_pass(): pl.pallas_call(functools.partial(expert_kernel, n, model // owner.shape[0...  82.9 us
    ppermute x44, starting transfers between devices, hop(): lax.ppermute(block, self.axis, self.down if sign == 1 else self.up)  73.2 us
    pallas_call x2, Pallas kernels, in_vmem(): pl.pallas_call(kernel, in_specs=[pl.BlockSpec(memory_space=pltpu.VMEM)] *...  49.7 us
    ppermute x45, starting transfers between devices, swap(): lax.ppermute(x, axis, [(i, i ^ bit) for i in range(lax.axis_size(axis))])  41.4 us
    unnamed x213, local copies, waits for them, and re-layouts  25.9 us
    ppermute x3, waiting for transfers between devices, exchange(): lax.ppermute(own[k], 'expert', [(i, i ^ r) for i in range(self.owners)])  23.2 us
  transfers between devices with their start and end apart: 94, of which 44 were waited for; matrix products, arithmetic and copies ran while one was open for 12% of the time, Pallas kernels for 16%

profile of v2, /device:TPU:0, one launch (start us, length us, event | category | flops | bytes accessed | tf_op | source)
XLA Modules:
  0.0 836.7 jit_solution(10305771596642232021)
XLA Ops:
  6.2 6.4 all-to-all-start
  21.9 38.8 %collective-permute-done.4 = bf16[128,2176]{1,0:T(8,128)(2,1)} collective-permute-done((bf16[128,2176]{1,0:T(8,128)(2,1)S(1)}, bf16[128,2176]{1,0:T(8,128)(2,1)}, u32[]{:S(2)}, u32[]{:S(2)}) %collective-permute-start.4) | collective-permute-done | bytes 557088 | tf_op jit(solution)/shard_map/ppermute | solution.py:129
  62.2 10.3 %collective-permute-start.5 = (bf16[128,2048]{1,0:T(8,128)(2,1)}, bf16[128,2048]{1,0:T(8,128)(2,1)}, u32[]{:S(2)}, u32[]{:S(2)}) collective-permute-start(bf16[128,2048]{1,0:T(8,128)(2,1)} %collective-permute-done.2.refs_3_.refs_11_), channel_id=1, source_target_pairs={{0,2},{2,4},{4,6},{6,7},{7,5},{5,3},{3,1},{1,0},{8,10},{10,12},{12... | collective-permute-start | bytes 1572872 | tf_op jit(solution)/shard_map/ppermute | solution.py:63
  86.0 9.2 %collective-permute-start.7 = (bf16[128,2048]{1,0:T(8,128)(2,1)}, bf16[128,2048]{1,0:T(8,128)(2,1)S(1)}, u32[]{:S(2)}, u32[]{:S(2)}) collective-permute-start(bf16[128,2048]{1,0:T(8,128)(2,1)} %collective-permute-done.5.refs_5_.refs_13_), channel_id=1, source_target_pairs={{0,2},{2,4},{4,6},{6,7},{7,5},{5,3},{3,1},{1,0},{8,10},{10,12},{12... | collective-permute-start | bytes 1572872 | tf_op jit(solution)/shard_map/ppermute | solution.py:63
  97.2 9.0 %collective-permute-done.7.refs_7_.refs_15_ = bf16[128,2048]{1,0:T(8,128)(2,1)S(1)} collective-permute-done((bf16[128,2048]{1,0:T(8,128)(2,1)}, bf16[128,2048]{1,0:T(8,128)(2,1)S(1)}, u32[]{:S(2)}, u32[]{:S(2)}) %collective-permute-start.7) | collective-permute-done | bytes 524320 | tf_op jit(solution)/shard_map/ppermute | solution.py:63
  111.7 19.7 %shard_map.325 = (bf16[1024,2048]{1,0:T(8,128)(2,1)}, f32[1024,1]{1,0:T(8,128)}, f32[1024,512]{1,0:T(8,128)}, bf16[1024,768]{1,0:T(8,128)(2,1)}, f32[1024,2]{1,0...) custom-call(bf16[128,2048]{1,0:T(8,128)(2,1)} %refs_8_.1, ...), custom_call_target="tpu_custom_call" | custom-call | flops 5368709120 | bytes 9454592 | tf_op jit(solution)/shard_map/pallas_call | solution.py:500
  131.5 12.8 %collective-permute-done.10 = bf16[768,512]{1,0:T(8,128)(2,1)} collective-permute-done((bf16[768,512]{1,0:T(8,128)(2,1)}, bf16[768,512]{1,0:T(8,128)(2,1)}, u32[]{:S(2)}, u32[]{:S(2)}) %collective-permute-start.10) | collective-permute-done | bytes 786464 | tf_op jit(solution)/shard_map/ppermute | solution.py:129
  147.5 10.4 %collective-permute-done.19 = bf16[128,2048]{1,0:T(8,128)(2,1)S(1)} collective-permute-done((bf16[128,2048]{1,0:T(8,128)(2,1)}, bf16[128,2048]{1,0:T(8,128)(2,1)S(1)}, u32[]{:S(2)}, u32[]{:S(2)}) %collective-permute-start.19) | collective-permute-done | bytes 524320 | tf_op jit(solution)/shard_map/ppermute | solution.py:63
  163.8 9.2 %collective-permute-done.20 = bf16[128,2048]{1,0:T(8,128)(2,1)S(1)} collective-permute-done((bf16[128,2048]{1,0:T(8,128)(2,1)S(1)}, bf16[128,2048]{1,0:T(8,128)(2,1)S(1)}, u32[]{:S(2)}, u32[]{:S(2)}) %collective-permute-start.20) | collective-permute-done | bytes 524320 | tf_op jit(solution)/shard_map/ppermute | solution.py:63
  174.6 32.4 %collective-permute-done.18 = bf16[128,2048]{1,0:T(8,128)(2,1)S(1)} collective-permute-done((bf16[128,2048]{1,0:T(8,128)(2,1)S(1)}, bf16[128,2048]{1,0:T(8,128)(2,1)S(1)}, u32[]{:S(2)}, u32[]{:S(2)}) %collective-permute-start.18) | collective-permute-done | bytes 524320 | tf_op jit(solution)/shard_map/ppermute | solution.py:63
  207.1 8.5 %collective-permute-done.21 = bf16[128,2048]{1,0:T(8,128)(2,1)S(1)} collective-permute-done((bf16[128,2048]{1,0:T(8,128)(2,1)S(1)}, bf16[128,2048]{1,0:T(8,128)(2,1)S(1)}, u32[]{:S(2)}, u32[]{:S(2)}) %collective-permute-start.21) | collective-permute-done | bytes 524320 | tf_op jit(solution)/shard_map/ppermute | solution.py:63
  221.2 7.3 collective-permute-done.24
  230.5 31.1 %collective-permute-done.26 = bf16[768,512]{1,0:T(8,128)(2,1)S(1)} collective-permute-done((bf16[768,512]{1,0:T(8,128)(2,1)S(1)}, bf16[768,512]{1,0:T(8,128)(2,1)S(1)}, u32[]{:S(2)}, u32[]{:S(2)}) %collective-permute-start.26) | collective-permute-done | bytes 786464 | tf_op jit(solution)/shard_map/ppermute | solution.py:129
  266.8 19.0 %collective-permute-done.27 = bf16[128,2048]{1,0:T(8,128)(2,1)S(1)} collective-permute-done((bf16[128,2048]{1,0:T(8,128)(2,1)S(1)}, bf16[128,2048]{1,0:T(8,128)(2,1)S(1)}, u32[]{:S(2)}, u32[]{:S(2)}) %collective-permute-start.27) | collective-permute-done | bytes 524320 | tf_op jit(solution)/shard_map/ppermute | solution.py:129
  289.8 9.8 %collective-permute-done.29 = bf16[128,2048]{1,0:T(8,128)(2,1)S(1)} collective-permute-done((bf16[128,2048]{1,0:T(8,128)(2,1)S(1)}, bf16[128,2048]{1,0:T(8,128)(2,1)S(1)}, u32[]{:S(2)}, u32[]{:S(2)}) %collective-permute-start.29) | collective-permute-done | bytes 524320 | tf_op jit(solution)/shard_map/ppermute | solution.py:129
  303.9 37.5 %collective-permute-done.34.refs_3_ = bf16[768,512]{1,0:T(8,128)(2,1)S(1)} collective-permute-done((bf16[768,512]{1,0:T(8,128)(2,1)S(1)}, bf16[768,512]{1,0:T(8,128)(2,1)S(1)}, u32[]{:S(2)}, u32[]{:S(2)}) %collective-permute-start.34) | collective-permute-done | bytes 786464 | tf_op jit(solution)/shard_map/ppermute | solution.py:63
  352.0 39.9 %shard_map.326 = (f32[1024,2048]{1,0:T(8,128)}, f32[1024,2048]{1,0:T(8,128)}, f32[1024,1]{1,0:T(8,128)}, bf16[1536,512]{1,0:T(8,128)(2,1)}, bf16[1536,512]{1,0:T...) custom-call(s32[8]{0:T(128)} %reshape.351.owner, ...), custom_call_target="tpu_custom_call" | custom-call | flops 19327352832 | bytes 12582912 | tf_op jit(solution)/shard_map/pallas_call | solution.py:334
  394.9 43.0 %shard_map.327 = (f32[1024,2048]{1,0:T(8,128)}, f32[1024,2048]{1,0:T(8,128)}, f32[1024,1]{1,0:T(8,128)}, bf16[1536,512]{1,0:T(8,128)(2,1)}, bf16[1536,512]{1,0:T...) custom-call(s32[8]{0:T(128)} %reshape.351.owner, ...), custom_call_target="tpu_custom_call" | custom-call | flops 19327352832 | bytes 12582912 | tf_op jit(solution)/shard_map/pallas_call | solution.py:334
  458.9 20.7 %collective-permute-done.49 = f32[128,2]{0,1:T(2,128)S(1)} collective-permute-done((f32[128,2]{0,1:T(2,128)S(1)}, f32[128,2]{0,1:T(2,128)S(1)}, u32[]{:S(2)}, u32[]{:S(2)}) %collective-permute-start.49) | collective-permute-done | bytes 1056 | tf_op jit(solution)/shard_map/ppermute | solution.py:213
  486.5 5.5 collective-permute-done.43
  494.8 22.2 %collective-permute-done.50 = bf16[128,2048]{1,0:T(8,128)(2,1)S(1)} collective-permute-done((bf16[128,2048]{1,0:T(8,128)(2,1)S(1)}, bf16[128,2048]{1,0:T(8,128)(2,1)S(1)}, u32[]{:S(2)}, u32[]{:S(2)}) %collective-permute-start.50) | collective-permute-done | bytes 524320 | tf_op jit(solution)/shard_map/ppermute | solution.py:129
  525.0 8.0 collective-permute-done.53.refs_1_
  539.3 5.7 collective-permute-done.54.refs_3_
  545.5 5.4 collective-permute-done.59.refs_4_
  568.2 30.0 %shard_map.328 = (bf16[1024,768]{1,0:T(8,128)(2,1)}, f32[1,2048]{1,0:T(1,128)}, f32[2,128]{1,0:T(2,128)}, bf16[128,2048]{1,0:T(8,128)(2,1)}, bf16[128,2048]{1,0:...) custom-call(bf16[128,2048]{1,0:T(8,128)(2,1)} %copy-done.57, ...), custom_call_target="tpu_custom_call" | custom-call | flops 6979321856 | bytes 17323008 | tf_op jit(solution)/shard_map/pallas_call | solution.py:500
  610.6 37.0 %collective-permute-done.63 = bf16[768,512]{1,0:T(8,128)(2,1)S(1)} collective-permute-done((bf16[768,512]{1,0:T(8,128)(2,1)S(1)}, bf16[768,512]{1,0:T(8,128)(2,1)S(1)}, u32[]{:S(2)}, u32[]{:S(2)}) %collective-permute-start.63) | collective-permute-done | bytes 786464 | tf_op jit(solution)/shard_map/ppermute | solution.py:129
  662.8 12.3 %collective-permute-start.67 = (bf16[128,2048]{1,0:T(8,128)(2,1)S(1)}, bf16[128,2048]{1,0:T(8,128)(2,1)S(1)}, u32[]{:S(2)}, u32[]{:S(2)}) collective-permute-start(bf16[128,2048]{1,0:T(8,128)(2,1)S(1)} %add_convert_fusion.8), channel_id=1, source_target_pairs={{0,2},{2,4},{4,6},{6,7},{7,5},{5,3},{3,1},{1,0},{8,10},{10,12},{12... | collective-permute-start | bytes 1572872 | tf_op jit(solution)/shard_map/ppermute | solution.py:63
  676.4 10.2 %collective-permute-done.67 = bf16[128,2048]{1,0:T(8,128)(2,1)S(1)} collective-permute-done((bf16[128,2048]{1,0:T(8,128)(2,1)S(1)}, bf16[128,2048]{1,0:T(8,128)(2,1)S(1)}, u32[]{:S(2)}, u32[]{:S(2)}) %collective-permute-start.67) | collective-permute-done | bytes 524320 | tf_op jit(solution)/shard_map/ppermute | solution.py:63
  697.0 7.9 collective-permute-done.70
  712.8 8.3 collective-permute-done.74
  752.5 20.5 %all-to-all-done.1 = bf16[8,64,768]{2,1,0:T(8,128)(2,1)} async-done(((bf16[8,64,768]{2,1,0:T(8,128)(2,1)}), bf16[8,64,768]{2,1,0:T(8,128)(2,1)}, u32[]{:S(2)}, u32[]{:S(2)}) %all-to-all-start.1) | async-done | bytes 786464 | tf_op jit(solution)/shard_map/all_to_all | solution.py:805
  792.4 18.0 %collective-permute-done.91 = f32[1,128]{1,0:T(1,128)S(1)} collective-permute-done((f32[1,128]{1,0:T(1,128)S(1)}, f32[1,128]{1,0:T(1,128)S(1)}, u32[]{:S(2)}, u32[]{:S(2)}) %collective-permute-start.91) | collective-permute-done | bytes 544 | tf_op jit(solution)/shard_map/ppermute | solution.py:129
  (542 shorter events, 267.5 us)
Async XLA Ops:
  6.2 54.4 %all-to-all-start = ((bf16[8,64,768]{2,1,0:T(8,128)(2,1)}), bf16[8,64,768]{2,1,0:T(8,128)(2,1)S(1)}, u32[]{:S(2)}, u32[]{:S(2)}) async-start(bf16[8,64,768]{2,1,0:T(8,128)(2,1)} %copy.154), calls=%async_computation | async-start | bytes 1572864 | tf_op jit(solution)/shard_map/all_to_all | solution.py:558
  12.8 47.8 %collective-permute-start.4 = (bf16[128,2176]{1,0:T(8,128)(2,1)S(1)}, bf16[128,2176]{1,0:T(8,128)(2,1)}, u32[]{:S(2)}, u32[]{:S(2)}) collective-permute-start(bf16[128,2176]{1,0:T(8,128)(2,1)S(1)} %pad_maximum_fusion.16), channel_id=1, source_target_pairs={{0,4},{1,5},{2,6},{3,7},{4,0},{5,1},{6,2},{7,3},{8,12},{9,13},{10,... | collective-permute-start | bytes 1671176 | tf_op jit(solution)/shard_map/ppermute | solution.py:129
  19.0 41.6 %collective-permute-start.2 = (bf16[128,2048]{1,0:T(8,128)(2,1)S(1)}, bf16[128,2048]{1,0:T(8,128)(2,1)}, u32[]{:S(2)}, u32[]{:S(2)}) collective-permute-start(bf16[128,2048]{1,0:T(8,128)(2,1)S(1)} %collective-permute-done.refs_1_.refs_9_), channel_id=1, source_target_pairs={{0,2},{2,4},{4,6},{6,7},{7,5},{5,3},{3,1},{1,0},{8,10},{10,12},{12... | collective-permute-start | bytes 1572872 | tf_op jit(solution)/shard_map/ppermute | solution.py:63
  20.6 40.1 %collective-permute-start.3 = (bf16[128,2048]{1,0:T(8,128)(2,1)}, bf16[128,2048]{1,0:T(8,128)(2,1)}, u32[]{:S(2)}, u32[]{:S(2)}) collective-permute-start(bf16[128,2048]{1,0:T(8,128)(2,1)} %collective-permute-done.1.refs_2_.refs_10_), channel_id=1, source_target_pairs={{2,0},{4,2},{6,4},{7,6},{5,7},{3,5},{1,3},{0,1},{10,8},{12,10},{14... | collective-permute-start | bytes 1572872 | tf_op jit(solution)/shard_map/ppermute | solution.py:63
  106.2 38.0 %collective-permute-start.10 = (bf16[768,512]{1,0:T(8,128)(2,1)}, bf16[768,512]{1,0:T(8,128)(2,1)}, u32[]{:S(2)}, u32[]{:S(2)}) collective-permute-start(bf16[768,512]{1,0:T(8,128)(2,1)} %get-tuple-element.170), channel_id=1, source_target_pairs={{0,4},{1,5},{2,6},{3,7},{4,0},{5,1},{6,2},{7,3},{8,12},{9,13},{10,... | collective-permute-start | bytes 2359304 | tf_op jit(solution)/shard_map/ppermute | solution.py:129
  159.7 56.0 %collective-permute-start.22 = (bf16[1536,512]{1,0:T(8,128)(2,1)S(1)}, bf16[1536,512]{1,0:T(8,128)(2,1)S(1)}, u32[]{:S(2)}, u32[]{:S(2)}) collective-permute-start(bf16[1536,512]{1,0:T(8,128)(2,1)S(1)} %pad_maximum_fusion.6.refs_0_), channel_id=1, source_target_pairs={{0,2},{2,3},{3,1},{1,0},{4,6},{6,7},{7,5},{5,4},{8,10},{10,11},{11... | collective-permute-start | bytes 4718600 | tf_op jit(solution)/shard_map/ppermute | solution.py:63
  160.5 55.3 %collective-permute-start.23 = (bf16[1536,512]{1,0:T(8,128)(2,1)S(1)}, bf16[1536,512]{1,0:T(8,128)(2,1)S(1)}, u32[]{:S(2)}, u32[]{:S(2)}) collective-permute-start(bf16[1536,512]{1,0:T(8,128)(2,1)S(1)} %pad_maximum_fusion.6.refs_0_), channel_id=1, source_target_pairs={{2,0},{3,2},{1,3},{0,1},{6,4},{7,6},{5,7},{4,5},{10,8},{11,10},{9,... | collective-permute-start | bytes 4718600 | tf_op jit(solution)/shard_map/ppermute | solution.py:63
  162.0 45.0 %collective-permute-start.18 = (bf16[128,2048]{1,0:T(8,128)(2,1)S(1)}, bf16[128,2048]{1,0:T(8,128)(2,1)S(1)}, u32[]{:S(2)}, u32[]{:S(2)}) collective-permute-start(bf16[128,2048]{1,0:T(8,128)(2,1)S(1)} %add_convert_fusion.13), channel_id=1, source_target_pairs={{2,0},{4,2},{6,4},{7,6},{5,7},{3,5},{1,3},{0,1},{10,8},{12,10},{14... | collective-permute-start | bytes 1572872 | tf_op jit(solution)/shard_map/ppermute | solution.py:63
  173.1 42.5 %collective-permute-start.21 = (bf16[128,2048]{1,0:T(8,128)(2,1)S(1)}, bf16[128,2048]{1,0:T(8,128)(2,1)S(1)}, u32[]{:S(2)}, u32[]{:S(2)}) collective-permute-start(bf16[128,2048]{1,0:T(8,128)(2,1)S(1)} %add_convert_fusion.10), channel_id=1, source_target_pairs={{0,2},{2,4},{4,6},{6,7},{7,5},{5,3},{3,1},{1,0},{8,10},{10,12},{12... | collective-permute-start | bytes 1572872 | tf_op jit(solution)/shard_map/ppermute | solution.py:63
  219.0 42.6 %collective-permute-start.26 = (bf16[768,512]{1,0:T(8,128)(2,1)S(1)}, bf16[768,512]{1,0:T(8,128)(2,1)S(1)}, u32[]{:S(2)}, u32[]{:S(2)}) collective-permute-start(bf16[768,512]{1,0:T(8,128)(2,1)S(1)} %copy-done.31), channel_id=1, source_target_pairs={{0,4},{1,5},{2,6},{3,7},{4,0},{5,1},{6,2},{7,3},{8,12},{9,13},{10,... | collective-permute-start | bytes 2359304 | tf_op jit(solution)/shard_map/ppermute | solution.py:129
  287.7 53.8 %collective-permute-start.36 = (bf16[1536,512]{1,0:T(8,128)(2,1)S(1)}, bf16[1536,512]{1,0:T(8,128)(2,1)S(1)}, u32[]{:S(2)}, u32[]{:S(2)}) collective-permute-start(bf16[1536,512]{1,0:T(8,128)(2,1)S(1)} %pad_maximum_fusion.8.refs_0_), channel_id=1, source_target_pairs={{0,2},{2,3},{3,1},{1,0},{4,6},{6,7},{7,5},{5,4},{8,10},{10,11},{11... | collective-permute-start | bytes 4718600 | tf_op jit(solution)/shard_map/ppermute | solution.py:63
  287.8 55.8 %collective-permute-start.37 = (bf16[1536,512]{1,0:T(8,128)(2,1)S(1)}, bf16[1536,512]{1,0:T(8,128)(2,1)}, u32[]{:S(2)}, u32[]{:S(2)}) collective-permute-start(bf16[1536,512]{1,0:T(8,128)(2,1)S(1)} %pad_maximum_fusion.8.refs_0_), channel_id=1, source_target_pairs={{2,0},{3,2},{1,3},{0,1},{6,4},{7,6},{5,7},{4,5},{10,8},{11,10},{9,... | collective-permute-start | bytes 4718600 | tf_op jit(solution)/shard_map/ppermute | solution.py:63
  299.8 41.6 %collective-permute-start.34 = (bf16[768,512]{1,0:T(8,128)(2,1)S(1)}, bf16[768,512]{1,0:T(8,128)(2,1)S(1)}, u32[]{:S(2)}, u32[]{:S(2)}) collective-permute-start(bf16[768,512]{1,0:T(8,128)(2,1)S(1)} %slice.392), channel_id=1, source_target_pairs={{0,2},{2,3},{3,1},{1,0},{4,6},{6,7},{7,5},{5,4},{8,10},{10,11},{11... | collective-permute-start | bytes 2359304 | tf_op jit(solution)/shard_map/ppermute | solution.py:63
  299.9 41.6 %collective-permute-start.35 = (bf16[768,512]{1,0:T(8,128)(2,1)S(1)}, bf16[768,512]{1,0:T(8,128)(2,1)S(1)}, u32[]{:S(2)}, u32[]{:S(2)}) collective-permute-start(bf16[768,512]{1,0:T(8,128)(2,1)S(1)} %slice.393), channel_id=1, source_target_pairs={{2,0},{3,2},{1,3},{0,1},{6,4},{7,6},{5,7},{4,5},{10,8},{11,10},{9,... | collective-permute-start | bytes 2359304 | tf_op jit(solution)/shard_map/ppermute | solution.py:63
  348.6 44.2 %collective-permute-start.38 = (bf16[768,512]{1,0:T(8,128)(2,1)S(1)}, bf16[768,512]{1,0:T(8,128)(2,1)}, u32[]{:S(2)}, u32[]{:S(2)}) collective-permute-start(bf16[768,512]{1,0:T(8,128)(2,1)S(1)} %slice.395), channel_id=1, source_target_pairs={{0,2},{2,3},{3,1},{1,0},{4,6},{6,7},{7,5},{5,4},{8,10},{10,11},{11... | collective-permute-start | bytes 2359304 | tf_op jit(solution)/shard_map/ppermute | solution.py:63
  350.3 42.6 %collective-permute-start.39 = (bf16[768,512]{1,0:T(8,128)(2,1)S(1)}, bf16[768,512]{1,0:T(8,128)(2,1)}, u32[]{:S(2)}, u32[]{:S(2)}) collective-permute-start(bf16[768,512]{1,0:T(8,128)(2,1)S(1)} %slice.396), channel_id=1, source_target_pairs={{2,0},{3,2},{1,3},{0,1},{6,4},{7,6},{5,7},{4,5},{10,8},{11,10},{9,... | collective-permute-start | bytes 2359304 | tf_op jit(solution)/shard_map/ppermute | solution.py:63
  392.9 45.1 %collective-permute-start.40 = (bf16[768,512]{1,0:T(8,128)(2,1)}, bf16[768,512]{1,0:T(8,128)(2,1)S(1)}, u32[]{:S(2)}, u32[]{:S(2)}) collective-permute-start(bf16[768,512]{1,0:T(8,128)(2,1)} %get-tuple-element.228), channel_id=1, source_target_pairs={{2,0},{3,2},{1,3},{0,1},{6,4},{7,6},{5,7},{4,5},{10,8},{11,10},{9,... | collective-permute-start | bytes 2359304 | tf_op jit(solution)/shard_map/ppermute | solution.py:63
  394.7 43.3 %collective-permute-start.41 = (bf16[768,512]{1,0:T(8,128)(2,1)}, bf16[768,512]{1,0:T(8,128)(2,1)S(1)}, u32[]{:S(2)}, u32[]{:S(2)}) collective-permute-start(bf16[768,512]{1,0:T(8,128)(2,1)} %get-tuple-element.229), channel_id=1, source_target_pairs={{0,2},{2,3},{3,1},{1,0},{4,6},{6,7},{7,5},{5,4},{8,10},{10,11},{11... | collective-permute-start | bytes 2359304 | tf_op jit(solution)/shard_map/ppermute | solution.py:63
  449.8 36.8 %collective-permute-start.42 = (bf16[1536,512]{1,0:T(8,128)(2,1)S(1)}, bf16[1536,512]{1,0:T(8,128)(2,1)S(1)}, u32[]{:S(2)}, u32[]{:S(2)}) collective-permute-start(bf16[1536,512]{1,0:T(8,128)(2,1)S(1)} %pad_maximum_fusion.9), channel_id=1, source_target_pairs={{2,0},{3,2},{1,3},{0,1},{6,4},{7,6},{5,7},{4,5},{10,8},{11,10},{9,... | collective-permute-start | bytes 4718600 | tf_op jit(solution)/shard_map/ppermute | solution.py:63
  455.7 36.3 %collective-permute-start.43 = (bf16[1536,512]{1,0:T(8,128)(2,1)S(1)}, bf16[1536,512]{1,0:T(8,128)(2,1)S(1)}, u32[]{:S(2)}, u32[]{:S(2)}) collective-permute-start(bf16[1536,512]{1,0:T(8,128)(2,1)S(1)} %pad_maximum_fusion.10), channel_id=1, source_target_pairs={{0,2},{2,3},{3,1},{1,0},{4,6},{6,7},{7,5},{5,4},{8,10},{10,11},{11... | collective-permute-start | bytes 4718600 | tf_op jit(solution)/shard_map/ppermute | solution.py:63
  561.7 38.0 %collective-permute-start.52 = (bf16[256,2048]{1,0:T(8,128)(2,1)}, bf16[256,2048]{1,0:T(8,128)(2,1)}, u32[]{:S(2)}, u32[]{:S(2)}) collective-permute-start(bf16[256,2048]{1,0:T(8,128)(2,1)} %slice.565), channel_id=1, source_target_pairs={{0,16},{8,24},{16,0},{24,8},{1,17},{9,25},{17,1},{25,9},{2,18},{10... | collective-permute-start | bytes 3145736 | tf_op jit(solution)/shard_map/ppermute | solution.py:129
  602.6 45.0 %collective-permute-start.63 = (bf16[768,512]{1,0:T(8,128)(2,1)S(1)}, bf16[768,512]{1,0:T(8,128)(2,1)S(1)}, u32[]{:S(2)}, u32[]{:S(2)}) collective-permute-start(bf16[768,512]{1,0:T(8,128)(2,1)S(1)} %slice.568), channel_id=1, source_target_pairs={{0,4},{1,5},{2,6},{3,7},{4,0},{5,1},{6,2},{7,3},{8,12},{9,13},{10,... | collective-permute-start | bytes 2359304 | tf_op jit(solution)/shard_map/ppermute | solution.py:129
  603.4 44.3 %collective-permute-start.61 = (bf16[768,512]{1,0:T(8,128)(2,1)S(1)}, bf16[768,512]{1,0:T(8,128)(2,1)S(1)}, u32[]{:S(2)}, u32[]{:S(2)}) collective-permute-start(bf16[768,512]{1,0:T(8,128)(2,1)S(1)} %copy-done.73), channel_id=1, source_target_pairs={{2,0},{3,2},{1,3},{0,1},{6,4},{7,6},{5,7},{4,5},{10,8},{11,10},{9,... | collective-permute-start | bytes 2359304 | tf_op jit(solution)/shard_map/ppermute | solution.py:63
  604.9 42.8 %collective-permute-start.62 = (bf16[768,512]{1,0:T(8,128)(2,1)S(1)}, bf16[768,512]{1,0:T(8,128)(2,1)S(1)}, u32[]{:S(2)}, u32[]{:S(2)}) collective-permute-start(bf16[768,512]{1,0:T(8,128)(2,1)S(1)} %copy-done.72), channel_id=1, source_target_pairs={{0,2},{2,3},{3,1},{1,0},{4,6},{6,7},{7,5},{5,4},{8,10},{10,11},{11... | collective-permute-start | bytes 2359304 | tf_op jit(solution)/shard_map/ppermute | solution.py:63
  608.2 122.5 %collective-permute-start.57 = (bf16[128,2048]{1,0:T(8,128)(2,1)S(1)}, bf16[128,2048]{1,0:T(8,128)(2,1)S(1)}, u32[]{:S(2)}, u32[]{:S(2)}) collective-permute-start(bf16[128,2048]{1,0:T(8,128)(2,1)S(1)} %slice.569), channel_id=1, source_target_pairs={{0,4},{1,5},{2,6},{3,7},{4,0},{5,1},{6,2},{7,3},{8,12},{9,13},{10,... | collective-permute-start | bytes 1572872 | tf_op jit(solution)/shard_map/ppermute | solution.py:129
  652.8 56.6 %collective-permute-start.76 = (bf16[2,8,64,768]{3,2,1,0:T(8,128)(2,1)S(1)}, bf16[2,8,64,768]{3,2,1,0:T(8,128)(2,1)S(1)}, u32[]{:S(2)}, u32[]{:S(2)}) collective-permute-start(bf16[2,8,64,768]{3,2,1,0:T(8,128)(2,1)S(1)} %fusion.1), channel_id=1, source_target_pairs={{0,8},{8,0},{16,24},{24,16},{1,9},{9,1},{17,25},{25,17},{2,10},{10... | collective-permute-start | bytes 4718600 | tf_op jit(solution)/shard_map/ppermute | solution.py:129
  726.7 49.5 %collective-permute-start.84 = (bf16[1536,512]{1,0:T(8,128)(2,1)}, bf16[1536,512]{1,0:T(8,128)(2,1)}, u32[]{:S(2)}, u32[]{:S(2)}) collective-permute-start(bf16[1536,512]{1,0:T(8,128)(2,1)} %pad_maximum_fusion.11), channel_id=1, source_target_pairs={{2,0},{3,2},{1,3},{0,1},{6,4},{7,6},{5,7},{4,5},{10,8},{11,10},{9,... | collective-permute-start | bytes 4718600 | tf_op jit(solution)/shard_map/ppermute | solution.py:63
  728.4 47.8 %collective-permute-start.85 = (bf16[1536,512]{1,0:T(8,128)(2,1)}, bf16[1536,512]{1,0:T(8,128)(2,1)}, u32[]{:S(2)}, u32[]{:S(2)}) collective-permute-start(bf16[1536,512]{1,0:T(8,128)(2,1)} %pad_maximum_fusion.12), channel_id=1, source_target_pairs={{0,2},{2,3},{3,1},{1,0},{4,6},{6,7},{7,5},{5,4},{8,10},{10,11},{11... | collective-permute-start | bytes 4718600 | tf_op jit(solution)/shard_map/ppermute | solution.py:63
  729.3 58.4 %collective-permute-start.83 = (bf16[2,64,2048]{2,1,0:T(8,128)(2,1)}, bf16[2,64,2048]{2,1,0:T(8,128)(2,1)}, u32[]{:S(2)}, u32[]{:S(2)}) collective-permute-start(bf16[2,64,2048]{2,1,0:T(8,128)(2,1)} %maximum_bitcast_fusion.2), channel_id=1, source_target_pairs={{0,8},{8,0},{16,24},{24,16},{1,9},{9,1},{17,25},{25,17},{2,10},{10... | collective-permute-start | bytes 1572872 | tf_op jit(solution)/shard_map/ppermute | solution.py:129
  732.7 40.3 %all-to-all-start.1 = ((bf16[8,64,768]{2,1,0:T(8,128)(2,1)}), bf16[8,64,768]{2,1,0:T(8,128)(2,1)}, u32[]{:S(2)}, u32[]{:S(2)}) async-start(bf16[8,64,768]{2,1,0:T(8,128)(2,1)} %fusion.23), calls=%async_computation.1 | async-start | bytes 1572864 | tf_op jit(solution)/shard_map/all_to_all | solution.py:805
  779.3 35.0 %collective-permute-start.86 = (bf16[768,512]{1,0:T(8,128)(2,1)S(1)}, bf16[768,512]{1,0:T(8,128)(2,1)S(1)}, u32[]{:S(2)}, u32[]{:S(2)}) collective-permute-start(bf16[768,512]{1,0:T(8,128)(2,1)S(1)} %slice.567), channel_id=1, source_target_pairs={{0,4},{1,5},{2,6},{3,7},{4,0},{5,1},{6,2},{7,3},{8,12},{9,13},{10,... | collective-permute-start | bytes 2359304 | tf_op jit(solution)/shard_map/ppermute | solution.py:129
  787.7 35.3 %collective-permute-start.79 = (bf16[2,8,64,768]{3,2,1,0:T(8,128)(2,1)}, bf16[2,8,64,768]{3,2,1,0:T(8,128)(2,1)}, u32[]{:S(2)}, u32[]{:S(2)}) collective-permute-start(bf16[2,8,64,768]{3,2,1,0:T(8,128)(2,1)} %maximum_bitcast_fusion.1), channel_id=1, source_target_pairs={{0,8},{8,0},{16,24},{24,16},{1,9},{9,1},{17,25},{25,17},{2,10},{10... | collective-permute-start | bytes 4718600 | tf_op jit(solution)/shard_map/ppermute | solution.py:129
  (152 other events, 2565.5 us)

commit v3 on v2

v3 whole, which is shorter than its diff:
```python
import functools
import math

import jax
import jax.numpy as jnp
from jax import lax
from jax.experimental import pallas as pl
from jax.experimental.pallas import tpu as pltpu
from jax.sharding import PartitionSpec as P

HEADS = 16
HEAD_DIM = 128
epsilon = 1e-06
rope_base = 50000.0
highest = lax.Precision.HIGHEST
bf16 = jnp.bfloat16
f32 = jnp.float32

NN = (((1,), (0,)), ((), ()))
NT = (((1,), (1,)), ((), ()))
TN = (((0,), (0,)), ((), ()))


def mm(a, b, dims=NN):
    return lax.dot_general(a, b, dims, preferred_element_type=f32)


def tie(*arrays):
    return lax.optimization_barrier(arrays)


def after(x, *others):
    return lax.optimization_barrier((x, others))[0]


def ring_order(n):
    return list(range(0, n, 2)) + list(range(n - 1, 0, -2))


class Ring:
    def __init__(self, axis, groups=1):
        self.axis = axis
        total = lax.axis_size(axis)
        n = total // groups
        order = ring_order(n)
        self.down = [
            (g * n + order[i], g * n + order[(i + 1) % n]) for g in range(groups) for i in range(n)
        ]
        self.up = [(b, a) for a, b in self.down]
        place = [order.index(w % n) for w in range(total)]
        here = jnp.asarray(place, jnp.int32)[lax.axis_index(axis)]
        self.half = n // 2
        self.offsets = [0]
        for s in range(1, self.half):
            self.offsets += [-s, s]
        self.offsets.append(-self.half)
        table = jnp.asarray(order, jnp.int32)
        first = lax.axis_index(axis) // n * n
        self.owner = first + table[(here + jnp.asarray(self.offsets, jnp.int32) + n) % n]

    def hop(self, moving):
        return {
            sign: lax.ppermute(block, self.axis, self.down if sign == 1 else self.up)
            for sign, block in moving.items()
        }

    def gather(self, own, halves=False, hook=None, first=None):
        got = {0: own}
        moving = {1: own, -1: own}
        for s in range(1, self.half + 1):
            if s == self.half:
                if halves:
                    middle = own.shape[0] // 2
                    moving = {1: moving[1][:middle], -1: moving[-1][middle:]}
                else:
                    moving.pop(-1)
            if hook:
                moving = hook(s, moving)
            moving = first if s == 1 and first else self.hop(moving)
            for sign, block in moving.items():
                got[-s * sign] = block
        blocks = [got[o] for o in self.offsets]
        return blocks + [moving[-1]] if halves else blocks

    def begin(self, parts, halves=False):
        moving = {1: parts[2 * self.half - 1]}
        if halves:
            moving[-1] = parts[-1]
        return self.hop(moving)

    def scatter(self, parts, halves=False, hook=None):
        return self.finish(parts, self.begin(parts, halves), halves, hook)

    def added(self, parts, moving, s):
        part = dict(zip(self.offsets, parts))
        distance = self.half - s + 1
        out = {}
        for sign in (1, -1):
            own = part[sign * distance]
            if sign not in moving:
                out[sign] = own
            elif moving[sign].shape == own.shape:
                out[sign] = (moving[sign].astype(f32) + own.astype(f32)).astype(bf16)
            else:
                middle = own.shape[0] // 2
                low, high = own[:middle], own[middle:]
                if sign == 1:
                    low = (moving[sign].astype(f32) + low.astype(f32)).astype(bf16)
                else:
                    high = (moving[sign].astype(f32) + high.astype(f32)).astype(bf16)
                out[sign] = jnp.concatenate([low, high], axis=0)
        return out

    def finish(self, parts, moving, halves=False, hook=None, first=2):
        for s in range(first, self.half + 1):
            moving = self.added(parts, moving, s)
            if hook:
                moving = hook(s, moving)
            moving = self.hop(moving)
        if hook:
            moving = hook(self.half + 1, moving)
        total = parts[0].astype(f32)
        for block in moving.values():
            total = total + block.astype(f32)
        return total


def bits_of(size):
    return [1 << b for b in range(size.bit_length() - 1)]


def swap(x, axis, bit):
    return lax.ppermute(x, axis, [(i, i ^ bit) for i in range(lax.axis_size(axis))])


def gather_bits(x, axis, holds=()):
    index = lax.axis_index(axis)
    out = x[None]
    for k, bit in enumerate(reversed(bits_of(lax.axis_size(axis)))):
        came = swap(out, axis, bit)
        if k < len(holds):
            came = after(came, holds[k])
        high = (index & bit) != 0
        out = jnp.stack([jnp.where(high, came, out), jnp.where(high, out, came)], axis=1)
        out = out.reshape((-1,) + x.shape)
    return out


class Fold:
    def __init__(self, x, axis):
        self.x, self.axis = x, axis
        self.left = bits_of(lax.axis_size(axis))

    def send(self):
        pairs = self.x.reshape((-1, 2) + self.x.shape[1:])
        bit = self.left.pop(0)
        high = (lax.axis_index(self.axis) & bit) != 0
        self.keep = jnp.where(high, pairs[:, 1], pairs[:, 0])
        return swap(jnp.where(high, pairs[:, 0], pairs[:, 1]), self.axis, bit)

    def add(self, came):
        self.x = (self.keep.astype(f32) + came.astype(f32)).astype(bf16)

    def finish(self):
        while self.left:
            self.add(self.send())
        return self.x[0]


class Sum:
    def __init__(self, x):
        self.total = x
        self.left = [
            (axis, bit)
            for axis in ("expert", "wshard")
            for bit in reversed(bits_of(lax.axis_size(axis)))
        ]

    def step(self):
        if self.left:
            self.total = self.total + swap(self.total, *self.left.pop(0))
        return self.total

    def finish(self):
        while self.left:
            self.step()
        return self.total


class Group:
    def __init__(self, split):
        self.owners = lax.axis_size("expert")
        self.split = split
        self.far = lax.axis_size("wshard") // 2
        self.rel = [0]
        for bit in reversed(bits_of(self.owners)):
            self.rel += [r ^ bit for r in self.rel]

    def far_block(self, x):
        return [swap(x, "wshard", self.far)] if self.split == 2 else []

    def join(self, own, far):
        if far:
            own = [block for pair in zip(own, far) for block in pair]
        return jnp.concatenate(own, axis=0)

    def gather(self, x, hook=None):
        blocks = [x]
        for bit in reversed(bits_of(self.owners)):
            came = [swap(b, "expert", bit) for b in blocks]
            if hook:
                came = hook(came)
            blocks += came
        return blocks

    def begin(self, send):
        return swap(send, "expert", 1)

    def scatter(self, keep, send=None, came=None):
        bits = bits_of(self.owners)
        came = self.begin(send) if came is None else came
        x = keep.astype(f32) + came.astype(f32)
        for bit in bits[1:]:
            half = x.shape[0] // 2
            size = half // self.split if bit == bits[-1] else half
            parts = []
            for start in reversed(range(0, half, size)):
                part = x[half + start : half + start + size].astype(bf16)
                parts.append(x[start : start + size] + swap(part, "expert", bit).astype(f32))
            x = parts[0] if len(parts) == 1 else parts[::-1]
        return x if isinstance(x, list) else [x]

    def exchange(self, x):
        x = x.reshape((self.owners, self.split, -1) + x.shape[1:])
        came = [
            lax.ppermute(x[k], "expert", [(i, i ^ r) for i in range(self.owners)]) if r else x[k]
            for k, r in enumerate(self.rel)
        ]
        return jnp.stack(came, axis=1)


def expert_kernel(expert, turn, n, owner, m_ref, x_hbm, g_hbm, *refs):
    weights, refs = refs[:n], refs[n:]
    mg_ref, mixing_ref, refs = refs[0], refs[1], refs[2:]
    ends, grads, refs = refs[:2], refs[2 : n + 2], refs[n + 2 :]
    x_ref, g_ref, y_ref, dx_ref, w_ref, d_ref, mixed_ref, gate_ref, up_ref = refs[:9]
    in_sem, w_sem, end_sem, d_sem = refs[9:]
    rows, model = x_ref.shape
    width = w_ref.shape[1]
    count = owner.shape[0] - 1
    depth = model // count
    tile = min(rows, 512)
    routing = m_ref.shape[0] == model
    starts = [sum(w.shape[0] for w in weights[:j]) for j in range(n)] + [w_ref.shape[0]]
    places = []
    for k in range(count):
        at = pl.ds(pl.multiple_of(owner[k] * depth, depth), depth)
        places.append((at, [pl.ds((3 * k + part) * depth, depth) for part in range(3)]))
    source = {start // (3 * depth): j for j, start in enumerate(starts[:-1])}
    final = {start // (3 * depth) - 1: j for j, start in enumerate(starts[1:])}
    copy = pltpu.make_async_copy

    def fetch(k, what):
        at = pl.ds(k * tile, tile)
        from_hbm, to = ((x_hbm, x_ref), (g_hbm, g_ref))[what]
        return copy(from_hbm.at[at], to.at[at], in_sem.at[what, k])

    def fetch_weight(j):
        here = pl.ds(starts[j], weights[j].shape[0])
        return copy(weights[j].at[:, pl.ds(turn * width, width)], w_ref.at[here], w_sem.at[j])

    def finish(k, e):
        at = places[k][0]
        return copy((y_ref, dx_ref)[e].at[:, at], ends[e].at[:, at], end_sem.at[e, k])

    def put(j):
        here = pl.ds(starts[j], weights[j].shape[0])
        return copy(d_ref.at[here], grads[j], d_sem.at[j])

    for what in range(2):
        fetch(0, what).start()
    for j in range(n):
        fetch_weight(j).start()
    for k in range(1, rows // tile):
        for what in range(2):
            fetch(k, what).start()

    for start in range(0, rows, tile):
        here = pl.ds(start, tile)
        for what in range(2):
            fetch(start // tile, what).wait()
        gate = up = back = logits = None
        for k, (at, parts) in enumerate(places):
            if start == 0 and k in source:
                fetch_weight(source[k]).wait()
            x, g = x_ref[here, at], g_ref[here, at]
            a, b, c = mm(x, w_ref[parts[0]]), mm(x, w_ref[parts[1]]), mm(g, w_ref[parts[2]])
            gate, up, back = (a, b, c) if k == 0 else (gate + a, up + b, back + c)
            if routing:
                a = mm(x, m_ref[at])
                logits = a if k == 0 else logits + a
        if routing:
            named = g_ref[here, model:].astype(f32) > 0.0
            top = jnp.max(jnp.where(named, logits, -1e30), axis=1, keepdims=True)
            lifted = jnp.where(named, jnp.exp(jnp.minimum(logits - top, 0.0)), 0.0)
            mixing = lifted * (1.0 / jnp.sum(lifted, axis=1, keepdims=True))
            mixing_ref[here] = mixing
        else:
            mixing = m_ref[here]
        lanes = lax.broadcasted_iota(jnp.int32, mixing.shape, 1)
        mine = jnp.where(lanes == owner[count] + expert, mixing, 0.0)
        mix = jnp.sum(mine, axis=1, keepdims=True)
        sig = 1.0 / (1.0 + jnp.exp(-gate))
        act = gate * sig
        hidden = act * up
        mg_ref[here] = jnp.sum(hidden * back, axis=1, keepdims=True)
        mixed_ref[here] = (mix * hidden).astype(bf16)
        hidden_grad = mix * back
        gate_ref[here] = (hidden_grad * up * sig * (1.0 + gate * (1.0 - sig))).astype(bf16)
        up_ref[here] = (hidden_grad * act).astype(bf16)
    if not routing:
        mixing_ref[...] = jnp.zeros_like(mixing_ref)

    mixed, gate_grad, up_grad = mixed_ref[...], gate_ref[...], up_ref[...]
    for k, (at, parts) in enumerate(places):
        y_ref[:, at] = mm(mixed, w_ref[parts[2]], NT).astype(bf16)
        dx = mm(gate_grad, w_ref[parts[0]], NT) + mm(up_grad, w_ref[parts[1]], NT)
        dx_ref[:, at] = dx.astype(bf16)
        for e in range(2):
            finish(k, e).start()
        x, g = x_ref[:, at], g_ref[:, at]
        d_ref[parts[0]] = mm(x, gate_grad, TN).astype(bf16)
        d_ref[parts[1]] = mm(x, up_grad, TN).astype(bf16)
        d_ref[parts[2]] = mm(g, mixed, TN).astype(bf16)
        if k in final:
            put(final[k]).start()
    for k in range(count):
        for e in range(2):
            finish(k, e).wait()
    for j in range(n):
        put(j).wait()


def expert_pass(expert, turn, turns, owner, x, g, mix, weights):
    n = len(weights)
    rows, model = x.shape
    deep, width = sum(w.shape[0] for w in weights), weights[0].shape[1] // turns
    anywhere, vmem = pl.BlockSpec(memory_space=pl.ANY), pl.BlockSpec(memory_space=pltpu.VMEM)
    count = owner.shape[0] - 1
    out = pl.pallas_call(
        functools.partial(expert_kernel, expert, turn, n),
        in_specs=[pl.BlockSpec(memory_space=pltpu.SMEM), vmem] + [anywhere] * (2 + n),
        out_specs=[vmem, vmem] + [anywhere] * (2 + n),
        scratch_shapes=[
            pltpu.VMEM((rows, model), bf16),
            pltpu.VMEM((rows, g.shape[1]), bf16),
            pltpu.VMEM((rows, model), bf16),
            pltpu.VMEM((rows, model), bf16),
            pltpu.VMEM((deep, width), bf16),
            pltpu.VMEM((deep, width), bf16),
            pltpu.VMEM((rows, width), bf16),
            pltpu.VMEM((rows, width), bf16),
            pltpu.VMEM((rows, width), bf16),
            pltpu.SemaphoreType.DMA((2, -(-rows // 512))),
            pltpu.SemaphoreType.DMA((n,)),
            pltpu.SemaphoreType.DMA((2, count)),
            pltpu.SemaphoreType.DMA((n,)),
        ],
        out_shape=[
            jax.ShapeDtypeStruct((rows, 1), f32),
            jax.ShapeDtypeStruct((rows if mix.shape[0] == model else 8, 128), f32),
        ]
        + [jax.ShapeDtypeStruct((rows, model), bf16)] * 2
        + [jax.ShapeDtypeStruct((w.shape[0], width), bf16) for w in weights],
        compiler_params=pltpu.CompilerParams(vmem_limit_bytes=60 << 20),
        cost_estimate=pl.CostEstimate(
            flops=18 * rows * model * width, transcendentals=0, bytes_accessed=4 * deep * width
        ),
    )(owner, mix, x, g, *weights)
    return list(out[2:4]), out[0], out[1], list(out[4:])


def inverse_rms(values):
    return lax.rsqrt(jnp.mean(values * values, axis=-1, keepdims=True) + epsilon)


def norm_back(values, inverse, gain_vector, grad_rows):
    scaled = values * inverse
    weighted = grad_rows * gain_vector
    return inverse * (weighted - scaled * jnp.mean(weighted * scaled, axis=-1, keepdims=True))


def rotate(values, cosine, sine):
    return values * cosine + pltpu.roll(values, HEAD_DIM // 2, 1) * sine


def each_block(count, size, body):
    def one(k, carry):
        body(pl.ds(pl.multiple_of(k * size, size), size))
        return carry

    lax.fori_loop(0, count // size, one, 0)


def row_places(refs):
    starts = [sum(ref.shape[0] for ref in refs[:b]) for b in range(len(refs))]
    return [pl.ds(start, ref.shape[0]) for start, ref in zip(starts, refs)]


def head_columns(h, part=0, heads=1):
    return pl.ds((part * heads + h) * HEAD_DIM, HEAD_DIM)


def scores_of(low_ref, seg_ref, segs_ref, here, h, heads):
    keys = low_ref[:, head_columns(h, 1, heads)]
    scores = mm(low_ref[here, head_columns(h)], keys, NT) * (1.0 / math.sqrt(HEAD_DIM))
    return jnp.where(seg_ref[here] == segs_ref[...], scores, -1e30)


def attention_kernel(n, heads, block, *refs):
    tokens, refs = refs[:n], refs[n:]
    w_ref, out_ref, gain_ref, qg_ref, kg_ref, cos_ref, sin_ref, seg_ref, segs_ref = refs[:9]
    normed_ref, inverse_ref, raw_ref, low_ref, lse_ref, mixed_ref = refs[9:15]
    parts = refs[15:]
    places = row_places(tokens)
    wide = heads * HEAD_DIM
    for b, here in enumerate(places):
        x = tokens[b][...].astype(f32)
        inverse = inverse_rms(x)
        inverse_ref[here] = inverse
        normed_ref[here] = (x * inverse * gain_ref[...]).astype(bf16)

    def project(here):
        raw = mm(normed_ref[here], w_ref[...])
        raw_ref[here] = raw[:, : 2 * wide]
        low_ref[here, 2 * wide :] = raw[:, 2 * wide :].astype(bf16)
        for part, g_ref in ((0, qg_ref), (1, kg_ref)):
            for h in range(heads):
                at = (part * heads + h) * HEAD_DIM
                u = raw[:, at : at + HEAD_DIM]
                u = u * inverse_rms(u) * g_ref[...]
                low_ref[here, at : at + HEAD_DIM] = rotate(u, cos_ref[here], sin_ref[here]).astype(bf16)

    count = normed_ref.shape[0]
    each_block(count, block, project)

    def attend(here):
        for h in range(heads):
            scores = scores_of(low_ref, seg_ref, segs_ref, here, h, heads)
            top = jnp.max(scores, axis=-1, keepdims=True)
            lifted = jnp.exp(scores - top)
            total = jnp.sum(lifted, axis=-1, keepdims=True)
            probs = (lifted * (1.0 / total)).astype(bf16)
            lse_ref[here, h : h + 1] = top + jnp.log(total)
            mixed_ref[here, head_columns(h)] = mm(
                probs, low_ref[:, head_columns(h, 2, heads)]
            ).astype(bf16)

    each_block(count, block, attend)
    for b, here in enumerate(places):
        parts[b][...] = mm(mixed_ref[here], out_ref[...]).astype(bf16)


def attention_back_kernel(n, heads, block, *refs):
    grads, tokens, refs = refs[:n], refs[n : 2 * n], refs[2 * n :]
    w_ref, out_ref, qg_ref, kg_ref, cos_ref, sin_ref, seg_ref, segs_ref = refs[:8]
    inverse_ref, raw_ref, low_ref, lse_ref = refs[8:12]
    raw_grad_ref, gain_ref, head_gain_ref = refs[12:15]
    parts, refs = refs[15 : 15 + n], refs[15 + n :]
    mixed_ref, query_ref, key_ref, value_ref = refs
    places = row_places(tokens)
    wide = heads * HEAD_DIM
    scale = 1.0 / math.sqrt(HEAD_DIM)
    for b, here in enumerate(places):
        mixed_ref[here] = mm(grads[b][...], out_ref[...], NT).astype(bf16)
    key_ref[...] = jnp.zeros_like(key_ref)
    value_ref[...] = jnp.zeros_like(value_ref)

    def attend(here):
        for h in range(heads):
            at = head_columns(h)
            scores = scores_of(low_ref, seg_ref, segs_ref, here, h, heads)
            probs = jnp.exp(scores - lse_ref[here, h : h + 1])
            mixed_grad = mixed_ref[here, at]
            probs_grad = mm(mixed_grad, low_ref[:, head_columns(h, 2, heads)], NT)
            mean = jnp.sum(probs * probs_grad, axis=-1, keepdims=True)
            scores_grad = (probs * (probs_grad - mean)).astype(bf16)
            query_ref[here, at] = mm(scores_grad, low_ref[:, head_columns(h, 1, heads)]) * scale
            key_ref[:, at] += mm(scores_grad, low_ref[here, at], TN) * scale
            value_ref[:, at] += mm(probs.astype(bf16), mixed_grad, TN)

    count = mixed_ref.shape[0]
    each_block(count, block, attend)
    head_gain_ref[...] = jnp.zeros_like(head_gain_ref)

    def norms_back(here):
        raw_grad_ref[here, 2 * wide :] = value_ref[here].astype(bf16)
        for part, g_ref, rot_ref in ((0, qg_ref, query_ref), (1, kg_ref, key_ref)):
            for h in range(heads):
                at = (part * heads + h) * HEAD_DIM
                grad = rotate(rot_ref[here, head_columns(h)], cos_ref[here], -sin_ref[here])
                u = raw_ref[here, at : at + HEAD_DIM]
                inverse = inverse_rms(u)
                head_gain_ref[part : part + 1] += jnp.sum(
                    grad * (u * inverse), axis=0, keepdims=True
                )
                raw_grad_ref[here, at : at + HEAD_DIM] = norm_back(
                    u, inverse, g_ref[...], grad
                ).astype(bf16)

    each_block(count, block, norms_back)
    gain = None
    for b, here in enumerate(places):
        part = mm(raw_grad_ref[here], w_ref[...], NT)
        parts[b][...] = part.astype(bf16)
        scaled = tokens[b][...].astype(f32) * inverse_ref[here]
        one = jnp.sum(part * scaled, axis=0, keepdims=True)
        gain = one if gain is None else gain + one
    gain_ref[...] = gain


def in_vmem(kernel, shapes, arrays, flops, scratch=()):
    return pl.pallas_call(
        kernel,
        in_specs=[pl.BlockSpec(memory_space=pltpu.VMEM)] * len(arrays),
        out_specs=[pl.BlockSpec(memory_space=pltpu.VMEM)] * len(shapes),
        out_shape=[jax.ShapeDtypeStruct(*shape) for shape in shapes],
        scratch_shapes=list(scratch),
        compiler_params=pltpu.CompilerParams(vmem_limit_bytes=60 << 20),
        cost_estimate=pl.CostEstimate(
            flops=flops,
            transcendentals=0,
            bytes_accessed=sum(a.size * a.dtype.itemsize for a in arrays),
        ),
    )(*arrays)


def local(
    tokens,
    segment_ids,
    routes,
    attn_gain,
    query_weight,
    key_weight,
    value_weight,
    out_weight,
    query_gain,
    key_gain,
    ffn_gain,
    router_weight,
    gate_weight,
    up_weight,
    down_weight,
    d_output,
):
    rows, model = tokens.shape
    owners, shards = lax.axis_size("expert"), lax.axis_size("wshard")
    rank = lax.axis_index("expert")
    local_experts = gate_weight.shape[0]
    experts = local_experts * owners
    heads = HEADS // shards
    wide = heads * HEAD_DIM
    ring = Ring("wshard")
    split = 2 if rows * owners <= 512 else 1
    far = shards // split
    group = Group(split)
    weight_ring = Ring("wshard", split)
    upper = lax.axis_index("wshard") >= far

    held = {}
    quarter = query_weight.shape[0] // owners
    own_rows = jnp.concatenate(
        [
            lax.dynamic_slice_in_dim(w, rank * quarter, quarter)
            .reshape(quarter, shards, wide)
            .transpose(1, 0, 2)
            for w in (query_weight, key_weight, value_weight)
        ],
        axis=2,
    )
    own_columns = lax.all_to_all(own_rows, "wshard", split_axis=0, concat_axis=0, tiled=True)
    named = jnp.sum(
        (routes[:, :, None] == jnp.arange(128, dtype=jnp.int32)).astype(bf16), axis=1
    )
    grad_rows = jnp.concatenate([d_output, named], axis=1)

    def token_hook(s, moving):
        if s == 3:
            moving, held["columns"] = tie(moving, own_columns)
            held["two"] = moving
        if s == ring.half:
            held["last"] = moving
        return moving

    token_blocks = ring.gather(tokens, True, token_hook)
    qkv_weight = gather_bits(held["columns"], "expert", [held["last"]])
    qkv_weight = qkv_weight.transpose(1, 0, 2, 3).reshape(model, 3 * wide)
    grad_own = group.gather(after(grad_rows, held["two"]))

    weights, _ = tie((gate_weight, up_weight, down_weight), held["two"])
    packed = [
        jnp.concatenate([weights[0][i], weights[1][i], weights[2][i].T], axis=0)
        for i in range(local_experts)
    ]
    half = packed[0].shape[1] // 2

    def cross(i, start):
        if split == 1:
            return packed[i][:0]
        send = jnp.where(upper, packed[i][:, :half], packed[i][:, half:])
        return swap(after(send, start), "wshard", far)

    def crossed(i, came):
        if split == 1:
            return packed[i]
        return jnp.concatenate(
            [jnp.where(upper, packed[i][:, half:], packed[i][:, :half]), came], axis=0
        )

    halves = split == 2
    block_owner = weight_ring.owner
    if split == 2:
        block_owner = jnp.stack([block_owner, block_owner ^ far], axis=1).reshape(-1)
    cross_first, cross_second = cross(0, token_blocks[-1]), cross(1, token_blocks[-1])

    sequence = rows * shards
    position = (ring.owner[:, None] * rows + jnp.arange(rows, dtype=jnp.int32)).reshape(-1)
    frequency = rope_base ** (-2.0 * jnp.arange(HEAD_DIM // 2, dtype=f32) / HEAD_DIM)
    angles = position.astype(f32)[:, None] * frequency[None, :]
    cosine, sine = jnp.cos(angles), jnp.sin(angles)
    tables = (
        jnp.concatenate([cosine, cosine], axis=1),
        jnp.concatenate([-sine, sine], axis=1),
    )
    segments = segment_ids.reshape(shards, rows)[ring.owner].reshape(-1)
    segments = (segments[:, None], segments[None, :])
    gains = (query_gain[None], key_gain[None])
    tile = 256
    normed_all, inverse_all, raw, low, log_total, mixed, *attended_part = in_vmem(
        functools.partial(attention_kernel, len(token_blocks), heads, tile),
        [
            ((sequence, model), bf16),
            ((sequence, 1), f32),
            ((sequence, 2 * wide), f32),
            ((sequence, 3 * wide), bf16),
            ((sequence, heads), f32),
            ((sequence, wide), bf16),
        ]
        + [(block.shape, bf16) for block in token_blocks],
        [*token_blocks, qkv_weight, out_weight, attn_gain[None], *gains, *tables, *segments],
        8 * sequence * wide * (4 * model + 2 * sequence),
    )
    attended_part, cross_first, cross_second, grad_own = tie(
        attended_part, cross_first, cross_second, grad_own
    )
    grad_far = group.far_block(after(grad_rows, attended_part[0]))
    first_block = crossed(0, cross_first)
    last_hop = weight_ring.half

    def attended_hook(s, moving):
        if s == 2:
            held["a2"] = moving
            held["send"] = after(first_block, moving)
            if last_hop == 2:
                held["near"] = weight_ring.hop({1: held["send"], -1: held["send"]})
        if s == 3:
            moving, held["grad"] = tie(moving, grad_far)
        if s == ring.half:
            moving, held["near"] = tie(moving, held.get("near"))
        return moving

    attended = ring.finish(
        attended_part, ring.begin(attended_part, True), True, hook=attended_hook
    )
    near = 2 * weight_ring.half - 1
    grad_far = [b for block in held["grad"] for b in group.gather(block)]

    stream = tokens.astype(f32)
    middle = stream + attended
    ffn_inverse = inverse_rms(middle)
    ffn_low = (middle * ffn_inverse * ffn_gain).astype(bf16)

    ffn_far = group.far_block(ffn_low)
    ffn_own = group.gather(ffn_low)
    first_weights = weight_ring.gather(held["send"], halves, first=held["near"])
    ffn_far, first_weights[near:] = tie(ffn_far, first_weights[near:])
    second_block = crossed(1, after(cross_second, ffn_far or ffn_low))

    second_near = weight_ring.hop({1: second_block, -1: second_block})
    ffn_far = [b for block in ffn_far for b in group.gather(block)]
    ffn_all = group.join(ffn_own, ffn_far)
    grad_and_names = group.join(grad_own, grad_far)
    ffn_all, first_weights = tie(ffn_all, first_weights)
    router = jnp.pad(router_weight, ((0, 0), (0, 128 - experts)))
    block_owner = jnp.concatenate([block_owner, rank[None] * local_experts])
    depth = gate_weight.shape[1]

    def uncross(total):
        if split == 1:
            return total[:0]
        return swap(total[3 * depth :].astype(bf16), "wshard", far)

    turns = 2
    call = functools.partial(expert_pass, owner=block_owner, x=ffn_all, g=grad_and_names)

    def part_call(expert, turn, mix, weights):
        return call(expert, turn, turns, mix=mix, weights=weights)

    (end00, mg00, mixing, parts00), second_near = tie(
        part_call(0, 0, router, first_weights), second_near
    )
    second_weights = weight_ring.gather(second_block, halves, first=second_near)
    m00 = weight_ring.begin(parts00, halves)
    (end01, mg01, _, parts01), second_weights, m00 = tie(
        part_call(0, 1, mixing, first_weights), second_weights, m00
    )
    m00 = weight_ring.hop(weight_ring.added(parts00, m00, 2))
    m01 = weight_ring.begin(parts01, halves)
    (end10, mg10, _, parts10), m00, m01 = tie(
        part_call(1, 0, mixing, second_weights), m00, m01
    )
    m01 = weight_ring.hop(weight_ring.added(parts01, m01, 2))
    m10 = weight_ring.begin(parts10, halves)
    sum00 = weight_ring.finish(parts00, m00, halves, first=3)
    home00 = uncross(sum00)
    (end11, mg11, _, parts11), m01, m10, home00 = tie(
        part_call(1, 1, mixing, second_weights), m01, m10, home00
    )

    def ends(which, begin):
        count = ffn_all.shape[0] // 2
        return sum(
            end[which][begin * count : (begin + 1) * count].astype(f32)
            for end in (end00, end01, end10, end11)
        )

    which = jnp.arange(experts, dtype=jnp.int32)[None, :]
    came = group.exchange(jnp.concatenate([mg00 + mg01, mg10 + mg11], axis=1))

    def far_sum(blocks, hold):
        if split == 1:
            return blocks[0]
        send = after(blocks[1].astype(bf16), hold)
        return blocks[0] + swap(send, "wshard", far).astype(f32)

    row_grads = group.scatter(ends(1, 0), ends(1, 1).astype(bf16))
    ffn_grad = far_sum(row_grads, came)
    if split == 2:
        came_far = swap(after(came[1], row_grads[-1]), "wshard", far)
        came = came[0] + after(came_far, row_grads[-1])
    else:
        came = came[0]
    mixing_own = mixing[:rows, :experts]
    mixing_grad = jnp.zeros_like(mixing_own)
    for k, r in enumerate(group.rel):
        block = came[k]
        for i in range(local_experts):
            at = which == (rank ^ r) * local_experts + i
            mixing_grad = jnp.where(at, block[:, i : i + 1], mixing_grad)

    logits_grad = mixing_own * (
        mixing_grad - jnp.sum(mixing_own * mixing_grad, axis=1, keepdims=True)
    )
    router_grad = lax.dot_general(
        logits_grad, ffn_low.astype(f32), TN, precision=highest, preferred_element_type=f32
    )
    ffn_grad = ffn_grad + lax.dot_general(
        logits_grad, router_weight.astype(f32), NT, precision=highest, preferred_element_type=f32
    )
    ffn_gain_grad = jnp.sum(ffn_grad * (middle * ffn_inverse), axis=0)
    middle_grad = d_output.astype(f32) + norm_back(middle, ffn_inverse, ffn_gain, ffn_grad)
    attended_low = middle_grad.astype(bf16)

    def uncrossed(total, other):
        if split == 1:
            return total
        own, other = total[: 3 * depth], other.astype(f32)
        return jnp.concatenate(
            [jnp.where(upper, other, own), jnp.where(upper, own, other)], axis=1
        )

    def middle_hook(s, moving):
        if s == 2:
            held["m11"] = weight_ring.begin(after(parts11, moving), halves)
        if s == 3:
            moving, held["y"] = tie(moving, held["y"])
        if s == ring.half:
            moving, held["m11"] = tie(moving, held["m11"])
        return moving

    end00, end01, end10, end11 = after((end00, end01, end10, end11), attended_low)
    held["y"] = group.scatter(ends(0, 0), ends(0, 1).astype(bf16))

    attended_blocks = ring.gather(attended_low, True, middle_hook)
    attended_blocks, produced = tie(attended_blocks, held["y"])
    expert_out = far_sum(produced, attended_blocks[-1])
    sum01 = weight_ring.finish(parts01, m01, halves, first=3)
    home01 = uncross(after(sum01, attended_blocks[-1]))
    parts10 = after(parts10, attended_blocks[-1])
    second_moving = [
        weight_ring.hop(weight_ring.added(parts10, m10, 2)),
        weight_ring.hop(weight_ring.added(parts11, held["m11"], 2)),
    ]
    raw_grad, attn_gain_grad, head_gain_grad, *normed_part = in_vmem(
        functools.partial(attention_back_kernel, len(token_blocks), heads, tile),
        [((sequence, 3 * wide), bf16), ((1, model), f32), ((2, HEAD_DIM), f32)]
        + [(block.shape, bf16) for block in token_blocks],
        [*attended_blocks, *token_blocks, qkv_weight, out_weight, *gains, *tables, *segments]
        + [inverse_all, raw, low, log_total],
        8 * sequence * wide * (4 * model + 5 * sequence),
        [pltpu.VMEM((sequence, wide), dtype) for dtype in (bf16, f32, f32, f32)],
    )
    due = (normed_part, raw_grad, attn_gain_grad, head_gain_grad)
    due, second_moving, expert_out, home01 = tie(due, second_moving, expert_out, home01)
    normed_part, raw_grad, attn_gain_grad, head_gain_grad = due
    final_stream = middle + expert_out
    output = final_stream.astype(bf16)
    query_gain_grad, key_gain_grad = head_gain_grad[0], head_gain_grad[1]
    router_size = experts * model
    squares = jnp.stack(
        [jnp.sum(v * v) for v in (middle, final_stream, attended, expert_out)]
    )
    small = Sum(
        jnp.concatenate(
            [
                router_grad.reshape(-1),
                ffn_gain_grad,
                attn_gain_grad[0],
                query_gain_grad,
                key_gain_grad,
                jnp.pad(squares, (0, 124)),
            ]
        ).reshape(-1, 128)
    )

    qkv_grad = mm(normed_all, raw_grad, TN).astype(bf16)
    qkv_grad = qkv_grad.reshape(shards, owners, quarter, 3 * wide).transpose(1, 0, 2, 3)
    fold = Fold(qkv_grad, "expert")
    held["fold"] = fold.send()

    def normed_hook(s, moving):
        if s <= ring.half:
            if s != 3:
                small.step()
            moving, small.total = tie(moving, small.step())
        if s in (2, 3) and held["fold"] is not None:
            moving, came = tie(moving, held["fold"])
            fold.add(came)
            held["fold"] = fold.send() if fold.left else None
        if s == 2:
            held["n2"] = moving
        if s == ring.half + 1:
            held["end"] = moving
        return moving

    normed_grad = ring.finish(normed_part, ring.begin(normed_part, True), True, hook=normed_hook)
    tokens_grad = (
        middle_grad + norm_back(stream, inverse_all[:rows], attn_gain, normed_grad)
    ).astype(bf16)
    if held["fold"] is not None:
        fold.add(held["fold"])
    qkv_grad = after(fold.finish(), small.total)
    qkv_grad = lax.all_to_all(qkv_grad, "wshard", split_axis=0, concat_axis=0, tiled=True)
    qkv_grad = gather_bits(qkv_grad, "expert")
    query_weight_grad, key_weight_grad, value_weight_grad = [
        qkv_grad[..., i * wide : (i + 1) * wide]
        .transpose(0, 2, 1, 3)
        .reshape(owners * quarter, model)
        .astype(f32)
        for i in range(3)
    ]
    out_grad = mm(mixed, after(jnp.concatenate(attended_blocks, axis=0), held["n2"]), TN)
    out_grad = Fold(out_grad.astype(bf16).reshape(owners, -1, model), "expert").finish()
    out_grad = gather_bits(out_grad, "expert").reshape(-1, model).astype(f32)

    second_sum = jnp.concatenate(
        [
            weight_ring.finish(parts, moving, halves, first=3)
            for parts, moving in zip((parts10, parts11), second_moving)
        ],
        axis=1,
    )
    second_home = uncross(after(second_sum, held["end"]))
    first_sum = jnp.concatenate([sum00, sum01], axis=1)
    first_home = jnp.concatenate([home00, home01], axis=1)
    summed = [uncrossed(first_sum, first_home), uncrossed(second_sum, second_home)]
    gate_weight_grad = jnp.stack([s[:depth] for s in summed])
    up_weight_grad = jnp.stack([s[depth : 2 * depth] for s in summed])
    down_weight_grad = jnp.stack([s[2 * depth :].T for s in summed])

    small_sums = small.finish().reshape(-1)
    sizes = [router_size, model, model, HEAD_DIM, HEAD_DIM, 4]
    starts = [sum(sizes[:k]) for k in range(len(sizes))]
    router_sum, ffn_gain_grad, attn_gain_grad, query_gain_grad, key_gain_grad, squares = [
        small_sums[a : a + b] for a, b in zip(starts, sizes)
    ]
    router_weight_grad = router_sum.reshape(experts, model).T
    stream_rms = jnp.sqrt(squares / (rows * owners * shards * model))
    return (
        output,
        tokens_grad,
        attn_gain_grad,
        query_weight_grad,
        key_weight_grad,
        value_weight_grad,
        out_grad,
        query_gain_grad,
        key_gain_grad,
        ffn_gain_grad,
        router_weight_grad,
        gate_weight_grad,
        up_weight_grad,
        down_weight_grad,
        stream_rms,
    )


def solution(mesh):
    rows = P(("expert", "wshard"), None)
    shard = P("wshard", None)
    wide = P("expert", "wshard", None)
    tall = P("expert", None, "wshard")
    return jax.shard_map(
        local,
        mesh=mesh,
        in_specs=(rows, P("expert"), rows, P(), shard, shard, shard, shard)
        + (P(), P(), P(), P(), wide, wide, tall, rows),
        out_specs=(rows, rows, P(), shard, shard, shard, shard)
        + (P(), P(), P(), P(), wide, wide, tall, P()),
        check_vma=False,
    )
```

time: 843 us -> 755 us (0.90)
  waiting for transfers between devices: 434 us -> 318 us
  other arithmetic: 67 us -> 94 us
    ppermute x45 -> x43, waiting for transfers between devices: 209 us -> 136 us  [swap(): lax.ppermute(x, axis, [(i, i ^ bit) for i in range(lax.axis_size(axis))])]
    ppermute x44 -> x56, waiting for transfers between devices: 181 us -> 159 us  [hop(): lax.ppermute(block, self.axis, self.down if sign == 1 else self.up)]
    convert_element_type x16 -> x26, other arithmetic: 3.7 us -> 22.6 us  [the longest x1 7.01 us: local(): row_grads = group.scatter(ends(1, 0), ends(1, 1).astype(bf16))]
    ppermute x3, waiting for transfers between devices: 23.2 us -> 11.7 us  [exchange(): lax.ppermute(x[k], 'expert', [(i, i ^ r) for i in range(self.owners)])]
    all_to_all x1, waiting for transfers between devices: 20.5 us -> 12 us  [local(): lax.all_to_all(qkv_grad, 'wshard', split_axis=0, concat_axis=0, tiled=True)]
    ppermute x44 -> x56, starting transfers between devices: 73.2 us -> 80.7 us  [hop(): lax.ppermute(block, self.axis, self.down if sign == 1 else self.up)]
    ppermute x45 -> x43, starting transfers between devices: 41.4 us -> 34.8 us  [swap(): lax.ppermute(x, axis, [(i, i ^ bit) for i in range(lax.axis_size(axis))])]
    unnamed x213 -> x261, local copies, waits for them, and re-layouts: 25.9 us -> 30.2 us
  transfers between devices with their start and end apart: 94 -> 104, of which waited for: 44 -> 48; matrix products, arithmetic and copies ran while one was open for 12% -> 15% of each run, Pallas kernels for 16% -> 17%
where the time goes in v3:
time: 755 us; the launch traced here: 748 us
  waiting for transfers between devices  318 us (42%)
  Pallas kernels  130 us (17%)
  starting transfers between devices  128 us (17%)
  other arithmetic  94 us (12%)
  local copies, waits for them, and re-layouts  65.1 us (9%)
  matrix products  8.91 us (1%)
    ppermute x56, waiting for transfers between devices, hop(): lax.ppermute(block, self.axis, self.down if sign == 1 else self.up)  159 us
    ppermute x43, waiting for transfers between devices, swap(): lax.ppermute(x, axis, [(i, i ^ bit) for i in range(lax.axis_size(axis))])  136 us
    ppermute x56, starting transfers between devices, hop(): lax.ppermute(block, self.axis, self.down if sign == 1 else self.up)  80.7 us
    pallas_call x4, Pallas kernels, expert_pass(): pl.pallas_call(functools.partial(expert_kernel, expert, turn, n), in_spec...  79.2 us
    pallas_call x2, Pallas kernels, in_vmem(): pl.pallas_call(kernel, in_specs=[pl.BlockSpec(memory_space=pltpu.VMEM)] *...  51.2 us
    ppermute x43, starting transfers between devices, swap(): lax.ppermute(x, axis, [(i, i ^ bit) for i in range(lax.axis_size(axis))])  34.8 us
    unnamed x261, local copies, waits for them, and re-layouts  30.2 us
  transfers between devices with their start and end apart: 104, of which 48 were waited for; matrix products, arithmetic and copies ran while one was open for 15% of the time, Pallas kernels for 17%

profile of v3, /device:TPU:0, one launch (start us, length us, event | category | flops | bytes accessed | tf_op | source)
XLA Modules:
  0.0 748.1 jit_solution(14707573560606978636)
XLA Ops:
  6.2 6.4 all-to-all-start
  21.9 17.2 %collective-permute-done.2.refs_3_.refs_12_ = bf16[128,2048]{1,0:T(8,128)(2,1)} collective-permute-done((bf16[128,2048]{1,0:T(8,128)(2,1)S(1)}, bf16[128,2048]{1,0:T(8,128)(2,1)}, u32[]{:S(2)}, u32[]{:S(2)}) %collective-permute-start.2) | collective-permute-done | bytes 524320 | tf_op jit(solution)/shard_map/ppermute | solution.py:63
  43.1 5.8 collective-permute-start.4
  67.9 5.7 collective-permute-start.6
  84.0 20.2 %shard_map.325 = (bf16[1024,2048]{1,0:T(8,128)(2,1)}, f32[1024,1]{1,0:T(8,128)}, f32[1024,512]{1,0:T(8,128)}, bf16[1024,768]{1,0:T(8,128)(2,1)}, f32[1024,2]{1,0...) custom-call(bf16[128,2048]{1,0:T(8,128)(2,1)} %refs_9_.1, ...), custom_call_target="tpu_custom_call" | custom-call | flops 21474836480 | bytes 9454592 | tf_op jit(solution)/shard_map/pallas_call | solution.py:523
  104.2 27.8 %collective-permute-done.10 = bf16[768,512]{1,0:T(8,128)(2,1)} collective-permute-done((bf16[768,512]{1,0:T(8,128)(2,1)}, bf16[768,512]{1,0:T(8,128)(2,1)}, u32[]{:S(2)}, u32[]{:S(2)}) %collective-permute-start.10) | collective-permute-done | bytes 786464 | tf_op jit(solution)/shard_map/ppermute | solution.py:133
  132.0 15.8 %collective-permute-done.11 = bf16[768,512]{1,0:T(8,128)(2,1)} collective-permute-done((bf16[768,512]{1,0:T(8,128)(2,1)}, bf16[768,512]{1,0:T(8,128)(2,1)}, u32[]{:S(2)}, u32[]{:S(2)}) %collective-permute-start.11) | collective-permute-done | bytes 786464 | tf_op jit(solution)/shard_map/ppermute | solution.py:133
  161.7 10.0 %collective-permute-start.22 = (bf16[1536,512]{1,0:T(8,128)(2,1)S(1)}, bf16[1536,512]{1,0:T(8,128)(2,1)S(1)}, u32[]{:S(2)}, u32[]{:S(2)}) collective-permute-start(bf16[1536,512]{1,0:T(8,128)(2,1)S(1)} %pad_maximum_fusion.9.refs_0_), channel_id=1, source_target_pairs={{2,0},{3,2},{1,3},{0,1},{6,4},{7,6},{5,7},{4,5},{10,8},{11,10},{9,... | collective-permute-start | bytes 4718600 | tf_op jit(solution)/shard_map/ppermute | solution.py:63
  178.4 13.7 %collective-permute-done.16 = bf16[128,2048]{1,0:T(8,128)(2,1)S(1)} collective-permute-done((bf16[128,2048]{1,0:T(8,128)(2,1)S(1)}, bf16[128,2048]{1,0:T(8,128)(2,1)S(1)}, u32[]{:S(2)}, u32[]{:S(2)}) %collective-permute-start.16) | collective-permute-done | bytes 524320 | tf_op jit(solution)/shard_map/ppermute | solution.py:63
  196.9 24.4 %collective-permute-done.21 = bf16[128,2048]{1,0:T(8,128)(2,1)S(1)} collective-permute-done((bf16[128,2048]{1,0:T(8,128)(2,1)S(1)}, bf16[128,2048]{1,0:T(8,128)(2,1)S(1)}, u32[]{:S(2)}, u32[]{:S(2)}) %collective-permute-start.21) | collective-permute-done | bytes 524320 | tf_op jit(solution)/shard_map/ppermute | solution.py:63
  230.4 9.3 %collective-permute-done.24 = bf16[128,2048]{1,0:T(8,128)(2,1)S(1)} collective-permute-done((bf16[128,2048]{1,0:T(8,128)(2,1)S(1)}, bf16[128,2048]{1,0:T(8,128)(2,1)S(1)}, u32[]{:S(2)}, u32[]{:S(2)}) %collective-permute-start.24) | collective-permute-done | bytes 524320 | tf_op jit(solution)/shard_map/ppermute | solution.py:63
  246.1 10.0 %collective-permute-done.27.refs_3_ = bf16[768,512]{1,0:T(8,128)(2,1)S(1)} collective-permute-done((bf16[768,512]{1,0:T(8,128)(2,1)S(1)}, bf16[768,512]{1,0:T(8,128)(2,1)S(1)}, u32[]{:S(2)}, u32[]{:S(2)}) %collective-permute-start.27) | collective-permute-done | bytes 786464 | tf_op jit(solution)/shard_map/ppermute | solution.py:63
  256.1 8.8 %collective-permute-done.28.refs_4_ = bf16[768,512]{1,0:T(8,128)(2,1)S(1)} collective-permute-done((bf16[768,512]{1,0:T(8,128)(2,1)S(1)}, bf16[768,512]{1,0:T(8,128)(2,1)S(1)}, u32[]{:S(2)}, u32[]{:S(2)}) %collective-permute-start.28) | collective-permute-done | bytes 786464 | tf_op jit(solution)/shard_map/ppermute | solution.py:63
  281.8 18.3 %shard_map.326 = (f32[1024,1]{1,0:T(8,128)}, f32[1024,128]{1,0:T(8,128)}, bf16[1024,2048]{1,0:T(8,128)(2,1)}, bf16[1024,2048]{1,0:T(8,128)(2,1)}, bf16[1536,256]...) custom-call(s32[9]{0:T(128)} %pad_add_fusion.1.owner, ...), custom_call_target="tpu_custom_call" | custom-call | flops 9663676416 | bytes 6291456 | tf_op jit(solution)/shard_map/pallas_call | solution.py:350
  312.5 20.3 %shard_map.327 = (f32[1024,1]{1,0:T(8,128)}, f32[8,128]{1,0:T(8,128)}, bf16[1024,2048]{1,0:T(8,128)(2,1)}, bf16[1024,2048]{1,0:T(8,128)(2,1)}, bf16[1536,256]{1,...) custom-call(s32[9]{0:T(128)} %pad_add_fusion.1.owner, ...), custom_call_target="tpu_custom_call" | custom-call | flops 9663676416 | bytes 6291456 | tf_op jit(solution)/shard_map/pallas_call | solution.py:350
  340.7 20.3 %shard_map.328 = (f32[1024,1]{1,0:T(8,128)}, f32[8,128]{1,0:T(8,128)}, bf16[1024,2048]{1,0:T(8,128)(2,1)}, bf16[1024,2048]{1,0:T(8,128)(2,1)}, bf16[1536,256]{1,...) custom-call(s32[9]{0:T(128)} %pad_add_fusion.1.owner, ...), custom_call_target="tpu_custom_call" | custom-call | flops 9663676416 | bytes 6291456 | tf_op jit(solution)/shard_map/pallas_call | solution.py:350
  373.2 20.3 %shard_map.329 = (f32[1024,1]{1,0:T(8,128)}, f32[8,128]{1,0:T(8,128)}, bf16[1024,2048]{1,0:T(8,128)(2,1)}, bf16[1024,2048]{1,0:T(8,128)(2,1)}, bf16[1536,256]{1,...) custom-call(s32[9]{0:T(128)} %pad_add_fusion.1.owner, ...), custom_call_target="tpu_custom_call" | custom-call | flops 9663676416 | bytes 6291456 | tf_op jit(solution)/shard_map/pallas_call | solution.py:350
  393.5 7.4 collective-permute-done.50
  400.9 7.0 add_convert_fusion.1
  412.4 6.3 fusion.49
  421.2 11.7 %collective-permute-done.56 = f32[2,128,2]{1,2,0:T(2,128)S(1)} collective-permute-done((f32[2,128,2]{1,2,0:T(2,128)S(1)}, f32[2,128,2]{1,2,0:T(2,128)S(1)}, u32[]{:S(2)}, u32[]{:S(2)}) %collective-permute-start.56) | collective-permute-done | bytes 2080 | tf_op jit(solution)/shard_map/ppermute | solution.py:236
  437.8 12.1 %collective-permute-done.60 = f32[4,128,2]{1,2,0:T(2,128)S(1)} collective-permute-done((f32[4,128,2]{1,2,0:T(2,128)S(1)}, f32[4,128,2]{1,2,0:T(2,128)S(1)}, u32[]{:S(2)}, u32[]{:S(2)}) %collective-permute-start.60) | collective-permute-done | bytes 4128 | tf_op jit(solution)/shard_map/ppermute | solution.py:133
  451.1 9.8 %collective-permute-done.59 = bf16[128,2048]{1,0:T(8,128)(2,1)S(1)} collective-permute-done((bf16[128,2048]{1,0:T(8,128)(2,1)S(1)}, bf16[128,2048]{1,0:T(8,128)(2,1)S(1)}, u32[]{:S(2)}, u32[]{:S(2)}) %collective-permute-start.59) | collective-permute-done | bytes 524320 | tf_op jit(solution)/shard_map/ppermute | solution.py:133
  491.1 9.5 %collective-permute-done.66 = bf16[128,2048]{1,0:T(8,128)(2,1)S(1)} collective-permute-done((bf16[128,2048]{1,0:T(8,128)(2,1)S(1)}, bf16[128,2048]{1,0:T(8,128)(2,1)S(1)}, u32[]{:S(2)}, u32[]{:S(2)}) %collective-permute-start.66) | collective-permute-done | bytes 524320 | tf_op jit(solution)/shard_map/ppermute | solution.py:133
  509.2 7.5 collective-permute-done.69.refs_6_
  517.3 6.1 collective-permute-done.70
  532.9 6.4 collective-permute-done.73.refs_8_
  548.1 31.0 %shard_map.330 = (bf16[1024,768]{1,0:T(8,128)(2,1)}, f32[1,2048]{1,0:T(1,128)}, f32[2,128]{1,0:T(2,128)}, bf16[128,2048]{1,0:T(8,128)(2,1)}, bf16[128,2048]{1,0:...) custom-call(bf16[128,2048]{1,0:T(8,128)(2,1)} %copy-done.32, ...), custom_call_target="tpu_custom_call" | custom-call | flops 27917287424 | bytes 17323008 | tf_op jit(solution)/shard_map/pallas_call | solution.py:523
  585.6 11.7 %collective-permute-done.79 = bf16[768,256]{1,0:T(8,128)(2,1)S(1)} collective-permute-done((bf16[768,256]{1,0:T(8,128)(2,1)S(1)}, bf16[768,256]{1,0:T(8,128)(2,1)S(1)}, u32[]{:S(2)}, u32[]{:S(2)}) %collective-permute-start.79) | collective-permute-done | bytes 393248 | tf_op jit(solution)/shard_map/ppermute | solution.py:133
  628.2 8.0 %collective-permute-done.86 = bf16[128,2048]{1,0:T(8,128)(2,1)S(1)} collective-permute-done((bf16[128,2048]{1,0:T(8,128)(2,1)S(1)}, bf16[128,2048]{1,0:T(8,128)(2,1)S(1)}, u32[]{:S(2)}, u32[]{:S(2)}) %collective-permute-start.86) | collective-permute-done | bytes 524320 | tf_op jit(solution)/shard_map/ppermute | solution.py:63
  671.7 12.0 %all-to-all-done.1 = bf16[8,64,768]{2,1,0:T(8,128)(2,1)} async-done(((bf16[8,64,768]{2,1,0:T(8,128)(2,1)}), bf16[8,64,768]{2,1,0:T(8,128)(2,1)}, u32[]{:S(2)}, u32[]{:S(2)}) %all-to-all-start.1) | async-done | bytes 786464 | tf_op jit(solution)/shard_map/all_to_all | solution.py:863
  702.2 23.1 %collective-permute-done.101 = bf16[768,512]{1,0:T(8,128)(2,1)S(1)} collective-permute-done((bf16[768,512]{1,0:T(8,128)(2,1)S(1)}, bf16[768,512]{1,0:T(8,128)(2,1)S(1)}, u32[]{:S(2)}, u32[]{:S(2)}) %collective-permute-start.101) | collective-permute-done | bytes 786464 | tf_op jit(solution)/shard_map/ppermute | solution.py:133
  (632 shorter events, 321.3 us)
Async XLA Ops:
  6.2 35.1 %all-to-all-start = ((bf16[8,64,768]{2,1,0:T(8,128)(2,1)}), bf16[8,64,768]{2,1,0:T(8,128)(2,1)S(1)}, u32[]{:S(2)}, u32[]{:S(2)}) async-start(bf16[8,64,768]{2,1,0:T(8,128)(2,1)} %copy.156), calls=%async_computation | async-start | bytes 1572864 | tf_op jit(solution)/shard_map/all_to_all | solution.py:581
  56.9 47.4 %collective-permute-start.13 = (bf16[128,2176]{1,0:T(8,128)(2,1)}, bf16[128,2176]{1,0:T(8,128)(2,1)}, u32[]{:S(2)}, u32[]{:S(2)}) collective-permute-start(bf16[128,2176]{1,0:T(8,128)(2,1)} %pad_maximum_fusion.23), channel_id=1, source_target_pairs={{0,8},{8,0},{16,24},{24,16},{1,9},{9,1},{17,25},{25,17},{2,10},{10... | collective-permute-start | bytes 1671176 | tf_op jit(solution)/shard_map/ppermute | solution.py:133
  73.5 30.7 %collective-permute-start.14 = (bf16[128,2176]{1,0:T(8,128)(2,1)}, bf16[128,2176]{1,0:T(8,128)(2,1)S(1)}, u32[]{:S(2)}, u32[]{:S(2)}) collective-permute-start(bf16[128,2176]{1,0:T(8,128)(2,1)} %collective-permute-done.12), channel_id=1, source_target_pairs={{0,8},{8,0},{16,24},{24,16},{1,9},{9,1},{17,25},{25,17},{2,10},{10... | collective-permute-start | bytes 1671176 | tf_op jit(solution)/shard_map/ppermute | solution.py:133
  77.9 54.1 %collective-permute-start.10 = (bf16[768,512]{1,0:T(8,128)(2,1)}, bf16[768,512]{1,0:T(8,128)(2,1)}, u32[]{:S(2)}, u32[]{:S(2)}) collective-permute-start(bf16[768,512]{1,0:T(8,128)(2,1)} %get-tuple-element.255), channel_id=1, source_target_pairs={{0,4},{1,5},{2,6},{3,7},{4,0},{5,1},{6,2},{7,3},{8,12},{9,13},{10,... | collective-permute-start | bytes 2359304 | tf_op jit(solution)/shard_map/ppermute | solution.py:133
  79.5 68.4 %collective-permute-start.11 = (bf16[768,512]{1,0:T(8,128)(2,1)}, bf16[768,512]{1,0:T(8,128)(2,1)}, u32[]{:S(2)}, u32[]{:S(2)}) collective-permute-start(bf16[768,512]{1,0:T(8,128)(2,1)} %get-tuple-element.256), channel_id=1, source_target_pairs={{0,4},{1,5},{2,6},{3,7},{4,0},{5,1},{6,2},{7,3},{8,12},{9,13},{10,... | collective-permute-start | bytes 2359304 | tf_op jit(solution)/shard_map/ppermute | solution.py:133
  152.0 40.1 %collective-permute-start.19 = (bf16[128,2176]{1,0:T(8,128)(2,1)}, bf16[128,2176]{1,0:T(8,128)(2,1)S(1)}, u32[]{:S(2)}, u32[]{:S(2)}) collective-permute-start(bf16[128,2176]{1,0:T(8,128)(2,1)} %pad_maximum_fusion.23), channel_id=1, source_target_pairs={{0,4},{1,5},{2,6},{3,7},{4,0},{5,1},{6,2},{7,3},{8,12},{9,13},{10,... | collective-permute-start | bytes 1671176 | tf_op jit(solution)/shard_map/ppermute | solution.py:133
  157.8 34.3 %collective-permute-start.16 = (bf16[128,2048]{1,0:T(8,128)(2,1)S(1)}, bf16[128,2048]{1,0:T(8,128)(2,1)S(1)}, u32[]{:S(2)}, u32[]{:S(2)}) collective-permute-start(bf16[128,2048]{1,0:T(8,128)(2,1)S(1)} %pad_maximum_fusion.26), channel_id=1, source_target_pairs={{2,0},{4,2},{6,4},{7,6},{5,7},{3,5},{1,3},{0,1},{10,8},{12,10},{14... | collective-permute-start | bytes 1572872 | tf_op jit(solution)/shard_map/ppermute | solution.py:63
  161.7 63.0 %collective-permute-start.22 = (bf16[1536,512]{1,0:T(8,128)(2,1)S(1)}, bf16[1536,512]{1,0:T(8,128)(2,1)S(1)}, u32[]{:S(2)}, u32[]{:S(2)}) collective-permute-start(bf16[1536,512]{1,0:T(8,128)(2,1)S(1)} %pad_maximum_fusion.9.refs_0_), channel_id=1, source_target_pairs={{2,0},{3,2},{1,3},{0,1},{6,4},{7,6},{5,7},{4,5},{10,8},{11,10},{9,... | collective-permute-start | bytes 4718600 | tf_op jit(solution)/shard_map/ppermute | solution.py:63
  171.7 53.0 %collective-permute-start.23 = (bf16[1536,512]{1,0:T(8,128)(2,1)S(1)}, bf16[1536,512]{1,0:T(8,128)(2,1)S(1)}, u32[]{:S(2)}, u32[]{:S(2)}) collective-permute-start(bf16[1536,512]{1,0:T(8,128)(2,1)S(1)} %pad_maximum_fusion.9.refs_0_), channel_id=1, source_target_pairs={{0,2},{2,3},{3,1},{1,0},{4,6},{6,7},{7,5},{5,4},{8,10},{10,11},{11... | collective-permute-start | bytes 4718600 | tf_op jit(solution)/shard_map/ppermute | solution.py:63
  192.2 29.1 %collective-permute-start.21 = (bf16[128,2048]{1,0:T(8,128)(2,1)S(1)}, bf16[128,2048]{1,0:T(8,128)(2,1)S(1)}, u32[]{:S(2)}, u32[]{:S(2)}) collective-permute-start(bf16[128,2048]{1,0:T(8,128)(2,1)S(1)} %add_convert_fusion.8), channel_id=1, source_target_pairs={{0,2},{2,4},{4,6},{6,7},{7,5},{5,3},{3,1},{1,0},{8,10},{10,12},{12... | collective-permute-start | bytes 1572872 | tf_op jit(solution)/shard_map/ppermute | solution.py:63
  193.1 31.4 %collective-permute-start.20 = (bf16[128,2048]{1,0:T(8,128)(2,1)S(1)}, bf16[128,2048]{1,0:T(8,128)(2,1)S(1)}, u32[]{:S(2)}, u32[]{:S(2)}) collective-permute-start(bf16[128,2048]{1,0:T(8,128)(2,1)S(1)} %add_convert_fusion.9), channel_id=1, source_target_pairs={{2,0},{4,2},{6,4},{7,6},{5,7},{3,5},{1,3},{0,1},{10,8},{12,10},{14... | collective-permute-start | bytes 1572872 | tf_op jit(solution)/shard_map/ppermute | solution.py:63
  194.3 30.4 %collective-permute-start.35 = (bf16[128,2176]{1,0:T(8,128)(2,1)S(1)}, bf16[128,2176]{1,0:T(8,128)(2,1)S(1)}, u32[]{:S(2)}, u32[]{:S(2)}) collective-permute-start(bf16[128,2176]{1,0:T(8,128)(2,1)S(1)} %collective-permute-done.19), channel_id=1, source_target_pairs={{0,16},{8,24},{16,0},{24,8},{1,17},{9,25},{17,1},{25,9},{2,18},{10... | collective-permute-start | bytes 1671176 | tf_op jit(solution)/shard_map/ppermute | solution.py:133
  228.2 28.0 %collective-permute-start.27 = (bf16[768,512]{1,0:T(8,128)(2,1)S(1)}, bf16[768,512]{1,0:T(8,128)(2,1)S(1)}, u32[]{:S(2)}, u32[]{:S(2)}) collective-permute-start(bf16[768,512]{1,0:T(8,128)(2,1)S(1)} %slice.400), channel_id=1, source_target_pairs={{0,2},{2,3},{3,1},{1,0},{4,6},{6,7},{7,5},{5,4},{8,10},{10,11},{11... | collective-permute-start | bytes 2359304 | tf_op jit(solution)/shard_map/ppermute | solution.py:63
  229.5 35.4 %collective-permute-start.28 = (bf16[768,512]{1,0:T(8,128)(2,1)S(1)}, bf16[768,512]{1,0:T(8,128)(2,1)S(1)}, u32[]{:S(2)}, u32[]{:S(2)}) collective-permute-start(bf16[768,512]{1,0:T(8,128)(2,1)S(1)} %slice.401), channel_id=1, source_target_pairs={{2,0},{3,2},{1,3},{0,1},{6,4},{7,6},{5,7},{4,5},{10,8},{11,10},{9,... | collective-permute-start | bytes 2359304 | tf_op jit(solution)/shard_map/ppermute | solution.py:63
  244.4 28.2 %collective-permute-start.29 = (bf16[128,2048]{1,0:T(8,128)(2,1)S(1)}, bf16[128,2048]{1,0:T(8,128)(2,1)S(1)}, u32[]{:S(2)}, u32[]{:S(2)}) collective-permute-start(bf16[128,2048]{1,0:T(8,128)(2,1)S(1)} %get-tuple-element.563), channel_id=1, source_target_pairs={{0,16},{8,24},{16,0},{24,8},{1,17},{9,25},{17,1},{25,9},{2,18},{10... | collective-permute-start | bytes 1572872 | tf_op jit(solution)/shard_map/ppermute | solution.py:133
  246.1 31.8 %collective-permute-start.31 = (bf16[128,2048]{1,0:T(8,128)(2,1)S(1)}, bf16[128,2048]{1,0:T(8,128)(2,1)S(1)}, u32[]{:S(2)}, u32[]{:S(2)}) collective-permute-start(bf16[128,2048]{1,0:T(8,128)(2,1)S(1)} %get-tuple-element.563), channel_id=1, source_target_pairs={{0,8},{8,0},{16,24},{24,16},{1,9},{9,1},{17,25},{25,17},{2,10},{10... | collective-permute-start | bytes 1572872 | tf_op jit(solution)/shard_map/ppermute | solution.py:133
  269.0 34.3 %collective-permute-start.38 = (bf16[1536,512]{1,0:T(8,128)(2,1)}, bf16[1536,512]{1,0:T(8,128)(2,1)}, u32[]{:S(2)}, u32[]{:S(2)}) collective-permute-start(bf16[1536,512]{1,0:T(8,128)(2,1)} %pad_maximum_fusion.10.refs_0_), channel_id=1, source_target_pairs={{2,0},{3,2},{1,3},{0,1},{6,4},{7,6},{5,7},{4,5},{10,8},{11,10},{9,... | collective-permute-start | bytes 4718600 | tf_op jit(solution)/shard_map/ppermute | solution.py:63
  271.7 34.0 %collective-permute-start.39 = (bf16[1536,512]{1,0:T(8,128)(2,1)}, bf16[1536,512]{1,0:T(8,128)(2,1)}, u32[]{:S(2)}, u32[]{:S(2)}) collective-permute-start(bf16[1536,512]{1,0:T(8,128)(2,1)} %pad_maximum_fusion.10.refs_0_), channel_id=1, source_target_pairs={{0,2},{2,3},{3,1},{1,0},{4,6},{6,7},{7,5},{5,4},{8,10},{10,11},{11... | collective-permute-start | bytes 4718600 | tf_op jit(solution)/shard_map/ppermute | solution.py:63
  306.8 28.2 %collective-permute-start.40 = (bf16[768,512]{1,0:T(8,128)(2,1)S(1)}, bf16[768,512]{1,0:T(8,128)(2,1)}, u32[]{:S(2)}, u32[]{:S(2)}) collective-permute-start(bf16[768,512]{1,0:T(8,128)(2,1)S(1)} %slice.403), channel_id=1, source_target_pairs={{0,2},{2,3},{3,1},{1,0},{4,6},{6,7},{7,5},{5,4},{8,10},{10,11},{11... | collective-permute-start | bytes 2359304 | tf_op jit(solution)/shard_map/ppermute | solution.py:63
  308.2 26.8 %collective-permute-start.41 = (bf16[768,512]{1,0:T(8,128)(2,1)S(1)}, bf16[768,512]{1,0:T(8,128)(2,1)}, u32[]{:S(2)}, u32[]{:S(2)}) collective-permute-start(bf16[768,512]{1,0:T(8,128)(2,1)S(1)} %slice.404), channel_id=1, source_target_pairs={{2,0},{3,2},{1,3},{0,1},{6,4},{7,6},{5,7},{4,5},{10,8},{11,10},{9,... | collective-permute-start | bytes 2359304 | tf_op jit(solution)/shard_map/ppermute | solution.py:63
  366.3 27.2 %collective-permute-start.52 = (bf16[768,256]{1,0:T(8,128)(2,1)S(1)}, bf16[768,256]{1,0:T(8,128)(2,1)S(1)}, u32[]{:S(2)}, u32[]{:S(2)}) collective-permute-start(bf16[768,256]{1,0:T(8,128)(2,1)S(1)} %slice.745), channel_id=1, source_target_pairs={{0,4},{1,5},{2,6},{3,7},{4,0},{5,1},{6,2},{7,3},{8,12},{9,13},{10,... | collective-permute-start | bytes 1179656 | tf_op jit(solution)/shard_map/ppermute | solution.py:133
  368.8 32.1 %collective-permute-start.49 = (bf16[1536,256]{1,0:T(8,128)(2,1)S(1)}, bf16[1536,256]{1,0:T(8,128)(2,1)}, u32[]{:S(2)}, u32[]{:S(2)}) collective-permute-start(bf16[1536,256]{1,0:T(8,128)(2,1)S(1)} %pad_maximum_fusion.17), channel_id=1, source_target_pairs={{0,2},{2,3},{3,1},{1,0},{4,6},{6,7},{7,5},{5,4},{8,10},{10,11},{11... | collective-permute-start | bytes 2359304 | tf_op jit(solution)/shard_map/ppermute | solution.py:63
  370.8 30.1 %collective-permute-start.48 = (bf16[1536,256]{1,0:T(8,128)(2,1)S(1)}, bf16[1536,256]{1,0:T(8,128)(2,1)}, u32[]{:S(2)}, u32[]{:S(2)}) collective-permute-start(bf16[1536,256]{1,0:T(8,128)(2,1)S(1)} %pad_maximum_fusion.16), channel_id=1, source_target_pairs={{2,0},{3,2},{1,3},{0,1},{6,4},{7,6},{5,7},{4,5},{10,8},{11,10},{9,... | collective-permute-start | bytes 2359304 | tf_op jit(solution)/shard_map/ppermute | solution.py:63
  371.1 29.8 %collective-permute-start.50 = (bf16[768,256]{1,0:T(8,128)(2,1)}, bf16[768,256]{1,0:T(8,128)(2,1)}, u32[]{:S(2)}, u32[]{:S(2)}) collective-permute-start(bf16[768,256]{1,0:T(8,128)(2,1)} %get-tuple-element.348), channel_id=1, source_target_pairs={{2,0},{3,2},{1,3},{0,1},{6,4},{7,6},{5,7},{4,5},{10,8},{11,10},{9,... | collective-permute-start | bytes 1179656 | tf_op jit(solution)/shard_map/ppermute | solution.py:63
  372.3 28.6 %collective-permute-start.51 = (bf16[768,256]{1,0:T(8,128)(2,1)}, bf16[768,256]{1,0:T(8,128)(2,1)}, u32[]{:S(2)}, u32[]{:S(2)}) collective-permute-start(bf16[768,256]{1,0:T(8,128)(2,1)} %get-tuple-element.349), channel_id=1, source_target_pairs={{0,2},{2,3},{3,1},{1,0},{4,6},{6,7},{7,5},{5,4},{8,10},{10,11},{11... | collective-permute-start | bytes 1179656 | tf_op jit(solution)/shard_map/ppermute | solution.py:63
  526.8 70.5 %collective-permute-start.77 = (bf16[1536,256]{1,0:T(8,128)(2,1)}, bf16[1536,256]{1,0:T(8,128)(2,1)}, u32[]{:S(2)}, u32[]{:S(2)}) collective-permute-start(bf16[1536,256]{1,0:T(8,128)(2,1)} %pad_maximum_fusion.21), channel_id=1, source_target_pairs={{0,2},{2,3},{3,1},{1,0},{4,6},{6,7},{7,5},{5,4},{8,10},{10,11},{11... | collective-permute-start | bytes 2359304 | tf_op jit(solution)/shard_map/ppermute | solution.py:63
  529.3 68.0 %collective-permute-start.76 = (bf16[1536,256]{1,0:T(8,128)(2,1)}, bf16[1536,256]{1,0:T(8,128)(2,1)}, u32[]{:S(2)}, u32[]{:S(2)}) collective-permute-start(bf16[1536,256]{1,0:T(8,128)(2,1)} %pad_maximum_fusion.20), channel_id=1, source_target_pairs={{2,0},{3,2},{1,3},{0,1},{6,4},{7,6},{5,7},{4,5},{10,8},{11,10},{9,... | collective-permute-start | bytes 2359304 | tf_op jit(solution)/shard_map/ppermute | solution.py:63
  539.3 42.2 %collective-permute-start.78 = (bf16[128,2048]{1,0:T(8,128)(2,1)}, bf16[128,2048]{1,0:T(8,128)(2,1)}, u32[]{:S(2)}, u32[]{:S(2)}) collective-permute-start(bf16[128,2048]{1,0:T(8,128)(2,1)} %slice_add_fusion), channel_id=1, source_target_pairs={{0,4},{1,5},{2,6},{3,7},{4,0},{5,1},{6,2},{7,3},{8,12},{9,13},{10,... | collective-permute-start | bytes 1572872 | tf_op jit(solution)/shard_map/ppermute | solution.py:133
  541.5 55.8 %collective-permute-start.75 = (bf16[1536,256]{1,0:T(8,128)(2,1)}, bf16[1536,256]{1,0:T(8,128)(2,1)}, u32[]{:S(2)}, u32[]{:S(2)}) collective-permute-start(bf16[1536,256]{1,0:T(8,128)(2,1)} %pad_maximum_fusion.19), channel_id=1, source_target_pairs={{0,2},{2,3},{3,1},{1,0},{4,6},{6,7},{7,5},{5,4},{8,10},{10,11},{11... | collective-permute-start | bytes 2359304 | tf_op jit(solution)/shard_map/ppermute | solution.py:63
  544.6 52.7 %collective-permute-start.74 = (bf16[1536,256]{1,0:T(8,128)(2,1)}, bf16[1536,256]{1,0:T(8,128)(2,1)}, u32[]{:S(2)}, u32[]{:S(2)}) collective-permute-start(bf16[1536,256]{1,0:T(8,128)(2,1)} %pad_maximum_fusion.18), channel_id=1, source_target_pairs={{2,0},{3,2},{1,3},{0,1},{6,4},{7,6},{5,7},{4,5},{10,8},{11,10},{9,... | collective-permute-start | bytes 2359304 | tf_op jit(solution)/shard_map/ppermute | solution.py:63
  687.5 37.8 %collective-permute-start.101 = (bf16[768,512]{1,0:T(8,128)(2,1)S(1)}, bf16[768,512]{1,0:T(8,128)(2,1)S(1)}, u32[]{:S(2)}, u32[]{:S(2)}) collective-permute-start(bf16[768,512]{1,0:T(8,128)(2,1)S(1)} %slice.743), channel_id=1, source_target_pairs={{0,4},{1,5},{2,6},{3,7},{4,0},{5,1},{6,2},{7,3},{8,12},{9,13},{10,... | collective-permute-start | bytes 2359304 | tf_op jit(solution)/shard_map/ppermute | solution.py:133
  699.3 34.6 %collective-permute-start.96 = (bf16[2,8,64,768]{3,2,1,0:T(8,128)(2,1)}, bf16[2,8,64,768]{3,2,1,0:T(8,128)(2,1)}, u32[]{:S(2)}, u32[]{:S(2)}) collective-permute-start(bf16[2,8,64,768]{3,2,1,0:T(8,128)(2,1)} %maximum_bitcast_fusion.1), channel_id=1, source_target_pairs={{0,8},{8,0},{16,24},{24,16},{1,9},{9,1},{17,25},{25,17},{2,10},{10... | collective-permute-start | bytes 4718600 | tf_op jit(solution)/shard_map/ppermute | solution.py:133
  (185 other events, 2752.2 us)

commit v4 on v3

--- a/solution.py
+++ b/solution.py
@@ -230,27 +230,22 @@
             x = parts[0] if len(parts) == 1 else parts[::-1]
         return x if isinstance(x, list) else [x]
 
-    def exchange(self, x):
-        x = x.reshape((self.owners, self.split, -1) + x.shape[1:])
-        came = [
-            lax.ppermute(x[k], "expert", [(i, i ^ r) for i in range(self.owners)]) if r else x[k]
-            for k, r in enumerate(self.rel)
-        ]
-        return jnp.stack(came, axis=1)
-
-
-def expert_kernel(expert, turn, n, owner, m_ref, x_hbm, g_hbm, *refs):
+
+def expert_kernel(expert, turn, first, last, n, owner, m_ref, x_hbm, g_hbm, *refs):
     weights, refs = refs[:n], refs[n:]
-    mg_ref, mixing_ref, refs = refs[0], refs[1], refs[2:]
-    ends, grads, refs = refs[:2], refs[2 : n + 2], refs[n + 2 :]
+    before, refs = ((), refs) if first else (refs[:2], refs[2:])
+    state_ref, refs = refs[0], refs[1:]
+    k = 2 if last else 1
+    ends, refs = (refs[:k], refs[k : 2 * k]), refs[2 * k :]
+    grads, refs = refs[:n], refs[n:]
     x_ref, g_ref, y_ref, dx_ref, w_ref, d_ref, mixed_ref, gate_ref, up_ref = refs[:9]
-    in_sem, w_sem, end_sem, d_sem = refs[9:]
+    old_refs = refs[9:11]
+    in_sem, w_sem, end_sem, d_sem, old_sem = refs[11:]
     rows, model = x_ref.shape
     width = w_ref.shape[1]
     count = owner.shape[0] - 1
     depth = model // count
     tile = min(rows, 512)
-    routing = m_ref.shape[0] == model
     starts = [sum(w.shape[0] for w in weights[:j]) for j in range(n)] + [w_ref.shape[0]]
     places = []
     for k in range(count):
@@ -269,9 +264,17 @@
         here = pl.ds(starts[j], weights[j].shape[0])
         return copy(weights[j].at[:, pl.ds(turn * width, width)], w_ref.at[here], w_sem.at[j])
 
-    def finish(k, e):
-        at = places[k][0]
-        return copy((y_ref, dx_ref)[e].at[:, at], ends[e].at[:, at], end_sem.at[e, k])
+    def finish(k):
+        at = places[k][0] if k < count else pl.ds(model, 128)
+        copies = []
+        for what, (ref, parts) in enumerate(zip((y_ref, dx_ref), ends)):
+            half = rows // len(parts)
+            for e, to in enumerate(parts):
+                if k < count or what == 1:
+                    rows_at = pl.ds(e * half, half)
+                    sem = end_sem.at[2 * what + e, k]
+                    copies.append(copy(ref.at[rows_at, at], to.at[:, at], sem))
+        return copies
 
     def put(j):
         here = pl.ds(starts[j], weights[j].shape[0])
@@ -284,6 +287,9 @@
     for k in range(1, rows // tile):
         for what in range(2):
             fetch(k, what).start()
+
+    for what, old in enumerate(before):
+        copy(old, old_refs[what], old_sem.at[what]).start()
 
     for start in range(0, rows, tile):
         here = pl.ds(start, tile)
@@ -296,88 +302,130 @@
             x, g = x_ref[here, at], g_ref[here, at]
             a, b, c = mm(x, w_ref[parts[0]]), mm(x, w_ref[parts[1]]), mm(g, w_ref[parts[2]])
             gate, up, back = (a, b, c) if k == 0 else (gate + a, up + b, back + c)
-            if routing:
+            if first:
                 a = mm(x, m_ref[at])
                 logits = a if k == 0 else logits + a
-        if routing:
+        if first:
             named = g_ref[here, model:].astype(f32) > 0.0
             top = jnp.max(jnp.where(named, logits, -1e30), axis=1, keepdims=True)
             lifted = jnp.where(named, jnp.exp(jnp.minimum(logits - top, 0.0)), 0.0)
-            mixing = lifted * (1.0 / jnp.sum(lifted, axis=1, keepdims=True))
-            mixing_ref[here] = mixing
+            state = lifted * (1.0 / jnp.sum(lifted, axis=1, keepdims=True))
         else:
-            mixing = m_ref[here]
-        lanes = lax.broadcasted_iota(jnp.int32, mixing.shape, 1)
-        mine = jnp.where(lanes == owner[count] + expert, mixing, 0.0)
-        mix = jnp.sum(mine, axis=1, keepdims=True)
+            state = m_ref[here]
+        lanes = lax.broadcasted_iota(jnp.int32, state.shape, 1)
+        lane = owner[count] + expert
+        mix = jnp.sum(jnp.where(lanes == lane, state, 0.0), axis=1, keepdims=True)
         sig = 1.0 / (1.0 + jnp.exp(-gate))
         act = gate * sig
         hidden = act * up
-        mg_ref[here] = jnp.sum(hidden * back, axis=1, keepdims=True)
+        mixing_grad = jnp.sum(hidden * back, axis=1, keepdims=True)
+        state = state + jnp.where(lanes == 64 + lane, mixing_grad, 0.0)
+        state_ref[here] = state
+        if last:
+            state = jnp.where(lanes >= 64, state, 0.0)
+            near = state.astype(bf16).astype(f32)
+            dx_ref[here, model:] = (near + pltpu.roll(state - near, 32, 1)).astype(bf16)
         mixed_ref[here] = (mix * hidden).astype(bf16)
         hidden_grad = mix * back
         gate_ref[here] = (hidden_grad * up * sig * (1.0 + gate * (1.0 - sig))).astype(bf16)
         up_ref[here] = (hidden_grad * act).astype(bf16)
-    if not routing:
-        mixing_ref[...] = jnp.zeros_like(mixing_ref)
-
+    for what, old in enumerate(before):
+        copy(old, old_refs[what], old_sem.at[what]).wait()
     mixed, gate_grad, up_grad = mixed_ref[...], gate_ref[...], up_ref[...]
     for k, (at, parts) in enumerate(places):
-        y_ref[:, at] = mm(mixed, w_ref[parts[2]], NT).astype(bf16)
+        y = mm(mixed, w_ref[parts[2]], NT)
         dx = mm(gate_grad, w_ref[parts[0]], NT) + mm(up_grad, w_ref[parts[1]], NT)
-        dx_ref[:, at] = dx.astype(bf16)
-        for e in range(2):
-            finish(k, e).start()
+        if before:
+            y = y + old_refs[0][:, at].astype(f32)
+            dx = dx + old_refs[1][:, at].astype(f32)
+        y_ref[:, at], dx_ref[:, at] = y.astype(bf16), dx.astype(bf16)
+        for end in finish(k):
+            end.start()
         x, g = x_ref[:, at], g_ref[:, at]
         d_ref[parts[0]] = mm(x, gate_grad, TN).astype(bf16)
         d_ref[parts[1]] = mm(x, up_grad, TN).astype(bf16)
         d_ref[parts[2]] = mm(g, mixed, TN).astype(bf16)
         if k in final:
             put(final[k]).start()
-    for k in range(count):
-        for e in range(2):
-            finish(k, e).wait()
+    if last:
+        for end in finish(count):
+            end.start()
+    for k in range(count + last):
+        for end in finish(k):
+            end.wait()
     for j in range(n):
         put(j).wait()
 
 
-def expert_pass(expert, turn, turns, owner, x, g, mix, weights):
+def expert_pass(expert, turn, first, last, turns, owner, x, g, mix, weights, before):
     n = len(weights)
     rows, model = x.shape
     deep, width = sum(w.shape[0] for w in weights), weights[0].shape[1] // turns
     anywhere, vmem = pl.BlockSpec(memory_space=pl.ANY), pl.BlockSpec(memory_space=pltpu.VMEM)
     count = owner.shape[0] - 1
+    k = 2 if last else 1
+    wide = model + 128 if last else model
+    ends = [jax.ShapeDtypeStruct((rows // k, model), bf16)] * k
+    ends += [jax.ShapeDtypeStruct((rows // k, wide), bf16)] * k
+    old = pltpu.VMEM((8, 128) if first else (rows, model), bf16)
     out = pl.pallas_call(
-        functools.partial(expert_kernel, expert, turn, n),
-        in_specs=[pl.BlockSpec(memory_space=pltpu.SMEM), vmem] + [anywhere] * (2 + n),
-        out_specs=[vmem, vmem] + [anywhere] * (2 + n),
+        functools.partial(expert_kernel, expert, turn, first, last, n),
+        in_specs=[pl.BlockSpec(memory_space=pltpu.SMEM), vmem]
+        + [anywhere] * (2 + n + len(before)),
+        out_specs=[vmem] + [anywhere] * (2 * k + n),
         scratch_shapes=[
             pltpu.VMEM((rows, model), bf16),
             pltpu.VMEM((rows, g.shape[1]), bf16),
             pltpu.VMEM((rows, model), bf16),
-            pltpu.VMEM((rows, model), bf16),
+            pltpu.VMEM((rows, wide), bf16),
             pltpu.VMEM((deep, width), bf16),
             pltpu.VMEM((deep, width), bf16),
             pltpu.VMEM((rows, width), bf16),
             pltpu.VMEM((rows, width), bf16),
             pltpu.VMEM((rows, width), bf16),
+            old,
+            old,
             pltpu.SemaphoreType.DMA((2, -(-rows // 512))),
             pltpu.SemaphoreType.DMA((n,)),
-            pltpu.SemaphoreType.DMA((2, count)),
+            pltpu.SemaphoreType.DMA((4, count + 1)),
             pltpu.SemaphoreType.DMA((n,)),
+            pltpu.SemaphoreType.DMA((2,)),
         ],
-        out_shape=[
-            jax.ShapeDtypeStruct((rows, 1), f32),
-            jax.ShapeDtypeStruct((rows if mix.shape[0] == model else 8, 128), f32),
-        ]
-        + [jax.ShapeDtypeStruct((rows, model), bf16)] * 2
+        out_shape=[jax.ShapeDtypeStruct((rows, 128), f32)]
+        + ends
         + [jax.ShapeDtypeStruct((w.shape[0], width), bf16) for w in weights],
         compiler_params=pltpu.CompilerParams(vmem_limit_bytes=60 << 20),
         cost_estimate=pl.CostEstimate(
             flops=18 * rows * model * width, transcendentals=0, bytes_accessed=4 * deep * width
         ),
-    )(owner, mix, x, g, *weights)
-    return list(out[2:4]), out[0], out[1], list(out[4:])
+    )(owner, mix, x, g, *weights, *before)
+    return out[0], list(out[1 : 1 + 2 * k]), list(out[1 + 2 * k :])
+
+
+def spread_kernel(x_ref, *out_refs):
+    owners, shards, rows, columns = x_ref.shape
+    wide = columns // len(out_refs)
+    for e in range(owners):
+        for w in range(shards):
+            for i, out_ref in enumerate(out_refs):
+                part = x_ref[e, w, :, i * wide : (i + 1) * wide].astype(f32)
+                out_ref[e * rows : (e + 1) * rows, w * wide : (w + 1) * wide] = part
+
+
+def merge_kernel(upper_ref, *refs):
+    gate_ref, up_ref, down_ref = refs[-3:]
+    half = refs[0].shape[1]
+    depth = gate_ref.shape[1]
+    upper = upper_ref[0] > 0
+    for i in range(gate_ref.shape[0]):
+        for part, out_ref in enumerate((gate_ref, up_ref, down_ref)):
+            rows = pl.ds(part * depth, depth)
+            own, other = refs[2 * i][rows], refs[2 * i + 1][rows].astype(f32)
+            low, high = jnp.where(upper, other, own), jnp.where(upper, own, other)
+            if part < 2:
+                out_ref[i, :, :half], out_ref[i, :, half:] = low, high
+            else:
+                out_ref[i, :half], out_ref[i, half:] = low.T, high.T
 
 
 def inverse_rms(values):
@@ -519,10 +567,11 @@
     gain_ref[...] = gain
 
 
-def in_vmem(kernel, shapes, arrays, flops, scratch=()):
+def in_vmem(kernel, shapes, arrays, flops, scratch=(), scalars=0):
     return pl.pallas_call(
         kernel,
-        in_specs=[pl.BlockSpec(memory_space=pltpu.VMEM)] * len(arrays),
+        in_specs=[pl.BlockSpec(memory_space=pltpu.SMEM)] * scalars
+        + [pl.BlockSpec(memory_space=pltpu.VMEM)] * (len(arrays) - scalars),
         out_specs=[pl.BlockSpec(memory_space=pltpu.VMEM)] * len(shapes),
         out_shape=[jax.ShapeDtypeStruct(*shape) for shape in shapes],
         scratch_shapes=list(scratch),
@@ -685,7 +734,6 @@
     first_weights = weight_ring.gather(held["send"], halves, first=held["near"])
     ffn_far, first_weights[near:] = tie(ffn_far, first_weights[near:])
     second_block = crossed(1, after(cross_second, ffn_far or ffn_low))
-
     second_near = weight_ring.hop({1: second_block, -1: second_block})
     ffn_far = [b for block in ffn_far for b in group.gather(block)]
     ffn_all = group.join(ffn_own, ffn_far)
@@ -703,39 +751,35 @@
     turns = 2
     call = functools.partial(expert_pass, owner=block_owner, x=ffn_all, g=grad_and_names)
 
-    def part_call(expert, turn, mix, weights):
-        return call(expert, turn, turns, mix=mix, weights=weights)
-
-    (end00, mg00, mixing, parts00), second_near = tie(
+    def part_call(expert, turn, mix, weights, *before):
+        first, last = (expert, turn) == (0, 0), (expert, turn) == (local_experts - 1, turns - 1)
+        return call(expert, turn, first, last, turns, mix=mix, weights=weights, before=before)
+
+    (state, ends, parts00), second_near = tie(
         part_call(0, 0, router, first_weights), second_near
     )
     second_weights = weight_ring.gather(second_block, halves, first=second_near)
     m00 = weight_ring.begin(parts00, halves)
-    (end01, mg01, _, parts01), second_weights, m00 = tie(
-        part_call(0, 1, mixing, first_weights), second_weights, m00
+    (state, ends, parts01), second_weights, m00 = tie(
+        part_call(0, 1, state, first_weights, *ends), second_weights, m00
     )
     m00 = weight_ring.hop(weight_ring.added(parts00, m00, 2))
     m01 = weight_ring.begin(parts01, halves)
-    (end10, mg10, _, parts10), m00, m01 = tie(
-        part_call(1, 0, mixing, second_weights), m00, m01
+    (state, ends, parts10), m00, m01 = tie(
+        part_call(1, 0, state, second_weights, *ends), m00, m01
     )
     m01 = weight_ring.hop(weight_ring.added(parts01, m01, 2))
     m10 = weight_ring.begin(parts10, halves)
+    (state, ends, parts11), m01, m10 = tie(
+        part_call(1, 1, state, second_weights, *ends), m01, m10
+    )
     sum00 = weight_ring.finish(parts00, m00, halves, first=3)
-    home00 = uncross(sum00)
-    (end11, mg11, _, parts11), m01, m10, home00 = tie(
-        part_call(1, 1, mixing, second_weights), m01, m10, home00
-    )
-
-    def ends(which, begin):
-        count = ffn_all.shape[0] // 2
-        return sum(
-            end[which][begin * count : (begin + 1) * count].astype(f32)
-            for end in (end00, end01, end10, end11)
-        )
-
-    which = jnp.arange(experts, dtype=jnp.int32)[None, :]
-    came = group.exchange(jnp.concatenate([mg00 + mg01, mg10 + mg11], axis=1))
+    m10 = weight_ring.hop(weight_ring.added(parts10, m10, 2))
+    came = group.begin(ends[3])
+    y_came = group.begin(after(ends[1], came))
+    row_grads = group.scatter(ends[2], came=came)
+    row_grads[-1], m10 = tie(row_grads[-1], m10)
+    produced = group.scatter(after(ends[0], row_grads[-1]), came=y_came)
 
     def far_sum(blocks, hold):
         if split == 1:
@@ -743,21 +787,11 @@
         send = after(blocks[1].astype(bf16), hold)
         return blocks[0] + swap(send, "wshard", far).astype(f32)
 
-    row_grads = group.scatter(ends(1, 0), ends(1, 1).astype(bf16))
     ffn_grad = far_sum(row_grads, came)
-    if split == 2:
-        came_far = swap(after(came[1], row_grads[-1]), "wshard", far)
-        came = came[0] + after(came_far, row_grads[-1])
-    else:
-        came = came[0]
-    mixing_own = mixing[:rows, :experts]
-    mixing_grad = jnp.zeros_like(mixing_own)
-    for k, r in enumerate(group.rel):
-        block = came[k]
-        for i in range(local_experts):
-            at = which == (rank ^ r) * local_experts + i
-            mixing_grad = jnp.where(at, block[:, i : i + 1], mixing_grad)
-
+    mixing_grad = ffn_grad[:, model + 64 : model + 64 + experts]
+    mixing_grad = mixing_grad + ffn_grad[:, model + 96 : model + 96 + experts]
+    ffn_grad = ffn_grad[:, :model]
+    mixing_own = state[:rows, :experts]
     logits_grad = mixing_own * (
         mixing_grad - jnp.sum(mixing_own * mixing_grad, axis=1, keepdims=True)
     )
@@ -770,37 +804,24 @@
     ffn_gain_grad = jnp.sum(ffn_grad * (middle * ffn_inverse), axis=0)
     middle_grad = d_output.astype(f32) + norm_back(middle, ffn_inverse, ffn_gain, ffn_grad)
     attended_low = middle_grad.astype(bf16)
-
-    def uncrossed(total, other):
-        if split == 1:
-            return total
-        own, other = total[: 3 * depth], other.astype(f32)
-        return jnp.concatenate(
-            [jnp.where(upper, other, own), jnp.where(upper, own, other)], axis=1
-        )
 
     def middle_hook(s, moving):
         if s == 2:
             held["m11"] = weight_ring.begin(after(parts11, moving), halves)
         if s == 3:
-            moving, held["y"] = tie(moving, held["y"])
+            moving, held["y"] = tie(moving, produced)
         if s == ring.half:
             moving, held["m11"] = tie(moving, held["m11"])
         return moving
 
-    end00, end01, end10, end11 = after((end00, end01, end10, end11), attended_low)
-    held["y"] = group.scatter(ends(0, 0), ends(0, 1).astype(bf16))
 
     attended_blocks = ring.gather(attended_low, True, middle_hook)
-    attended_blocks, produced = tie(attended_blocks, held["y"])
-    expert_out = far_sum(produced, attended_blocks[-1])
+    expert_out = far_sum(held["y"], attended_blocks[-1])
     sum01 = weight_ring.finish(parts01, m01, halves, first=3)
-    home01 = uncross(after(sum01, attended_blocks[-1]))
-    parts10 = after(parts10, attended_blocks[-1])
-    second_moving = [
-        weight_ring.hop(weight_ring.added(parts10, m10, 2)),
-        weight_ring.hop(weight_ring.added(parts11, held["m11"], 2)),
-    ]
+    first_sum = jnp.concatenate([sum00, sum01], axis=1)
+    first_home = uncross(after(first_sum, attended_blocks[-1]))
+    second_moving = weight_ring.added(after(parts11, attended_blocks[-1]), held["m11"], 2)
+    second_moving = weight_ring.hop(second_moving)
     raw_grad, attn_gain_grad, head_gain_grad, *normed_part = in_vmem(
         functools.partial(attention_back_kernel, len(token_blocks), heads, tile),
         [((sequence, 3 * wide), bf16), ((1, model), f32), ((2, HEAD_DIM), f32)]
@@ -811,7 +832,9 @@
         [pltpu.VMEM((sequence, wide), dtype) for dtype in (bf16, f32, f32, f32)],
     )
     due = (normed_part, raw_grad, attn_gain_grad, head_gain_grad)
-    due, second_moving, expert_out, home01 = tie(due, second_moving, expert_out, home01)
+    due, second_moving, expert_out, first_home = tie(
+        due, second_moving, expert_out, first_home
+    )
     normed_part, raw_grad, attn_gain_grad, head_gain_grad = due
     final_stream = middle + expert_out
     output = final_stream.astype(bf16)
@@ -849,6 +872,8 @@
             held["fold"] = fold.send() if fold.left else None
         if s == 2:
             held["n2"] = moving
+        if s == ring.half:
+            held["n4"] = moving
         if s == ring.half + 1:
             held["end"] = moving
         return moving
@@ -859,34 +884,41 @@
     ).astype(bf16)
     if held["fold"] is not None:
         fold.add(held["fold"])
-    qkv_grad = after(fold.finish(), small.total)
+    qkv_grad = fold.finish()
     qkv_grad = lax.all_to_all(qkv_grad, "wshard", split_axis=0, concat_axis=0, tiled=True)
     qkv_grad = gather_bits(qkv_grad, "expert")
-    query_weight_grad, key_weight_grad, value_weight_grad = [
-        qkv_grad[..., i * wide : (i + 1) * wide]
-        .transpose(0, 2, 1, 3)
-        .reshape(owners * quarter, model)
-        .astype(f32)
-        for i in range(3)
-    ]
-    out_grad = mm(mixed, after(jnp.concatenate(attended_blocks, axis=0), held["n2"]), TN)
+    query_weight_grad, key_weight_grad, value_weight_grad = in_vmem(
+        spread_kernel, [((owners * quarter, model), f32)] * 3, [qkv_grad], 0
+    )
+    out_grad = mm(mixed, after(jnp.concatenate(attended_blocks, axis=0), held["n4"]), TN)
     out_grad = Fold(out_grad.astype(bf16).reshape(owners, -1, model), "expert").finish()
     out_grad = gather_bits(out_grad, "expert").reshape(-1, model).astype(f32)
 
     second_sum = jnp.concatenate(
         [
             weight_ring.finish(parts, moving, halves, first=3)
-            for parts, moving in zip((parts10, parts11), second_moving)
+            for parts, moving in ((parts10, m10), (parts11, second_moving))
         ],
         axis=1,
     )
     second_home = uncross(after(second_sum, held["end"]))
-    first_sum = jnp.concatenate([sum00, sum01], axis=1)
-    first_home = jnp.concatenate([home00, home01], axis=1)
-    summed = [uncrossed(first_sum, first_home), uncrossed(second_sum, second_home)]
-    gate_weight_grad = jnp.stack([s[:depth] for s in summed])
-    up_weight_grad = jnp.stack([s[depth : 2 * depth] for s in summed])
-    down_weight_grad = jnp.stack([s[2 * depth :].T for s in summed])
+    if split == 2:
+        flag = jnp.where(upper, 1, 0).astype(jnp.int32)[None]
+        pairs = [first_sum[: 3 * depth], first_home, second_sum[: 3 * depth], second_home]
+        hidden = gate_weight.shape[2]
+        wide_shape, tall_shape = (local_experts, depth, hidden), (local_experts, hidden, depth)
+        gate_weight_grad, up_weight_grad, down_weight_grad = in_vmem(
+            merge_kernel,
+            [(wide_shape, f32), (wide_shape, f32), (tall_shape, f32)],
+            [flag, *pairs],
+            0,
+            scalars=1,
+        )
+    else:
+        summed = (first_sum, second_sum)
+        gate_weight_grad = jnp.stack([s[:depth] for s in summed])
+        up_weight_grad = jnp.stack([s[depth : 2 * depth] for s in summed])
+        down_weight_grad = jnp.stack([s[2 * depth :].T for s in summed])
 
     small_sums = small.finish().reshape(-1)
     sizes = [router_size, model, model, HEAD_DIM, HEAD_DIM, 4]

time: 755 us -> 716 us (0.948)
  other arithmetic: 94 us -> 59.3 us
  local copies, waits for them, and re-layouts: 65.1 us -> 50 us
  Pallas kernels: 130 us -> 144 us
    another operation x9 -> x2, other arithmetic: 16.4 us -> 1.58 us
    unnamed x261 -> x206, local copies, waits for them, and re-layouts: 30.2 us -> 16.8 us
    pallas_call x6 -> x8, Pallas kernels: 130 us -> 144 us  [the longest x4 81.9 us: expert_pass(): pl.pallas_call(functools.partial(expert_kernel, expert, turn, first, last...]
    convert_element_type x4 -> x0, other arithmetic: 12.5 us -> none  [the longest x1 7.01 us: local(): row_grads = group.scatter(ends(1, 0), ends(1, 1).astype(bf16))]
    all_to_all x1, waiting for transfers between devices: 12 us -> 0.01 us  [local(): lax.all_to_all(qkv_grad, 'wshard', split_axis=0, concat_axis=0, tiled=True)]
    ppermute x3 -> x0, waiting for transfers between devices: 11.7 us -> none  [exchange(): lax.ppermute(x[k], 'expert', [(i, i ^ r) for i in range(self.owners)])]
    ppermute x43 -> x41, waiting for transfers between devices: 136 us -> 147 us  [swap(): lax.ppermute(x, axis, [(i, i ^ bit) for i in range(lax.axis_size(axis))])]
    ppermute x56, waiting for transfers between devices: 159 us -> 169 us  [hop(): lax.ppermute(block, self.axis, self.down if sign == 1 else self.up)]
  transfers between devices with their start and end apart: 104 -> 99, of which waited for: 48 -> 47; matrix products, arithmetic and copies ran while one was open for 15% -> 14% of each run, Pallas kernels for 17% -> 20%
where the time goes in v4:
time: 716 us; the launch traced here: 710 us
  waiting for transfers between devices  316 us (44%)
  Pallas kernels  144 us (20%)
  starting transfers between devices  128 us (18%)
  other arithmetic  59.3 us (8%)
  local copies, waits for them, and re-layouts  50 us (7%)
  matrix products  10.3 us (1%)
    ppermute x56, waiting for transfers between devices, hop(): lax.ppermute(block, self.axis, self.down if sign == 1 else self.up)  169 us
    ppermute x41, waiting for transfers between devices, swap(): lax.ppermute(x, axis, [(i, i ^ bit) for i in range(lax.axis_size(axis))])  147 us
    pallas_call x4, Pallas kernels, expert_pass(): pl.pallas_call(functools.partial(expert_kernel, expert, turn, first, last...  81.9 us
    ppermute x56, starting transfers between devices, hop(): lax.ppermute(block, self.axis, self.down if sign == 1 else self.up)  79.6 us
    pallas_call x4, Pallas kernels, in_vmem(): pl.pallas_call(kernel, in_specs=[pl.BlockSpec(memory_space=pltpu.SMEM)] *...  61.7 us
    ppermute x41, starting transfers between devices, swap(): lax.ppermute(x, axis, [(i, i ^ bit) for i in range(lax.axis_size(axis))])  38 us
    unnamed x206, local copies, waits for them, and re-layouts  16.8 us
  transfers between devices with their start and end apart: 99, of which 47 were waited for; matrix products, arithmetic and copies ran while one was open for 14% of the time, Pallas kernels for 20%

profile of v4, /device:TPU:0, one launch (start us, length us, event | category | flops | bytes accessed | tf_op | source)
XLA Modules:
  0.0 709.7 jit_solution(7086356665224017988)
XLA Ops:
  6.2 6.4 all-to-all-start
  21.9 17.2 %collective-permute-done.2.refs_3_.refs_12_ = bf16[128,2048]{1,0:T(8,128)(2,1)} collective-permute-done((bf16[128,2048]{1,0:T(8,128)(2,1)S(1)}, bf16[128,2048]{1,0:T(8,128)(2,1)}, u32[]{:S(2)}, u32[]{:S(2)}) %collective-permute-start.2) | collective-permute-done | bytes 524320 | tf_op jit(solution)/shard_map/ppermute | solution.py:63
  43.1 5.8 collective-permute-start.4
  67.6 5.7 collective-permute-start.6
  83.8 20.2 %shard_map.325 = (bf16[1024,2048]{1,0:T(8,128)(2,1)}, f32[1024,1]{1,0:T(8,128)}, f32[1024,512]{1,0:T(8,128)}, bf16[1024,768]{1,0:T(8,128)(2,1)}, f32[1024,2]{1,0...) custom-call(bf16[128,2048]{1,0:T(8,128)(2,1)} %refs_9_.1, ...), custom_call_target="tpu_custom_call" | custom-call | flops 21474836480 | bytes 9454592 | tf_op jit(solution)/shard_map/pallas_call | solution.py:571
  104.0 27.8 %collective-permute-done.10 = bf16[768,512]{1,0:T(8,128)(2,1)} collective-permute-done((bf16[768,512]{1,0:T(8,128)(2,1)}, bf16[768,512]{1,0:T(8,128)(2,1)}, u32[]{:S(2)}, u32[]{:S(2)}) %collective-permute-start.10) | collective-permute-done | bytes 786464 | tf_op jit(solution)/shard_map/ppermute | solution.py:133
  131.8 15.7 %collective-permute-done.11 = bf16[768,512]{1,0:T(8,128)(2,1)S(1)} collective-permute-done((bf16[768,512]{1,0:T(8,128)(2,1)}, bf16[768,512]{1,0:T(8,128)(2,1)S(1)}, u32[]{:S(2)}, u32[]{:S(2)}) %collective-permute-start.11) | collective-permute-done | bytes 786464 | tf_op jit(solution)/shard_map/ppermute | solution.py:133
  161.9 10.0 %collective-permute-start.22 = (bf16[1536,512]{1,0:T(8,128)(2,1)S(1)}, bf16[1536,512]{1,0:T(8,128)(2,1)S(1)}, u32[]{:S(2)}, u32[]{:S(2)}) collective-permute-start(bf16[1536,512]{1,0:T(8,128)(2,1)S(1)} %pad_maximum_fusion.6.refs_0_), channel_id=1, source_target_pairs={{2,0},{3,2},{1,3},{0,1},{6,4},{7,6},{5,7},{4,5},{10,8},{11,10},{9,... | collective-permute-start | bytes 4718600 | tf_op jit(solution)/shard_map/ppermute | solution.py:63
  178.4 14.1 %collective-permute-done.16 = bf16[128,2048]{1,0:T(8,128)(2,1)S(1)} collective-permute-done((bf16[128,2048]{1,0:T(8,128)(2,1)S(1)}, bf16[128,2048]{1,0:T(8,128)(2,1)S(1)}, u32[]{:S(2)}, u32[]{:S(2)}) %collective-permute-start.16) | collective-permute-done | bytes 524320 | tf_op jit(solution)/shard_map/ppermute | solution.py:63
  197.5 24.4 %collective-permute-done.21 = bf16[128,2048]{1,0:T(8,128)(2,1)S(1)} collective-permute-done((bf16[128,2048]{1,0:T(8,128)(2,1)S(1)}, bf16[128,2048]{1,0:T(8,128)(2,1)S(1)}, u32[]{:S(2)}, u32[]{:S(2)}) %collective-permute-start.21) | collective-permute-done | bytes 524320 | tf_op jit(solution)/shard_map/ppermute | solution.py:63
  230.9 9.3 %collective-permute-done.24 = bf16[128,2048]{1,0:T(8,128)(2,1)S(1)} collective-permute-done((bf16[128,2048]{1,0:T(8,128)(2,1)S(1)}, bf16[128,2048]{1,0:T(8,128)(2,1)S(1)}, u32[]{:S(2)}, u32[]{:S(2)}) %collective-permute-start.24) | collective-permute-done | bytes 524320 | tf_op jit(solution)/shard_map/ppermute | solution.py:63
  247.7 8.9 %collective-permute-done.27.refs_3_ = bf16[768,512]{1,0:T(8,128)(2,1)S(1)} collective-permute-done((bf16[768,512]{1,0:T(8,128)(2,1)S(1)}, bf16[768,512]{1,0:T(8,128)(2,1)S(1)}, u32[]{:S(2)}, u32[]{:S(2)}) %collective-permute-start.27) | collective-permute-done | bytes 786464 | tf_op jit(solution)/shard_map/ppermute | solution.py:63
  256.7 8.8 %collective-permute-done.28.refs_4_ = bf16[768,512]{1,0:T(8,128)(2,1)S(1)} collective-permute-done((bf16[768,512]{1,0:T(8,128)(2,1)S(1)}, bf16[768,512]{1,0:T(8,128)(2,1)S(1)}, u32[]{:S(2)}, u32[]{:S(2)}) %collective-permute-start.28) | collective-permute-done | bytes 786464 | tf_op jit(solution)/shard_map/ppermute | solution.py:63
  282.3 18.3 %shard_map.326 = (f32[1024,128]{1,0:T(8,128)}, bf16[1024,2048]{1,0:T(8,128)(2,1)}, bf16[1024,2048]{1,0:T(8,128)(2,1)}, bf16[1536,256]{1,0:T(8,128)(2,1)}, bf16[1...) custom-call(s32[9]{0:T(128)} %pad_add_fusion.1.owner, ...), custom_call_target="tpu_custom_call" | custom-call | flops 9663676416 | bytes 6291456 | tf_op jit(solution)/shard_map/pallas_call | solution.py:371
  310.5 21.2 %shard_map.327 = (f32[1024,128]{1,0:T(8,128)}, bf16[1024,2048]{1,0:T(8,128)(2,1)}, bf16[1024,2048]{1,0:T(8,128)(2,1)}, bf16[1536,256]{1,0:T(8,128)(2,1)}, bf16[1...) custom-call(s32[9]{0:T(128)} %pad_add_fusion.1.owner, ...), custom_call_target="tpu_custom_call" | custom-call | flops 9663676416 | bytes 6291456 | tf_op jit(solution)/shard_map/pallas_call | solution.py:371
  339.2 20.5 %shard_map.328 = (f32[1024,128]{1,0:T(8,128)}, bf16[1024,2048]{1,0:T(8,128)(2,1)}, bf16[1024,2048]{1,0:T(8,128)(2,1)}, bf16[1536,256]{1,0:T(8,128)(2,1)}, bf16[1...) custom-call(s32[9]{0:T(128)} %pad_add_fusion.1.owner, ...), custom_call_target="tpu_custom_call" | custom-call | flops 9663676416 | bytes 6291456 | tf_op jit(solution)/shard_map/pallas_call | solution.py:371
  367.4 21.8 %shard_map.329 = (f32[1024,128]{1,0:T(8,128)}, bf16[512,2048]{1,0:T(8,128)(2,1)}, bf16[512,2048]{1,0:T(8,128)(2,1)}, bf16[512,2176]{1,0:T(8,128)(2,1)}, bf16[512...) custom-call(s32[9]{0:T(128)} %pad_add_fusion.1.owner, ...), custom_call_target="tpu_custom_call" | custom-call | flops 9663676416 | bytes 6291456 | tf_op jit(solution)/shard_map/pallas_call | solution.py:371
  406.4 9.2 %collective-permute-done.54 = bf16[128,2176]{1,0:T(8,128)(2,1)S(1)} collective-permute-done((bf16[128,2176]{1,0:T(8,128)(2,1)S(1)}, bf16[128,2176]{1,0:T(8,128)(2,1)S(1)}, u32[]{:S(2)}, u32[]{:S(2)}) %collective-permute-start.54) | collective-permute-done | bytes 557088 | tf_op jit(solution)/shard_map/ppermute | solution.py:133
  418.8 8.0 %collective-permute-done.53 = bf16[128,2176]{1,0:T(8,128)(2,1)S(1)} collective-permute-done((bf16[128,2176]{1,0:T(8,128)(2,1)S(1)}, bf16[128,2176]{1,0:T(8,128)(2,1)S(1)}, u32[]{:S(2)}, u32[]{:S(2)}) %collective-permute-start.53) | collective-permute-done | bytes 557088 | tf_op jit(solution)/shard_map/ppermute | solution.py:133
  426.8 17.3 %collective-permute-done.57 = bf16[128,2176]{1,0:T(8,128)(2,1)S(1)} collective-permute-done((bf16[128,2176]{1,0:T(8,128)(2,1)S(1)}, bf16[128,2176]{1,0:T(8,128)(2,1)S(1)}, u32[]{:S(2)}, u32[]{:S(2)}) %collective-permute-start.57) | collective-permute-done | bytes 557088 | tf_op jit(solution)/shard_map/ppermute | solution.py:133
  455.3 7.1 collective-permute-done.58.refs_1_
  469.2 8.5 %collective-permute-done.63 = bf16[128,2048]{1,0:T(8,128)(2,1)S(1)} collective-permute-done((bf16[128,2048]{1,0:T(8,128)(2,1)S(1)}, bf16[128,2048]{1,0:T(8,128)(2,1)S(1)}, u32[]{:S(2)}, u32[]{:S(2)}) %collective-permute-start.63) | collective-permute-done | bytes 524320 | tf_op jit(solution)/shard_map/ppermute | solution.py:133
  477.9 7.1 %collective-permute-done.60.refs_3_ = bf16[128,2048]{1,0:T(8,128)(2,1)S(1)} collective-permute-done((bf16[128,2048]{1,0:T(8,128)(2,1)S(1)}, bf16[128,2048]{1,0:T(8,128)(2,1)S(1)}, u32[]{:S(2)}, u32[]{:S(2)}) %collective-permute-start.60) | collective-permute-done | bytes 524320 | tf_op jit(solution)/shard_map/ppermute | solution.py:63
  487.2 9.3 %collective-permute-done.66.refs_6_ = bf16[128,2048]{1,0:T(8,128)(2,1)S(1)} collective-permute-done((bf16[128,2048]{1,0:T(8,128)(2,1)S(1)}, bf16[128,2048]{1,0:T(8,128)(2,1)S(1)}, u32[]{:S(2)}, u32[]{:S(2)}) %collective-permute-start.66) | collective-permute-done | bytes 524320 | tf_op jit(solution)/shard_map/ppermute | solution.py:63
  513.6 31.0 %shard_map.330 = (bf16[1024,768]{1,0:T(8,128)(2,1)}, f32[1,2048]{1,0:T(1,128)}, f32[2,128]{1,0:T(2,128)}, bf16[128,2048]{1,0:T(8,128)(2,1)}, bf16[128,2048]{1,0:...) custom-call(bf16[128,2048]{1,0:T(8,128)(2,1)} %copy-done.38, ...), custom_call_target="tpu_custom_call" | custom-call | flops 27917287424 | bytes 17323008 | tf_op jit(solution)/shard_map/pallas_call | solution.py:571
  547.2 13.2 %collective-permute-done.73 = bf16[128,2048]{1,0:T(8,128)(2,1)} collective-permute-done((bf16[128,2048]{1,0:T(8,128)(2,1)}, bf16[128,2048]{1,0:T(8,128)(2,1)}, u32[]{:S(2)}, u32[]{:S(2)}) %collective-permute-start.73) | collective-permute-done | bytes 524320 | tf_op jit(solution)/shard_map/ppermute | solution.py:133
  590.1 8.4 %collective-permute-done.81 = bf16[128,2048]{1,0:T(8,128)(2,1)S(1)} collective-permute-done((bf16[128,2048]{1,0:T(8,128)(2,1)S(1)}, bf16[128,2048]{1,0:T(8,128)(2,1)S(1)}, u32[]{:S(2)}, u32[]{:S(2)}) %collective-permute-start.81) | collective-permute-done | bytes 524320 | tf_op jit(solution)/shard_map/ppermute | solution.py:63
  600.0 6.7 collective-permute-done.83
  611.5 9.1 %collective-permute-done.87 = f32[163,128]{1,0:T(8,128)S(1)} collective-permute-done((f32[163,128]{1,0:T(8,128)S(1)}, f32[163,128]{1,0:T(8,128)S(1)}, u32[]{:S(2)}, u32[]{:S(2)}) %collective-permute-start.87) | collective-permute-done | bytes 83488 | tf_op jit(solution)/shard_map/ppermute | solution.py:133
  627.7 15.0 %collective-permute-done.84 = bf16[128,2048]{1,0:T(8,128)(2,1)S(1)} collective-permute-done((bf16[128,2048]{1,0:T(8,128)(2,1)}, bf16[128,2048]{1,0:T(8,128)(2,1)S(1)}, u32[]{:S(2)}, u32[]{:S(2)}) %collective-permute-start.84) | collective-permute-done | bytes 524320 | tf_op jit(solution)/shard_map/ppermute | solution.py:63
  670.5 14.1 %collective-permute-done.90 = bf16[1,8,64,768]{3,2,1,0:T(8,128)(2,1)S(1)} collective-permute-done((bf16[1,8,64,768]{3,2,1,0:T(8,128)(2,1)S(1)}, bf16[1,8,64,768]{3,2,1,0:T(8,128)(2,1)S(1)}, u32[]{:S(2)}, u32[]{:S(2)}) %collective-permute-start.90) | collective-permute-done | bytes 786464 | tf_op jit(solution)/shard_map/ppermute | solution.py:133
  692.2 5.8 shard_map.332
  (542 shorter events, 280.8 us)
Async XLA Ops:
  6.2 35.1 %all-to-all-start = ((bf16[8,64,768]{2,1,0:T(8,128)(2,1)}), bf16[8,64,768]{2,1,0:T(8,128)(2,1)S(1)}, u32[]{:S(2)}, u32[]{:S(2)}) async-start(bf16[8,64,768]{2,1,0:T(8,128)(2,1)} %copy.87), calls=%async_computation | async-start | bytes 1572864 | tf_op jit(solution)/shard_map/all_to_all | solution.py:630
  54.3 49.6 %collective-permute-start.13 = (bf16[128,2176]{1,0:T(8,128)(2,1)S(1)}, bf16[128,2176]{1,0:T(8,128)(2,1)}, u32[]{:S(2)}, u32[]{:S(2)}) collective-permute-start(bf16[128,2176]{1,0:T(8,128)(2,1)S(1)} %pad_maximum_fusion.17), channel_id=1, source_target_pairs={{0,8},{8,0},{16,24},{24,16},{1,9},{9,1},{17,25},{25,17},{2,10},{10... | collective-permute-start | bytes 1671176 | tf_op jit(solution)/shard_map/ppermute | solution.py:133
  73.3 30.7 %collective-permute-start.14 = (bf16[128,2176]{1,0:T(8,128)(2,1)}, bf16[128,2176]{1,0:T(8,128)(2,1)}, u32[]{:S(2)}, u32[]{:S(2)}) collective-permute-start(bf16[128,2176]{1,0:T(8,128)(2,1)} %collective-permute-done.12), channel_id=1, source_target_pairs={{0,8},{8,0},{16,24},{24,16},{1,9},{9,1},{17,25},{25,17},{2,10},{10... | collective-permute-start | bytes 1671176 | tf_op jit(solution)/shard_map/ppermute | solution.py:133
  77.7 54.1 %collective-permute-start.10 = (bf16[768,512]{1,0:T(8,128)(2,1)}, bf16[768,512]{1,0:T(8,128)(2,1)}, u32[]{:S(2)}, u32[]{:S(2)}) collective-permute-start(bf16[768,512]{1,0:T(8,128)(2,1)} %get-tuple-element.246), channel_id=1, source_target_pairs={{0,4},{1,5},{2,6},{3,7},{4,0},{5,1},{6,2},{7,3},{8,12},{9,13},{10,... | collective-permute-start | bytes 2359304 | tf_op jit(solution)/shard_map/ppermute | solution.py:133
  79.2 68.3 %collective-permute-start.11 = (bf16[768,512]{1,0:T(8,128)(2,1)}, bf16[768,512]{1,0:T(8,128)(2,1)S(1)}, u32[]{:S(2)}, u32[]{:S(2)}) collective-permute-start(bf16[768,512]{1,0:T(8,128)(2,1)} %get-tuple-element.247), channel_id=1, source_target_pairs={{0,4},{1,5},{2,6},{3,7},{4,0},{5,1},{6,2},{7,3},{8,12},{9,13},{10,... | collective-permute-start | bytes 2359304 | tf_op jit(solution)/shard_map/ppermute | solution.py:133
  152.4 40.3 %collective-permute-start.19 = (bf16[128,2176]{1,0:T(8,128)(2,1)S(1)}, bf16[128,2176]{1,0:T(8,128)(2,1)S(1)}, u32[]{:S(2)}, u32[]{:S(2)}) collective-permute-start(bf16[128,2176]{1,0:T(8,128)(2,1)S(1)} %pad_maximum_fusion.17), channel_id=1, source_target_pairs={{0,4},{1,5},{2,6},{3,7},{4,0},{5,1},{6,2},{7,3},{8,12},{9,13},{10,... | collective-permute-start | bytes 1671176 | tf_op jit(solution)/shard_map/ppermute | solution.py:133
  157.9 34.6 %collective-permute-start.16 = (bf16[128,2048]{1,0:T(8,128)(2,1)S(1)}, bf16[128,2048]{1,0:T(8,128)(2,1)S(1)}, u32[]{:S(2)}, u32[]{:S(2)}) collective-permute-start(bf16[128,2048]{1,0:T(8,128)(2,1)S(1)} %pad_maximum_fusion.20), channel_id=1, source_target_pairs={{2,0},{4,2},{6,4},{7,6},{5,7},{3,5},{1,3},{0,1},{10,8},{12,10},{14... | collective-permute-start | bytes 1572872 | tf_op jit(solution)/shard_map/ppermute | solution.py:63
  161.9 63.3 %collective-permute-start.22 = (bf16[1536,512]{1,0:T(8,128)(2,1)S(1)}, bf16[1536,512]{1,0:T(8,128)(2,1)S(1)}, u32[]{:S(2)}, u32[]{:S(2)}) collective-permute-start(bf16[1536,512]{1,0:T(8,128)(2,1)S(1)} %pad_maximum_fusion.6.refs_0_), channel_id=1, source_target_pairs={{2,0},{3,2},{1,3},{0,1},{6,4},{7,6},{5,7},{4,5},{10,8},{11,10},{9,... | collective-permute-start | bytes 4718600 | tf_op jit(solution)/shard_map/ppermute | solution.py:63
  172.0 53.3 %collective-permute-start.23 = (bf16[1536,512]{1,0:T(8,128)(2,1)S(1)}, bf16[1536,512]{1,0:T(8,128)(2,1)S(1)}, u32[]{:S(2)}, u32[]{:S(2)}) collective-permute-start(bf16[1536,512]{1,0:T(8,128)(2,1)S(1)} %pad_maximum_fusion.6.refs_0_), channel_id=1, source_target_pairs={{0,2},{2,3},{3,1},{1,0},{4,6},{6,7},{7,5},{5,4},{8,10},{10,11},{11... | collective-permute-start | bytes 4718600 | tf_op jit(solution)/shard_map/ppermute | solution.py:63
  192.7 29.1 %collective-permute-start.21 = (bf16[128,2048]{1,0:T(8,128)(2,1)S(1)}, bf16[128,2048]{1,0:T(8,128)(2,1)S(1)}, u32[]{:S(2)}, u32[]{:S(2)}) collective-permute-start(bf16[128,2048]{1,0:T(8,128)(2,1)S(1)} %add_convert_fusion.6), channel_id=1, source_target_pairs={{0,2},{2,4},{4,6},{6,7},{7,5},{5,3},{3,1},{1,0},{8,10},{10,12},{12... | collective-permute-start | bytes 1572872 | tf_op jit(solution)/shard_map/ppermute | solution.py:63
  193.6 31.4 %collective-permute-start.20 = (bf16[128,2048]{1,0:T(8,128)(2,1)S(1)}, bf16[128,2048]{1,0:T(8,128)(2,1)S(1)}, u32[]{:S(2)}, u32[]{:S(2)}) collective-permute-start(bf16[128,2048]{1,0:T(8,128)(2,1)S(1)} %add_convert_fusion.7), channel_id=1, source_target_pairs={{2,0},{4,2},{6,4},{7,6},{5,7},{3,5},{1,3},{0,1},{10,8},{12,10},{14... | collective-permute-start | bytes 1572872 | tf_op jit(solution)/shard_map/ppermute | solution.py:63
  194.8 30.4 %collective-permute-start.35 = (bf16[128,2176]{1,0:T(8,128)(2,1)S(1)}, bf16[128,2176]{1,0:T(8,128)(2,1)S(1)}, u32[]{:S(2)}, u32[]{:S(2)}) collective-permute-start(bf16[128,2176]{1,0:T(8,128)(2,1)S(1)} %collective-permute-done.19), channel_id=1, source_target_pairs={{0,16},{8,24},{16,0},{24,8},{1,17},{9,25},{17,1},{25,9},{2,18},{10... | collective-permute-start | bytes 1671176 | tf_op jit(solution)/shard_map/ppermute | solution.py:133
  228.7 28.0 %collective-permute-start.27 = (bf16[768,512]{1,0:T(8,128)(2,1)S(1)}, bf16[768,512]{1,0:T(8,128)(2,1)S(1)}, u32[]{:S(2)}, u32[]{:S(2)}) collective-permute-start(bf16[768,512]{1,0:T(8,128)(2,1)S(1)} %slice.272), channel_id=1, source_target_pairs={{0,2},{2,3},{3,1},{1,0},{4,6},{6,7},{7,5},{5,4},{8,10},{10,11},{11... | collective-permute-start | bytes 2359304 | tf_op jit(solution)/shard_map/ppermute | solution.py:63
  230.0 35.5 %collective-permute-start.28 = (bf16[768,512]{1,0:T(8,128)(2,1)S(1)}, bf16[768,512]{1,0:T(8,128)(2,1)S(1)}, u32[]{:S(2)}, u32[]{:S(2)}) collective-permute-start(bf16[768,512]{1,0:T(8,128)(2,1)S(1)} %slice.273), channel_id=1, source_target_pairs={{2,0},{3,2},{1,3},{0,1},{6,4},{7,6},{5,7},{4,5},{10,8},{11,10},{9,... | collective-permute-start | bytes 2359304 | tf_op jit(solution)/shard_map/ppermute | solution.py:63
  247.7 30.7 %collective-permute-start.31 = (bf16[128,2048]{1,0:T(8,128)(2,1)S(1)}, bf16[128,2048]{1,0:T(8,128)(2,1)S(1)}, u32[]{:S(2)}, u32[]{:S(2)}) collective-permute-start(bf16[128,2048]{1,0:T(8,128)(2,1)S(1)} %get-tuple-element.454), channel_id=1, source_target_pairs={{0,8},{8,0},{16,24},{24,16},{1,9},{9,1},{17,25},{25,17},{2,10},{10... | collective-permute-start | bytes 1572872 | tf_op jit(solution)/shard_map/ppermute | solution.py:133
  267.3 34.2 %collective-permute-start.38 = (bf16[1536,512]{1,0:T(8,128)(2,1)S(1)}, bf16[1536,512]{1,0:T(8,128)(2,1)}, u32[]{:S(2)}, u32[]{:S(2)}) collective-permute-start(bf16[1536,512]{1,0:T(8,128)(2,1)S(1)} %pad_maximum_fusion.7.refs_0_), channel_id=1, source_target_pairs={{2,0},{3,2},{1,3},{0,1},{6,4},{7,6},{5,7},{4,5},{10,8},{11,10},{9,... | collective-permute-start | bytes 4718600 | tf_op jit(solution)/shard_map/ppermute | solution.py:63
  270.0 33.8 %collective-permute-start.39 = (bf16[1536,512]{1,0:T(8,128)(2,1)S(1)}, bf16[1536,512]{1,0:T(8,128)(2,1)}, u32[]{:S(2)}, u32[]{:S(2)}) collective-permute-start(bf16[1536,512]{1,0:T(8,128)(2,1)S(1)} %pad_maximum_fusion.7.refs_0_), channel_id=1, source_target_pairs={{0,2},{2,3},{3,1},{1,0},{4,6},{6,7},{7,5},{5,4},{8,10},{10,11},{11... | collective-permute-start | bytes 4718600 | tf_op jit(solution)/shard_map/ppermute | solution.py:63
  305.0 28.1 %collective-permute-start.40 = (bf16[768,512]{1,0:T(8,128)(2,1)S(1)}, bf16[768,512]{1,0:T(8,128)(2,1)}, u32[]{:S(2)}, u32[]{:S(2)}) collective-permute-start(bf16[768,512]{1,0:T(8,128)(2,1)S(1)} %slice.274), channel_id=1, source_target_pairs={{0,2},{2,3},{3,1},{1,0},{4,6},{6,7},{7,5},{5,4},{8,10},{10,11},{11... | collective-permute-start | bytes 2359304 | tf_op jit(solution)/shard_map/ppermute | solution.py:63
  306.3 26.8 %collective-permute-start.41 = (bf16[768,512]{1,0:T(8,128)(2,1)S(1)}, bf16[768,512]{1,0:T(8,128)(2,1)}, u32[]{:S(2)}, u32[]{:S(2)}) collective-permute-start(bf16[768,512]{1,0:T(8,128)(2,1)S(1)} %slice.275), channel_id=1, source_target_pairs={{2,0},{3,2},{1,3},{0,1},{6,4},{7,6},{5,7},{4,5},{10,8},{11,10},{9,... | collective-permute-start | bytes 2359304 | tf_op jit(solution)/shard_map/ppermute | solution.py:63
  334.4 27.3 %collective-permute-start.45 = (bf16[1536,256]{1,0:T(8,128)(2,1)S(1)}, bf16[1536,256]{1,0:T(8,128)(2,1)}, u32[]{:S(2)}, u32[]{:S(2)}) collective-permute-start(bf16[1536,256]{1,0:T(8,128)(2,1)S(1)} %pad_maximum_fusion.10), channel_id=1, source_target_pairs={{0,2},{2,3},{3,1},{1,0},{4,6},{6,7},{7,5},{5,4},{8,10},{10,11},{11... | collective-permute-start | bytes 2359304 | tf_op jit(solution)/shard_map/ppermute | solution.py:63
  336.3 25.3 %collective-permute-start.44 = (bf16[1536,256]{1,0:T(8,128)(2,1)S(1)}, bf16[1536,256]{1,0:T(8,128)(2,1)}, u32[]{:S(2)}, u32[]{:S(2)}) collective-permute-start(bf16[1536,256]{1,0:T(8,128)(2,1)S(1)} %pad_maximum_fusion.9), channel_id=1, source_target_pairs={{2,0},{3,2},{1,3},{0,1},{6,4},{7,6},{5,7},{4,5},{10,8},{11,10},{9,... | collective-permute-start | bytes 2359304 | tf_op jit(solution)/shard_map/ppermute | solution.py:63
  362.9 26.4 %collective-permute-start.49 = (bf16[1536,256]{1,0:T(8,128)(2,1)S(1)}, bf16[1536,256]{1,0:T(8,128)(2,1)}, u32[]{:S(2)}, u32[]{:S(2)}) collective-permute-start(bf16[1536,256]{1,0:T(8,128)(2,1)S(1)} %pad_maximum_fusion.12), channel_id=1, source_target_pairs={{0,2},{2,3},{3,1},{1,0},{4,6},{6,7},{7,5},{5,4},{8,10},{10,11},{11... | collective-permute-start | bytes 2359304 | tf_op jit(solution)/shard_map/ppermute | solution.py:63
  406.4 45.5 %collective-permute-start.62 = (bf16[512,2048]{1,0:T(8,128)(2,1)S(1)}, bf16[512,2048]{1,0:T(8,128)(2,1)S(1)}, u32[]{:S(2)}, u32[]{:S(2)}) collective-permute-start(bf16[512,2048]{1,0:T(8,128)(2,1)S(1)} %copy-done.70), channel_id=1, source_target_pairs={{0,8},{8,0},{16,24},{24,16},{1,9},{9,1},{17,25},{25,17},{2,10},{10... | collective-permute-start | bytes 6291464 | tf_op jit(solution)/shard_map/ppermute | solution.py:133
  417.5 26.6 %collective-permute-start.57 = (bf16[128,2176]{1,0:T(8,128)(2,1)S(1)}, bf16[128,2176]{1,0:T(8,128)(2,1)S(1)}, u32[]{:S(2)}, u32[]{:S(2)}) collective-permute-start(bf16[128,2176]{1,0:T(8,128)(2,1)S(1)} %slice_add_fusion), channel_id=1, source_target_pairs={{0,4},{1,5},{2,6},{3,7},{4,0},{5,1},{6,2},{7,3},{8,12},{9,13},{10,... | collective-permute-start | bytes 1671176 | tf_op jit(solution)/shard_map/ppermute | solution.py:133
  462.4 35.3 %collective-permute-start.67 = (bf16[768,256]{1,0:T(8,128)(2,1)S(1)}, bf16[768,256]{1,0:T(8,128)(2,1)S(1)}, u32[]{:S(2)}, u32[]{:S(2)}) collective-permute-start(bf16[768,256]{1,0:T(8,128)(2,1)S(1)} %copy-done.75), channel_id=1, source_target_pairs={{2,0},{3,2},{1,3},{0,1},{6,4},{7,6},{5,7},{4,5},{10,8},{11,10},{9,... | collective-permute-start | bytes 1179656 | tf_op jit(solution)/shard_map/ppermute | solution.py:63
  464.1 33.6 %collective-permute-start.68 = (bf16[768,256]{1,0:T(8,128)(2,1)S(1)}, bf16[768,256]{1,0:T(8,128)(2,1)S(1)}, u32[]{:S(2)}, u32[]{:S(2)}) collective-permute-start(bf16[768,256]{1,0:T(8,128)(2,1)S(1)} %copy-done.74), channel_id=1, source_target_pairs={{0,2},{2,3},{3,1},{1,0},{4,6},{6,7},{7,5},{5,4},{8,10},{10,11},{11... | collective-permute-start | bytes 1179656 | tf_op jit(solution)/shard_map/ppermute | solution.py:63
  505.4 56.2 %collective-permute-start.74 = (bf16[768,512]{1,0:T(8,128)(2,1)}, bf16[768,512]{1,0:T(8,128)(2,1)}, u32[]{:S(2)}, u32[]{:S(2)}) collective-permute-start(bf16[768,512]{1,0:T(8,128)(2,1)} %slice.467), channel_id=1, source_target_pairs={{0,4},{1,5},{2,6},{3,7},{4,0},{5,1},{6,2},{7,3},{8,12},{9,13},{10,... | collective-permute-start | bytes 2359304 | tf_op jit(solution)/shard_map/ppermute | solution.py:133
  506.5 54.0 %collective-permute-start.73 = (bf16[128,2048]{1,0:T(8,128)(2,1)}, bf16[128,2048]{1,0:T(8,128)(2,1)}, u32[]{:S(2)}, u32[]{:S(2)}) collective-permute-start(bf16[128,2048]{1,0:T(8,128)(2,1)} %slice_add_fusion.2), channel_id=1, source_target_pairs={{0,4},{1,5},{2,6},{3,7},{4,0},{5,1},{6,2},{7,3},{8,12},{9,13},{10,... | collective-permute-start | bytes 1572872 | tf_op jit(solution)/shard_map/ppermute | solution.py:133
  509.4 52.2 %collective-permute-start.72 = (bf16[1536,256]{1,0:T(8,128)(2,1)}, bf16[1536,256]{1,0:T(8,128)(2,1)}, u32[]{:S(2)}, u32[]{:S(2)}) collective-permute-start(bf16[1536,256]{1,0:T(8,128)(2,1)} %pad_maximum_fusion.16), channel_id=1, source_target_pairs={{0,2},{2,3},{3,1},{1,0},{4,6},{6,7},{7,5},{5,4},{8,10},{10,11},{11... | collective-permute-start | bytes 2359304 | tf_op jit(solution)/shard_map/ppermute | solution.py:63
  511.3 50.3 %collective-permute-start.71 = (bf16[1536,256]{1,0:T(8,128)(2,1)}, bf16[1536,256]{1,0:T(8,128)(2,1)}, u32[]{:S(2)}, u32[]{:S(2)}) collective-permute-start(bf16[1536,256]{1,0:T(8,128)(2,1)} %pad_maximum_fusion.15), channel_id=1, source_target_pairs={{2,0},{3,2},{1,3},{0,1},{6,4},{7,6},{5,7},{4,5},{10,8},{11,10},{9,... | collective-permute-start | bytes 2359304 | tf_op jit(solution)/shard_map/ppermute | solution.py:63
  621.9 39.1 %all-to-all-start.1 = ((bf16[8,64,768]{2,1,0:T(8,128)(2,1)}), bf16[8,64,768]{2,1,0:T(8,128)(2,1)S(1)}, u32[]{:S(2)}, u32[]{:S(2)}) async-start(bf16[8,64,768]{2,1,0:T(8,128)(2,1)} %fusion.16), calls=%async_computation.1 | async-start | bytes 1572864 | tf_op jit(solution)/shard_map/all_to_all | solution.py:888
  658.3 33.9 %collective-permute-start.96 = (bf16[768,512]{1,0:T(8,128)(2,1)}, bf16[768,512]{1,0:T(8,128)(2,1)}, u32[]{:S(2)}, u32[]{:S(2)}) collective-permute-start(bf16[768,512]{1,0:T(8,128)(2,1)} %slice.466), channel_id=1, source_target_pairs={{0,4},{1,5},{2,6},{3,7},{4,0},{5,1},{6,2},{7,3},{8,12},{9,13},{10,... | collective-permute-start | bytes 2359304 | tf_op jit(solution)/shard_map/ppermute | solution.py:133
  (155 other events, 2185.0 us)

commit v5 on v4

--- a/solution.py
+++ b/solution.py
@@ -816,10 +816,13 @@
 
 
     attended_blocks = ring.gather(attended_low, True, middle_hook)
-    expert_out = far_sum(held["y"], attended_blocks[-1])
+    far_rows = after(held["y"][-1].astype(bf16), attended_blocks[-1])
+    expert_out = held["y"][0]
+    if split == 2:
+        expert_out = expert_out + swap(far_rows, "wshard", far).astype(f32)
     sum01 = weight_ring.finish(parts01, m01, halves, first=3)
     first_sum = jnp.concatenate([sum00, sum01], axis=1)
-    first_home = uncross(after(first_sum, attended_blocks[-1]))
+    first_home = uncross(after(first_sum, far_rows))
     second_moving = weight_ring.added(after(parts11, attended_blocks[-1]), held["m11"], 2)
     second_moving = weight_ring.hop(second_moving)
     raw_grad, attn_gain_grad, head_gain_grad, *normed_part = in_vmem(
@@ -867,7 +870,10 @@
                 small.step()
             moving, small.total = tie(moving, small.step())
         if s in (2, 3) and held["fold"] is not None:
-            moving, came = tie(moving, held["fold"])
+            if s == 2:
+                moving, came = tie(moving, held["fold"])
+            else:
+                came = after(held["fold"], moving)
             fold.add(came)
             held["fold"] = fold.send() if fold.left else None
         if s == 2:

time: 716 us -> 707 us (0.987)
  waiting for transfers between devices: 316 us -> 291 us
  starting transfers between devices: 128 us -> 143 us
    ppermute x41, waiting for transfers between devices: 147 us -> 128 us  [swap(): lax.ppermute(x, axis, [(i, i ^ bit) for i in range(lax.axis_size(axis))])]
    ppermute x41, starting transfers between devices: 38 us -> 51.1 us  [swap(): lax.ppermute(x, axis, [(i, i ^ bit) for i in range(lax.axis_size(axis))])]
  transfers between devices with their start and end apart: 99 -> 99, of which waited for: 47 -> 45; matrix products, arithmetic and copies ran while one was open for 14% -> 15% of each run, Pallas kernels for 20% -> 20%
where the time goes in v5:
time: 707 us; the launch traced here: 701 us
  waiting for transfers between devices  291 us (41%)
  Pallas kernels  144 us (20%)
  starting transfers between devices  143 us (20%)
  other arithmetic  59.4 us (8%)
  local copies, waits for them, and re-layouts  50 us (7%)
  matrix products  10.3 us (1%)
    ppermute x56, waiting for transfers between devices, hop(): lax.ppermute(block, self.axis, self.down if sign == 1 else self.up)  163 us
    ppermute x41, waiting for transfers between devices, swap(): lax.ppermute(x, axis, [(i, i ^ bit) for i in range(lax.axis_size(axis))])  128 us
    pallas_call x4, Pallas kernels, expert_pass(): pl.pallas_call(functools.partial(expert_kernel, expert, turn, first, last...  81.9 us
    ppermute x56, starting transfers between devices, hop(): lax.ppermute(block, self.axis, self.down if sign == 1 else self.up)  81.9 us
    pallas_call x4, Pallas kernels, in_vmem(): pl.pallas_call(kernel, in_specs=[pl.BlockSpec(memory_space=pltpu.SMEM)] *...  61.7 us
    ppermute x41, starting transfers between devices, swap(): lax.ppermute(x, axis, [(i, i ^ bit) for i in range(lax.axis_size(axis))])  51.1 us
    unnamed x206, local copies, waits for them, and re-layouts  16.8 us
  transfers between devices with their start and end apart: 99, of which 45 were waited for; matrix products, arithmetic and copies ran while one was open for 15% of the time, Pallas kernels for 20%

profile of v5, /device:TPU:0, one launch (start us, length us, event | category | flops | bytes accessed | tf_op | source)
XLA Modules:
  0.0 700.6 jit_solution(10650835725474609340)
XLA Ops:
  6.2 6.4 all-to-all-start
  21.9 17.2 %collective-permute-done.2.refs_3_.refs_12_ = bf16[128,2048]{1,0:T(8,128)(2,1)} collective-permute-done((bf16[128,2048]{1,0:T(8,128)(2,1)S(1)}, bf16[128,2048]{1,0:T(8,128)(2,1)}, u32[]{:S(2)}, u32[]{:S(2)}) %collective-permute-start.2) | collective-permute-done | bytes 524320 | tf_op jit(solution)/shard_map/ppermute | solution.py:63
  43.1 5.8 collective-permute-start.4
  67.6 5.7 collective-permute-start.6
  83.8 20.2 %shard_map.325 = (bf16[1024,2048]{1,0:T(8,128)(2,1)}, f32[1024,1]{1,0:T(8,128)}, f32[1024,512]{1,0:T(8,128)}, bf16[1024,768]{1,0:T(8,128)(2,1)}, f32[1024,2]{1,0...) custom-call(bf16[128,2048]{1,0:T(8,128)(2,1)} %refs_9_.1, ...), custom_call_target="tpu_custom_call" | custom-call | flops 21474836480 | bytes 9454592 | tf_op jit(solution)/shard_map/pallas_call | solution.py:571
  104.0 27.8 %collective-permute-done.10 = bf16[768,512]{1,0:T(8,128)(2,1)} collective-permute-done((bf16[768,512]{1,0:T(8,128)(2,1)}, bf16[768,512]{1,0:T(8,128)(2,1)}, u32[]{:S(2)}, u32[]{:S(2)}) %collective-permute-start.10) | collective-permute-done | bytes 786464 | tf_op jit(solution)/shard_map/ppermute | solution.py:133
  131.8 15.7 %collective-permute-done.11 = bf16[768,512]{1,0:T(8,128)(2,1)S(1)} collective-permute-done((bf16[768,512]{1,0:T(8,128)(2,1)}, bf16[768,512]{1,0:T(8,128)(2,1)S(1)}, u32[]{:S(2)}, u32[]{:S(2)}) %collective-permute-start.11) | collective-permute-done | bytes 786464 | tf_op jit(solution)/shard_map/ppermute | solution.py:133
  161.9 10.0 %collective-permute-start.22 = (bf16[1536,512]{1,0:T(8,128)(2,1)S(1)}, bf16[1536,512]{1,0:T(8,128)(2,1)S(1)}, u32[]{:S(2)}, u32[]{:S(2)}) collective-permute-start(bf16[1536,512]{1,0:T(8,128)(2,1)S(1)} %pad_maximum_fusion.6.refs_0_), channel_id=1, source_target_pairs={{2,0},{3,2},{1,3},{0,1},{6,4},{7,6},{5,7},{4,5},{10,8},{11,10},{9,... | collective-permute-start | bytes 4718600 | tf_op jit(solution)/shard_map/ppermute | solution.py:63
  178.4 14.1 %collective-permute-done.16 = bf16[128,2048]{1,0:T(8,128)(2,1)S(1)} collective-permute-done((bf16[128,2048]{1,0:T(8,128)(2,1)S(1)}, bf16[128,2048]{1,0:T(8,128)(2,1)S(1)}, u32[]{:S(2)}, u32[]{:S(2)}) %collective-permute-start.16) | collective-permute-done | bytes 524320 | tf_op jit(solution)/shard_map/ppermute | solution.py:63
  197.5 24.4 %collective-permute-done.21 = bf16[128,2048]{1,0:T(8,128)(2,1)S(1)} collective-permute-done((bf16[128,2048]{1,0:T(8,128)(2,1)S(1)}, bf16[128,2048]{1,0:T(8,128)(2,1)S(1)}, u32[]{:S(2)}, u32[]{:S(2)}) %collective-permute-start.21) | collective-permute-done | bytes 524320 | tf_op jit(solution)/shard_map/ppermute | solution.py:63
  230.9 9.3 %collective-permute-done.24 = bf16[128,2048]{1,0:T(8,128)(2,1)S(1)} collective-permute-done((bf16[128,2048]{1,0:T(8,128)(2,1)S(1)}, bf16[128,2048]{1,0:T(8,128)(2,1)S(1)}, u32[]{:S(2)}, u32[]{:S(2)}) %collective-permute-start.24) | collective-permute-done | bytes 524320 | tf_op jit(solution)/shard_map/ppermute | solution.py:63
  247.7 8.9 %collective-permute-done.27.refs_3_ = bf16[768,512]{1,0:T(8,128)(2,1)S(1)} collective-permute-done((bf16[768,512]{1,0:T(8,128)(2,1)S(1)}, bf16[768,512]{1,0:T(8,128)(2,1)S(1)}, u32[]{:S(2)}, u32[]{:S(2)}) %collective-permute-start.27) | collective-permute-done | bytes 786464 | tf_op jit(solution)/shard_map/ppermute | solution.py:63
  256.7 8.8 %collective-permute-done.28.refs_4_ = bf16[768,512]{1,0:T(8,128)(2,1)S(1)} collective-permute-done((bf16[768,512]{1,0:T(8,128)(2,1)S(1)}, bf16[768,512]{1,0:T(8,128)(2,1)S(1)}, u32[]{:S(2)}, u32[]{:S(2)}) %collective-permute-start.28) | collective-permute-done | bytes 786464 | tf_op jit(solution)/shard_map/ppermute | solution.py:63
  271.9 5.7 collective-permute-done.30
  282.3 18.3 %shard_map.326 = (f32[1024,128]{1,0:T(8,128)}, bf16[1024,2048]{1,0:T(8,128)(2,1)}, bf16[1024,2048]{1,0:T(8,128)(2,1)}, bf16[1536,256]{1,0:T(8,128)(2,1)}, bf16[1...) custom-call(s32[9]{0:T(128)} %pad_add_fusion.1.owner, ...), custom_call_target="tpu_custom_call" | custom-call | flops 9663676416 | bytes 6291456 | tf_op jit(solution)/shard_map/pallas_call | solution.py:371
  310.5 21.2 %shard_map.327 = (f32[1024,128]{1,0:T(8,128)}, bf16[1024,2048]{1,0:T(8,128)(2,1)}, bf16[1024,2048]{1,0:T(8,128)(2,1)}, bf16[1536,256]{1,0:T(8,128)(2,1)}, bf16[1...) custom-call(s32[9]{0:T(128)} %pad_add_fusion.1.owner, ...), custom_call_target="tpu_custom_call" | custom-call | flops 9663676416 | bytes 6291456 | tf_op jit(solution)/shard_map/pallas_call | solution.py:371
  339.2 20.5 %shard_map.328 = (f32[1024,128]{1,0:T(8,128)}, bf16[1024,2048]{1,0:T(8,128)(2,1)}, bf16[1024,2048]{1,0:T(8,128)(2,1)}, bf16[1536,256]{1,0:T(8,128)(2,1)}, bf16[1...) custom-call(s32[9]{0:T(128)} %pad_add_fusion.1.owner, ...), custom_call_target="tpu_custom_call" | custom-call | flops 9663676416 | bytes 6291456 | tf_op jit(solution)/shard_map/pallas_call | solution.py:371
  367.4 21.8 %shard_map.329 = (f32[1024,128]{1,0:T(8,128)}, bf16[512,2048]{1,0:T(8,128)(2,1)}, bf16[512,2048]{1,0:T(8,128)(2,1)}, bf16[512,2176]{1,0:T(8,128)(2,1)}, bf16[512...) custom-call(s32[9]{0:T(128)} %pad_add_fusion.1.owner, ...), custom_call_target="tpu_custom_call" | custom-call | flops 9663676416 | bytes 6291456 | tf_op jit(solution)/shard_map/pallas_call | solution.py:371
  406.4 9.2 %collective-permute-done.54 = bf16[128,2176]{1,0:T(8,128)(2,1)S(1)} collective-permute-done((bf16[128,2176]{1,0:T(8,128)(2,1)S(1)}, bf16[128,2176]{1,0:T(8,128)(2,1)S(1)}, u32[]{:S(2)}, u32[]{:S(2)}) %collective-permute-start.54) | collective-permute-done | bytes 557088 | tf_op jit(solution)/shard_map/ppermute | solution.py:133
  418.8 8.0 %collective-permute-done.53 = bf16[128,2176]{1,0:T(8,128)(2,1)S(1)} collective-permute-done((bf16[128,2176]{1,0:T(8,128)(2,1)S(1)}, bf16[128,2176]{1,0:T(8,128)(2,1)S(1)}, u32[]{:S(2)}, u32[]{:S(2)}) %collective-permute-start.53) | collective-permute-done | bytes 557088 | tf_op jit(solution)/shard_map/ppermute | solution.py:133
  426.8 17.3 %collective-permute-done.57 = bf16[128,2176]{1,0:T(8,128)(2,1)S(1)} collective-permute-done((bf16[128,2176]{1,0:T(8,128)(2,1)S(1)}, bf16[128,2176]{1,0:T(8,128)(2,1)S(1)}, u32[]{:S(2)}, u32[]{:S(2)}) %collective-permute-start.57) | collective-permute-done | bytes 557088 | tf_op jit(solution)/shard_map/ppermute | solution.py:133
  455.3 7.1 %collective-permute-done.58.refs_1_ = bf16[128,2048]{1,0:T(8,128)(2,1)S(1)} collective-permute-done((bf16[128,2048]{1,0:T(8,128)(2,1)S(1)}, bf16[128,2048]{1,0:T(8,128)(2,1)S(1)}, u32[]{:S(2)}, u32[]{:S(2)}) %collective-permute-start.58) | collective-permute-done | bytes 524320 | tf_op jit(solution)/shard_map/ppermute | solution.py:63
  469.2 8.5 %collective-permute-done.63 = bf16[128,2048]{1,0:T(8,128)(2,1)S(1)} collective-permute-done((bf16[128,2048]{1,0:T(8,128)(2,1)S(1)}, bf16[128,2048]{1,0:T(8,128)(2,1)S(1)}, u32[]{:S(2)}, u32[]{:S(2)}) %collective-permute-start.63) | collective-permute-done | bytes 524320 | tf_op jit(solution)/shard_map/ppermute | solution.py:133
  477.9 7.1 %collective-permute-done.60.refs_3_ = bf16[128,2048]{1,0:T(8,128)(2,1)S(1)} collective-permute-done((bf16[128,2048]{1,0:T(8,128)(2,1)S(1)}, bf16[128,2048]{1,0:T(8,128)(2,1)S(1)}, u32[]{:S(2)}, u32[]{:S(2)}) %collective-permute-start.60) | collective-permute-done | bytes 524320 | tf_op jit(solution)/shard_map/ppermute | solution.py:63
  487.2 9.3 %collective-permute-done.66.refs_6_ = bf16[128,2048]{1,0:T(8,128)(2,1)S(1)} collective-permute-done((bf16[128,2048]{1,0:T(8,128)(2,1)S(1)}, bf16[128,2048]{1,0:T(8,128)(2,1)S(1)}, u32[]{:S(2)}, u32[]{:S(2)}) %collective-permute-start.66) | collective-permute-done | bytes 524320 | tf_op jit(solution)/shard_map/ppermute | solution.py:63
  504.8 14.1 %collective-permute-start.73 = (bf16[128,2048]{1,0:T(8,128)(2,1)}, bf16[128,2048]{1,0:T(8,128)(2,1)}, u32[]{:S(2)}, u32[]{:S(2)}) collective-permute-start(bf16[128,2048]{1,0:T(8,128)(2,1)} %slice_add_fusion.2), channel_id=1, source_target_pairs={{0,4},{1,5},{2,6},{3,7},{4,0},{5,1},{6,2},{7,3},{8,12},{9,13},{10,... | collective-permute-start | bytes 1572872 | tf_op jit(solution)/shard_map/ppermute | solution.py:133
  527.2 31.0 %shard_map.330 = (bf16[1024,768]{1,0:T(8,128)(2,1)}, f32[1,2048]{1,0:T(1,128)}, f32[2,128]{1,0:T(2,128)}, bf16[128,2048]{1,0:T(8,128)(2,1)}, bf16[128,2048]{1,0:...) custom-call(bf16[128,2048]{1,0:T(8,128)(2,1)} %copy-done.38, ...), custom_call_target="tpu_custom_call" | custom-call | flops 27917287424 | bytes 17323008 | tf_op jit(solution)/shard_map/pallas_call | solution.py:571
  587.5 8.9 %collective-permute-done.81 = bf16[128,2048]{1,0:T(8,128)(2,1)S(1)} collective-permute-done((bf16[128,2048]{1,0:T(8,128)(2,1)S(1)}, bf16[128,2048]{1,0:T(8,128)(2,1)S(1)}, u32[]{:S(2)}, u32[]{:S(2)}) %collective-permute-start.81) | collective-permute-done | bytes 524320 | tf_op jit(solution)/shard_map/ppermute | solution.py:63
  606.1 6.9 collective-permute-done.86
  629.8 13.1 %collective-permute-done.87 = bf16[128,2048]{1,0:T(8,128)(2,1)S(1)} collective-permute-done((bf16[128,2048]{1,0:T(8,128)(2,1)}, bf16[128,2048]{1,0:T(8,128)(2,1)S(1)}, u32[]{:S(2)}, u32[]{:S(2)}) %collective-permute-start.87) | collective-permute-done | bytes 524320 | tf_op jit(solution)/shard_map/ppermute | solution.py:63
  660.6 16.4 %collective-permute-done.90 = bf16[1,8,64,768]{3,2,1,0:T(8,128)(2,1)S(1)} collective-permute-done((bf16[1,8,64,768]{3,2,1,0:T(8,128)(2,1)S(1)}, bf16[1,8,64,768]{3,2,1,0:T(8,128)(2,1)S(1)}, u32[]{:S(2)}, u32[]{:S(2)}) %collective-permute-start.90) | collective-permute-done | bytes 786464 | tf_op jit(solution)/shard_map/ppermute | solution.py:133
  683.1 5.8 shard_map.332
  (542 shorter events, 273.3 us)
Async XLA Ops:
  6.2 35.1 %all-to-all-start = ((bf16[8,64,768]{2,1,0:T(8,128)(2,1)}), bf16[8,64,768]{2,1,0:T(8,128)(2,1)S(1)}, u32[]{:S(2)}, u32[]{:S(2)}) async-start(bf16[8,64,768]{2,1,0:T(8,128)(2,1)} %copy.87), calls=%async_computation | async-start | bytes 1572864 | tf_op jit(solution)/shard_map/all_to_all | solution.py:630
  54.3 49.6 %collective-permute-start.13 = (bf16[128,2176]{1,0:T(8,128)(2,1)S(1)}, bf16[128,2176]{1,0:T(8,128)(2,1)}, u32[]{:S(2)}, u32[]{:S(2)}) collective-permute-start(bf16[128,2176]{1,0:T(8,128)(2,1)S(1)} %pad_maximum_fusion.17), channel_id=1, source_target_pairs={{0,8},{8,0},{16,24},{24,16},{1,9},{9,1},{17,25},{25,17},{2,10},{10... | collective-permute-start | bytes 1671176 | tf_op jit(solution)/shard_map/ppermute | solution.py:133
  73.3 30.7 %collective-permute-start.14 = (bf16[128,2176]{1,0:T(8,128)(2,1)}, bf16[128,2176]{1,0:T(8,128)(2,1)}, u32[]{:S(2)}, u32[]{:S(2)}) collective-permute-start(bf16[128,2176]{1,0:T(8,128)(2,1)} %collective-permute-done.12), channel_id=1, source_target_pairs={{0,8},{8,0},{16,24},{24,16},{1,9},{9,1},{17,25},{25,17},{2,10},{10... | collective-permute-start | bytes 1671176 | tf_op jit(solution)/shard_map/ppermute | solution.py:133
  77.7 54.1 %collective-permute-start.10 = (bf16[768,512]{1,0:T(8,128)(2,1)}, bf16[768,512]{1,0:T(8,128)(2,1)}, u32[]{:S(2)}, u32[]{:S(2)}) collective-permute-start(bf16[768,512]{1,0:T(8,128)(2,1)} %get-tuple-element.244), channel_id=1, source_target_pairs={{0,4},{1,5},{2,6},{3,7},{4,0},{5,1},{6,2},{7,3},{8,12},{9,13},{10,... | collective-permute-start | bytes 2359304 | tf_op jit(solution)/shard_map/ppermute | solution.py:133
  79.2 68.3 %collective-permute-start.11 = (bf16[768,512]{1,0:T(8,128)(2,1)}, bf16[768,512]{1,0:T(8,128)(2,1)S(1)}, u32[]{:S(2)}, u32[]{:S(2)}) collective-permute-start(bf16[768,512]{1,0:T(8,128)(2,1)} %get-tuple-element.245), channel_id=1, source_target_pairs={{0,4},{1,5},{2,6},{3,7},{4,0},{5,1},{6,2},{7,3},{8,12},{9,13},{10,... | collective-permute-start | bytes 2359304 | tf_op jit(solution)/shard_map/ppermute | solution.py:133
  152.4 40.3 %collective-permute-start.19 = (bf16[128,2176]{1,0:T(8,128)(2,1)S(1)}, bf16[128,2176]{1,0:T(8,128)(2,1)S(1)}, u32[]{:S(2)}, u32[]{:S(2)}) collective-permute-start(bf16[128,2176]{1,0:T(8,128)(2,1)S(1)} %pad_maximum_fusion.17), channel_id=1, source_target_pairs={{0,4},{1,5},{2,6},{3,7},{4,0},{5,1},{6,2},{7,3},{8,12},{9,13},{10,... | collective-permute-start | bytes 1671176 | tf_op jit(solution)/shard_map/ppermute | solution.py:133
  157.9 34.6 %collective-permute-start.16 = (bf16[128,2048]{1,0:T(8,128)(2,1)S(1)}, bf16[128,2048]{1,0:T(8,128)(2,1)S(1)}, u32[]{:S(2)}, u32[]{:S(2)}) collective-permute-start(bf16[128,2048]{1,0:T(8,128)(2,1)S(1)} %pad_maximum_fusion.20), channel_id=1, source_target_pairs={{2,0},{4,2},{6,4},{7,6},{5,7},{3,5},{1,3},{0,1},{10,8},{12,10},{14... | collective-permute-start | bytes 1572872 | tf_op jit(solution)/shard_map/ppermute | solution.py:63
  161.9 63.3 %collective-permute-start.22 = (bf16[1536,512]{1,0:T(8,128)(2,1)S(1)}, bf16[1536,512]{1,0:T(8,128)(2,1)S(1)}, u32[]{:S(2)}, u32[]{:S(2)}) collective-permute-start(bf16[1536,512]{1,0:T(8,128)(2,1)S(1)} %pad_maximum_fusion.6.refs_0_), channel_id=1, source_target_pairs={{2,0},{3,2},{1,3},{0,1},{6,4},{7,6},{5,7},{4,5},{10,8},{11,10},{9,... | collective-permute-start | bytes 4718600 | tf_op jit(solution)/shard_map/ppermute | solution.py:63
  172.0 53.3 %collective-permute-start.23 = (bf16[1536,512]{1,0:T(8,128)(2,1)S(1)}, bf16[1536,512]{1,0:T(8,128)(2,1)S(1)}, u32[]{:S(2)}, u32[]{:S(2)}) collective-permute-start(bf16[1536,512]{1,0:T(8,128)(2,1)S(1)} %pad_maximum_fusion.6.refs_0_), channel_id=1, source_target_pairs={{0,2},{2,3},{3,1},{1,0},{4,6},{6,7},{7,5},{5,4},{8,10},{10,11},{11... | collective-permute-start | bytes 4718600 | tf_op jit(solution)/shard_map/ppermute | solution.py:63
  192.7 29.1 %collective-permute-start.21 = (bf16[128,2048]{1,0:T(8,128)(2,1)S(1)}, bf16[128,2048]{1,0:T(8,128)(2,1)S(1)}, u32[]{:S(2)}, u32[]{:S(2)}) collective-permute-start(bf16[128,2048]{1,0:T(8,128)(2,1)S(1)} %add_convert_fusion.6), channel_id=1, source_target_pairs={{0,2},{2,4},{4,6},{6,7},{7,5},{5,3},{3,1},{1,0},{8,10},{10,12},{12... | collective-permute-start | bytes 1572872 | tf_op jit(solution)/shard_map/ppermute | solution.py:63
  193.6 31.4 %collective-permute-start.20 = (bf16[128,2048]{1,0:T(8,128)(2,1)S(1)}, bf16[128,2048]{1,0:T(8,128)(2,1)S(1)}, u32[]{:S(2)}, u32[]{:S(2)}) collective-permute-start(bf16[128,2048]{1,0:T(8,128)(2,1)S(1)} %add_convert_fusion.7), channel_id=1, source_target_pairs={{2,0},{4,2},{6,4},{7,6},{5,7},{3,5},{1,3},{0,1},{10,8},{12,10},{14... | collective-permute-start | bytes 1572872 | tf_op jit(solution)/shard_map/ppermute | solution.py:63
  194.8 30.4 %collective-permute-start.35 = (bf16[128,2176]{1,0:T(8,128)(2,1)S(1)}, bf16[128,2176]{1,0:T(8,128)(2,1)S(1)}, u32[]{:S(2)}, u32[]{:S(2)}) collective-permute-start(bf16[128,2176]{1,0:T(8,128)(2,1)S(1)} %collective-permute-done.19), channel_id=1, source_target_pairs={{0,16},{8,24},{16,0},{24,8},{1,17},{9,25},{17,1},{25,9},{2,18},{10... | collective-permute-start | bytes 1671176 | tf_op jit(solution)/shard_map/ppermute | solution.py:133
  228.7 28.0 %collective-permute-start.27 = (bf16[768,512]{1,0:T(8,128)(2,1)S(1)}, bf16[768,512]{1,0:T(8,128)(2,1)S(1)}, u32[]{:S(2)}, u32[]{:S(2)}) collective-permute-start(bf16[768,512]{1,0:T(8,128)(2,1)S(1)} %slice.272), channel_id=1, source_target_pairs={{0,2},{2,3},{3,1},{1,0},{4,6},{6,7},{7,5},{5,4},{8,10},{10,11},{11... | collective-permute-start | bytes 2359304 | tf_op jit(solution)/shard_map/ppermute | solution.py:63
  230.0 35.5 %collective-permute-start.28 = (bf16[768,512]{1,0:T(8,128)(2,1)S(1)}, bf16[768,512]{1,0:T(8,128)(2,1)S(1)}, u32[]{:S(2)}, u32[]{:S(2)}) collective-permute-start(bf16[768,512]{1,0:T(8,128)(2,1)S(1)} %slice.273), channel_id=1, source_target_pairs={{2,0},{3,2},{1,3},{0,1},{6,4},{7,6},{5,7},{4,5},{10,8},{11,10},{9,... | collective-permute-start | bytes 2359304 | tf_op jit(solution)/shard_map/ppermute | solution.py:63
  247.7 30.7 %collective-permute-start.31 = (bf16[128,2048]{1,0:T(8,128)(2,1)S(1)}, bf16[128,2048]{1,0:T(8,128)(2,1)S(1)}, u32[]{:S(2)}, u32[]{:S(2)}) collective-permute-start(bf16[128,2048]{1,0:T(8,128)(2,1)S(1)} %get-tuple-element.450), channel_id=1, source_target_pairs={{0,8},{8,0},{16,24},{24,16},{1,9},{9,1},{17,25},{25,17},{2,10},{10... | collective-permute-start | bytes 1572872 | tf_op jit(solution)/shard_map/ppermute | solution.py:133
  267.3 34.2 %collective-permute-start.38 = (bf16[1536,512]{1,0:T(8,128)(2,1)S(1)}, bf16[1536,512]{1,0:T(8,128)(2,1)}, u32[]{:S(2)}, u32[]{:S(2)}) collective-permute-start(bf16[1536,512]{1,0:T(8,128)(2,1)S(1)} %pad_maximum_fusion.7.refs_0_), channel_id=1, source_target_pairs={{2,0},{3,2},{1,3},{0,1},{6,4},{7,6},{5,7},{4,5},{10,8},{11,10},{9,... | collective-permute-start | bytes 4718600 | tf_op jit(solution)/shard_map/ppermute | solution.py:63
  270.0 33.8 %collective-permute-start.39 = (bf16[1536,512]{1,0:T(8,128)(2,1)S(1)}, bf16[1536,512]{1,0:T(8,128)(2,1)}, u32[]{:S(2)}, u32[]{:S(2)}) collective-permute-start(bf16[1536,512]{1,0:T(8,128)(2,1)S(1)} %pad_maximum_fusion.7.refs_0_), channel_id=1, source_target_pairs={{0,2},{2,3},{3,1},{1,0},{4,6},{6,7},{7,5},{5,4},{8,10},{10,11},{11... | collective-permute-start | bytes 4718600 | tf_op jit(solution)/shard_map/ppermute | solution.py:63
  305.0 28.1 %collective-permute-start.40 = (bf16[768,512]{1,0:T(8,128)(2,1)S(1)}, bf16[768,512]{1,0:T(8,128)(2,1)}, u32[]{:S(2)}, u32[]{:S(2)}) collective-permute-start(bf16[768,512]{1,0:T(8,128)(2,1)S(1)} %slice.274), channel_id=1, source_target_pairs={{0,2},{2,3},{3,1},{1,0},{4,6},{6,7},{7,5},{5,4},{8,10},{10,11},{11... | collective-permute-start | bytes 2359304 | tf_op jit(solution)/shard_map/ppermute | solution.py:63
  306.3 26.8 %collective-permute-start.41 = (bf16[768,512]{1,0:T(8,128)(2,1)S(1)}, bf16[768,512]{1,0:T(8,128)(2,1)}, u32[]{:S(2)}, u32[]{:S(2)}) collective-permute-start(bf16[768,512]{1,0:T(8,128)(2,1)S(1)} %slice.275), channel_id=1, source_target_pairs={{2,0},{3,2},{1,3},{0,1},{6,4},{7,6},{5,7},{4,5},{10,8},{11,10},{9,... | collective-permute-start | bytes 2359304 | tf_op jit(solution)/shard_map/ppermute | solution.py:63
  334.4 27.3 %collective-permute-start.45 = (bf16[1536,256]{1,0:T(8,128)(2,1)S(1)}, bf16[1536,256]{1,0:T(8,128)(2,1)}, u32[]{:S(2)}, u32[]{:S(2)}) collective-permute-start(bf16[1536,256]{1,0:T(8,128)(2,1)S(1)} %pad_maximum_fusion.10), channel_id=1, source_target_pairs={{0,2},{2,3},{3,1},{1,0},{4,6},{6,7},{7,5},{5,4},{8,10},{10,11},{11... | collective-permute-start | bytes 2359304 | tf_op jit(solution)/shard_map/ppermute | solution.py:63
  362.9 26.4 %collective-permute-start.49 = (bf16[1536,256]{1,0:T(8,128)(2,1)S(1)}, bf16[1536,256]{1,0:T(8,128)(2,1)}, u32[]{:S(2)}, u32[]{:S(2)}) collective-permute-start(bf16[1536,256]{1,0:T(8,128)(2,1)S(1)} %pad_maximum_fusion.12), channel_id=1, source_target_pairs={{0,2},{2,3},{3,1},{1,0},{4,6},{6,7},{7,5},{5,4},{8,10},{10,11},{11... | collective-permute-start | bytes 2359304 | tf_op jit(solution)/shard_map/ppermute | solution.py:63
  406.4 45.5 %collective-permute-start.62 = (bf16[512,2048]{1,0:T(8,128)(2,1)S(1)}, bf16[512,2048]{1,0:T(8,128)(2,1)S(1)}, u32[]{:S(2)}, u32[]{:S(2)}) collective-permute-start(bf16[512,2048]{1,0:T(8,128)(2,1)S(1)} %copy-done.70), channel_id=1, source_target_pairs={{0,8},{8,0},{16,24},{24,16},{1,9},{9,1},{17,25},{25,17},{2,10},{10... | collective-permute-start | bytes 6291464 | tf_op jit(solution)/shard_map/ppermute | solution.py:133
  417.5 26.6 %collective-permute-start.57 = (bf16[128,2176]{1,0:T(8,128)(2,1)S(1)}, bf16[128,2176]{1,0:T(8,128)(2,1)S(1)}, u32[]{:S(2)}, u32[]{:S(2)}) collective-permute-start(bf16[128,2176]{1,0:T(8,128)(2,1)S(1)} %slice_add_fusion), channel_id=1, source_target_pairs={{0,4},{1,5},{2,6},{3,7},{4,0},{5,1},{6,2},{7,3},{8,12},{9,13},{10,... | collective-permute-start | bytes 1671176 | tf_op jit(solution)/shard_map/ppermute | solution.py:133
  462.4 35.3 %collective-permute-start.67 = (bf16[768,256]{1,0:T(8,128)(2,1)S(1)}, bf16[768,256]{1,0:T(8,128)(2,1)S(1)}, u32[]{:S(2)}, u32[]{:S(2)}) collective-permute-start(bf16[768,256]{1,0:T(8,128)(2,1)S(1)} %copy-done.75), channel_id=1, source_target_pairs={{2,0},{3,2},{1,3},{0,1},{6,4},{7,6},{5,7},{4,5},{10,8},{11,10},{9,... | collective-permute-start | bytes 1179656 | tf_op jit(solution)/shard_map/ppermute | solution.py:63
  464.1 33.6 %collective-permute-start.68 = (bf16[768,256]{1,0:T(8,128)(2,1)S(1)}, bf16[768,256]{1,0:T(8,128)(2,1)S(1)}, u32[]{:S(2)}, u32[]{:S(2)}) collective-permute-start(bf16[768,256]{1,0:T(8,128)(2,1)S(1)} %copy-done.74), channel_id=1, source_target_pairs={{0,2},{2,3},{3,1},{1,0},{4,6},{6,7},{7,5},{5,4},{8,10},{10,11},{11... | collective-permute-start | bytes 1179656 | tf_op jit(solution)/shard_map/ppermute | solution.py:63
  498.2 28.3 %collective-permute-start.69 = (bf16[64,2048]{1,0:T(8,128)(2,1)S(1)}, bf16[64,2048]{1,0:T(8,128)(2,1)S(1)}, u32[]{:S(2)}, u32[]{:S(2)}) collective-permute-start(bf16[64,2048]{1,0:T(8,128)(2,1)S(1)} %slice.361), channel_id=1, source_target_pairs={{0,2},{2,4},{4,6},{6,7},{7,5},{5,3},{3,1},{1,0},{8,10},{10,12},{12... | collective-permute-start | bytes 786440 | tf_op jit(solution)/shard_map/ppermute | solution.py:63
  504.8 56.0 %collective-permute-start.73 = (bf16[128,2048]{1,0:T(8,128)(2,1)}, bf16[128,2048]{1,0:T(8,128)(2,1)}, u32[]{:S(2)}, u32[]{:S(2)}) collective-permute-start(bf16[128,2048]{1,0:T(8,128)(2,1)} %slice_add_fusion.2), channel_id=1, source_target_pairs={{0,4},{1,5},{2,6},{3,7},{4,0},{5,1},{6,2},{7,3},{8,12},{9,13},{10,... | collective-permute-start | bytes 1572872 | tf_op jit(solution)/shard_map/ppermute | solution.py:133
  519.8 42.3 %collective-permute-start.74 = (bf16[768,512]{1,0:T(8,128)(2,1)}, bf16[768,512]{1,0:T(8,128)(2,1)}, u32[]{:S(2)}, u32[]{:S(2)}) collective-permute-start(bf16[768,512]{1,0:T(8,128)(2,1)} %slice.467), channel_id=1, source_target_pairs={{0,4},{1,5},{2,6},{3,7},{4,0},{5,1},{6,2},{7,3},{8,12},{9,13},{10,... | collective-permute-start | bytes 2359304 | tf_op jit(solution)/shard_map/ppermute | solution.py:133
  520.9 41.2 %collective-permute-start.72 = (bf16[1536,256]{1,0:T(8,128)(2,1)}, bf16[1536,256]{1,0:T(8,128)(2,1)}, u32[]{:S(2)}, u32[]{:S(2)}) collective-permute-start(bf16[1536,256]{1,0:T(8,128)(2,1)} %pad_maximum_fusion.16), channel_id=1, source_target_pairs={{0,2},{2,3},{3,1},{1,0},{4,6},{6,7},{7,5},{5,4},{8,10},{10,11},{11... | collective-permute-start | bytes 2359304 | tf_op jit(solution)/shard_map/ppermute | solution.py:63
  526.1 36.0 %collective-permute-start.71 = (bf16[1536,256]{1,0:T(8,128)(2,1)}, bf16[1536,256]{1,0:T(8,128)(2,1)}, u32[]{:S(2)}, u32[]{:S(2)}) collective-permute-start(bf16[1536,256]{1,0:T(8,128)(2,1)} %pad_maximum_fusion.15), channel_id=1, source_target_pairs={{2,0},{3,2},{1,3},{0,1},{6,4},{7,6},{5,7},{4,5},{10,8},{11,10},{9,... | collective-permute-start | bytes 2359304 | tf_op jit(solution)/shard_map/ppermute | solution.py:63
  614.2 37.0 %all-to-all-start.1 = ((bf16[8,64,768]{2,1,0:T(8,128)(2,1)}), bf16[8,64,768]{2,1,0:T(8,128)(2,1)S(1)}, u32[]{:S(2)}, u32[]{:S(2)}) async-start(bf16[8,64,768]{2,1,0:T(8,128)(2,1)} %fusion.16), calls=%async_computation.1 | async-start | bytes 1572864 | tf_op jit(solution)/shard_map/all_to_all | solution.py:894
  645.2 38.0 %collective-permute-start.96 = (bf16[768,512]{1,0:T(8,128)(2,1)}, bf16[768,512]{1,0:T(8,128)(2,1)}, u32[]{:S(2)}, u32[]{:S(2)}) collective-permute-start(bf16[768,512]{1,0:T(8,128)(2,1)} %slice.466), channel_id=1, source_target_pairs={{0,4},{1,5},{2,6},{3,7},{4,0},{5,1},{6,2},{7,3},{8,12},{9,13},{10,... | collective-permute-start | bytes 2359304 | tf_op jit(solution)/shard_map/ppermute | solution.py:133
  (155 other events, 2183.3 us)
